TPU v7x, 128 devices: a whole 4x4x4 slice. The times are simulated.
128 devices in a mesh: section: 2 (over z_lo), dp: 8 (over z_hi, y), ctx: 8 (over x, core).
Axes of the slice: x: 4, y: 4, z: 4 (z_hi: 2, z_lo: 2; z = z_hi * 2 + z_lo), core: 2. Of those that a mesh axis runs over, the one named last changes fastest.
Arguments:
- token_ids: int32 [2048], P('ctx'), may hold values from 0 to 511
- embedding: bfloat16 [512, 4096], P(None, 'dp'), may hold values from -6 to 6
- project_in: bfloat16 [2, 4096, 3, 4096], P('section', 'ctx', None, 'dp'), may hold values from -0.09375 to 0.09375
- short_taps: float32 [2, 3, 3, 4096], P('section', None, None, 'dp'), may hold values from -3.5 to 3.5
- filter_taps: float32 [2, 128, 4096], P('section', None, 'dp'), may hold values from -0.5 to 0.5
- decay_rates: float32 [2, 4096], P('section', 'dp'), may hold values from 0.5 to 4
- project_out: bfloat16 [2, 4096, 4096], P('section', 'dp', 'ctx'), may hold values from -0.09375 to 0.09375
- cotangent: bfloat16 [2048, 4096], P('ctx', 'dp'), may hold values from -0.125 to 0.125
Outputs:
- grad_project_in: float32 [2, 4096, 3, 4096], P('section', 'ctx', None, 'dp')
- grad_project_out: float32 [2, 4096, 4096], P('section', 'dp', 'ctx')
- grad_filter: float32 [2, 128, 4096], P('section', None, 'dp')
- grad_decay: float32 [2, 4096], P('section', 'dp')
- grad_short: float32 [2, 3, 3, 4096], P('section', None, None, 'dp')
All inputs are finite; a program needn't handle non-finite values.
Results may differ from a plain program's by a relative error of at most 0.03.
Values may be sent and summed in bfloat16 or wider, within the bound.
A program may use at most 128 MiB of HBM per device.

v0:
```python
import jax
import jax.numpy as jnp
from jax import lax
from jax.sharding import PartitionSpec as P

EPSILON = 1e-06


def gather_turned(arrays, axis, dims):
    turned = [jnp.moveaxis(a, dim, 0) for a, dim in zip(arrays, dims)]
    both = jnp.concatenate([t.reshape(len(t), -1) for t in turned], axis=1)
    filled, at, finished = (lax.all_gather(both, axis, axis=0, tiled=True), 0, [])
    for t, dim in zip(turned, dims):
        section = filled[:, at : at + t[0].size].reshape(-1, *t.shape[1:])
        finished.append(jnp.moveaxis(section, 0, dim))
        at += t[0].size
    return tuple(finished)


def laid_out(pieces, dim):
    pieces = jnp.moveaxis(pieces, 0, dim)
    shape = pieces.shape
    return pieces.reshape(*shape[:dim], shape[dim] * shape[dim + 1], *shape[dim + 2 :])


def from_everyone(shard, axis):
    copies = jnp.broadcast_to(shard, (lax.axis_size(axis), *shard.shape))
    return lax.all_to_all(copies, axis, split_axis=0, concat_axis=0, tiled=True)


def gather_directly(shard, axis, dim):
    return laid_out(from_everyone(shard, axis), dim)


def from_behind(value, axis, steps):
    count = lax.axis_size(axis)
    initial, last = (max(0, -steps), min(count, count - steps))
    return lax.ppermute(value, axis, [(source, source + steps) for source in range(initial, last)])


def cut_along(shard, dim, peers):
    shape = shard.shape
    pieces = shard.reshape(*shape[:dim], peers, shape[dim] // peers, *shape[dim + 1 :])
    return jnp.moveaxis(pieces, dim, 0)


def summed_on_arrival(shard, axis, dim):
    peers = lax.axis_size(axis)
    pieces = lax.all_to_all(cut_along(shard, dim, peers), axis, 0, 0, tiled=True)
    return jnp.sum(pieces.astype(jnp.float32), axis=0)


def taken_together(shard, axis):
    everything = from_everyone(shard, axis)
    return jnp.sum(everything, axis=0)


def over_copies(shard, axis):
    everything = from_everyone(shard, axis)
    return jnp.sum(everything.astype(jnp.float32), axis=0)


def correlate(signal, kernel):
    channels = signal.shape[1]
    result = lax.conv_general_dilated(
        signal[None],
        kernel[:, None, :],
        (1,),
        "VALID",
        dimension_numbers=("NWC", "WIO", "NWC"),
        feature_group_count=channels,
        precision=lax.Precision.HIGHEST,
    )
    return result[0]


def local(
    token_ids, embedding, project_in, short_taps, filter_taps, decay_rates, project_out, cotangent
):
    section_zero = lax.axis_index("section") == 0
    tok_rows = token_ids.shape[0]
    weights_in, weights_out = gather_turned((project_in[0], project_out[0]), "ctx", (0, 1))
    full_width = weights_in.shape[0]
    chan_count = weights_in.shape[2]
    flat_in = weights_in.reshape(full_width, 3 * chan_count)
    taps_local = short_taps[0]
    filter_local = filter_taps[0]
    tap_count = filter_local.shape[0]
    positions = jnp.arange(tap_count).astype(jnp.float32)
    damping = jnp.exp(-decay_rates[0][None, :] * positions[:, None] / tap_count)
    kernel = filter_local * damping
    onehot = (
        token_ids[:, None] == jnp.arange(embedding.shape[0], dtype=jnp.int32)[None, :]
    ).astype(jnp.bfloat16)
    first_input = jnp.dot(onehot, embedding, preferred_element_type=jnp.float32).astype(
        jnp.bfloat16
    )

    def forward(inputs, apply_out):
        rows_all = gather_directly(inputs, "dp", 1)
        rows_float = rows_all.astype(jnp.float32)
        inv_rms = lax.rsqrt(jnp.mean(rows_float * rows_float, axis=1, keepdims=True) + EPSILON)
        normed = (rows_float * inv_rms).astype(jnp.bfloat16)
        projected = jnp.dot(normed, flat_in, preferred_element_type=jnp.float32).reshape(
            tok_rows, 3, chan_count
        )
        earlier = from_behind(projected[tok_rows - 2 :], "ctx", 1)
        padded_proj = jnp.concatenate([earlier, projected], axis=0)
        shortened = (
            taps_local[0] * padded_proj[2:]
            + taps_local[1] * padded_proj[1:-1]
            + taps_local[2] * padded_proj[:-2]
        )
        products = shortened[:, 1] * shortened[:, 2]
        earlier_prod = from_behind(
            products[tok_rows - tap_count + 1 :].astype(jnp.bfloat16), "ctx", 1
        ).astype(jnp.float32)
        padded_prod = jnp.concatenate([earlier_prod, products], axis=0)
        filtered = correlate(padded_prod, kernel[::-1])
        gated_rows = (shortened[:, 0] * filtered).astype(jnp.bfloat16)
        saved = (
            inputs,
            rows_float,
            inv_rms,
            normed,
            padded_proj,
            shortened,
            padded_prod,
            filtered,
            gated_rows,
        )
        if apply_out:
            partials = jnp.dot(gated_rows, weights_out, preferred_element_type=jnp.float32)
            summed = summed_on_arrival(partials.astype(jnp.bfloat16), "dp", 1)
            return ((inputs.astype(jnp.float32) + summed).astype(jnp.bfloat16), saved)
        return (None, saved)

    def backward(saved, grad_local, need_input):
        (
            inputs,
            rows_float,
            inv_rms,
            normed,
            padded_proj,
            shortened,
            padded_prod,
            filtered,
            gated_rows,
        ) = saved
        grad_rows = gather_directly(grad_local, "dp", 1)
        grad_gated = lax.dot_general(
            grad_rows, weights_out, (((1,), (1,)), ((), ())), preferred_element_type=jnp.float32
        )
        grad_query = grad_gated * filtered
        grad_filtered = grad_gated * shortened[:, 0]
        later_rows = from_behind(
            grad_filtered[: tap_count - 1].astype(jnp.bfloat16), "ctx", -1
        ).astype(jnp.float32)
        grad_prod = correlate(jnp.concatenate([grad_filtered, later_rows], axis=0), kernel)
        grad_kernel = correlate(padded_prod, grad_filtered)[::-1]
        grad_short_out = jnp.stack(
            [grad_query, grad_prod * shortened[:, 2], grad_prod * shortened[:, 1]], axis=1
        )
        later_short = from_behind(grad_short_out[:2], "ctx", -1)
        padded_short = jnp.concatenate([grad_short_out, later_short], axis=0)
        grad_proj = (
            taps_local[0] * padded_short[:-2]
            + taps_local[1] * padded_short[1:-1]
            + taps_local[2] * padded_short[2:]
        )
        grad_taps = jnp.stack(
            [
                jnp.sum(grad_short_out * padded_proj[2:], axis=0),
                jnp.sum(grad_short_out * padded_proj[1:-1], axis=0),
                jnp.sum(grad_short_out * padded_proj[:-2], axis=0),
            ],
            axis=0,
        )
        grad_proj_b = grad_proj.astype(jnp.bfloat16)
        grad_inputs = None
        if need_input:
            partials = lax.dot_general(
                grad_proj_b.reshape(tok_rows, 3 * chan_count),
                flat_in,
                (((1,), (1,)), ((), ())),
                preferred_element_type=jnp.float32,
            )
            shared_part = summed_on_arrival(partials.astype(jnp.bfloat16), "dp", 1)
            own_rows = inputs.astype(jnp.float32)
            row_stat = (
                taken_together(jnp.sum(own_rows * shared_part, axis=1), "dp")[:, None] / full_width
            )
            local_grad = inv_rms * shared_part - own_rows * inv_rms**3 * row_stat
            grad_inputs = (grad_local.astype(jnp.float32) + local_grad).astype(jnp.bfloat16)
        return (grad_inputs, (normed, gated_rows, grad_rows, grad_proj_b, grad_kernel, grad_taps))

    out_first, saved_first = forward(first_input, True)
    arrived = from_behind(out_first, "section", 1)
    unused_out, saved_second = forward(arrived, False)
    back_grad, late_parts = backward(saved_second, cotangent, True)
    returned = from_behind(back_grad, "section", -1)
    unused_grad, early_parts = backward(saved_first, returned, False)
    normed, gated_rows, grad_rows, grad_proj_b, grad_kernel, grad_taps = tuple(
        (
            jnp.where(section_zero, early_item, late_item)
            for early_item, late_item in zip(early_parts, late_parts)
        )
    )
    kernel_sum, taps_sum = (
        over_copies(grad_kernel.astype(jnp.bfloat16), "ctx").astype(jnp.float32),
        over_copies(grad_taps.astype(jnp.bfloat16), "ctx").astype(jnp.float32),
    )
    grad_filter = kernel_sum * damping
    grad_decay = (
        -jnp.sum(kernel_sum * filter_local * damping * positions[:, None], axis=0) / tap_count
    )
    flat_grad = grad_proj_b.reshape(tok_rows, 3 * chan_count)
    row_block = lax.slice_in_dim(
        normed, 0, full_width // lax.axis_size("ctx") * lax.axis_size("ctx"), axis=1
    )
    grad_in = lax.psum_scatter(
        lax.dot_general(
            row_block, flat_grad, (((0,), (0,)), ((), ())), preferred_element_type=jnp.float32
        )
        .reshape(full_width // lax.axis_size("ctx") * lax.axis_size("ctx"), 3, chan_count)
        .astype(jnp.bfloat16),
        "ctx",
        scatter_dimension=0,
        tiled=True,
    ).astype(jnp.float32)
    out_partials = lax.dot_general(
        gated_rows, grad_rows, (((0,), (0,)), ((), ())), preferred_element_type=jnp.float32
    )
    grad_out = summed_on_arrival(out_partials.astype(jnp.bfloat16), "ctx", 1)
    return (grad_in[None], grad_out[None], grad_filter[None], grad_decay[None], taps_sum[None])


def solution(mesh):
    return jax.shard_map(
        local,
        mesh=mesh,
        in_specs=(
            P("ctx"),
            P(None, "dp"),
            P("section", "ctx", None, "dp"),
            P("section", None, None, "dp"),
            P("section", None, "dp"),
            P("section", "dp"),
            P("section", "dp", "ctx"),
            P("ctx", "dp"),
        ),
        out_specs=(
            P("section", "ctx", None, "dp"),
            P("section", "dp", "ctx"),
            P("section", None, "dp"),
            P("section", "dp"),
            P("section", None, None, "dp"),
        ),
        check_vma=False,
    )
```

profile of v0, /device:TPU:1, one launch (start us, length us, event | category | flops | bytes accessed | tf_op | source)
XLA Modules:
  0.0 550.6 jit_solution(13177721387538396610)
XLA Ops:
  13.2 8.5 %all-to-all-start = ((bf16[8,256,512]{1,2,0:T(8,128)(2,1)}), bf16[8,256,512]{1,2,0:T(8,128)(2,1)S(1)}, u32[]{:S(2)}, u32[]{:S(2)}) async-start(bf16[8,256,512]{1,2,0:T(8,128)(2,1)} %broadcast_in_dim.68), calls=%async_computation | async-start | bytes 4194304 | tf_op jit(solution)/shard_map/all_to_all | solution.py:28
  21.9 28.4 %all-to-all-done = bf16[8,256,512]{1,2,0:T(8,128)(2,1)S(1)} async-done(((bf16[8,256,512]{1,2,0:T(8,128)(2,1)}), bf16[8,256,512]{1,2,0:T(8,128)(2,1)S(1)}, u32[]{:S(2)}, u32[]{:S(2)}) %all-to-all-start) | async-done | bytes 2097184 | tf_op jit(solution)/shard_map/all_to_all | solution.py:28
  52.7 46.5 %all-gather.2.cloned.1.call-done = bf16[4096,2048]{0,1:T(8,128)(2,1)} async-done(((bf16[512,2048]{0,1:T(8,128)(2,1)}), bf16[4096,2048]{0,1:T(8,128)(2,1)}) %all-gather.2.cloned.1.call-update) | async-done | bytes 16777232 | tf_op jit(solution)/shard_map/all_gather | solution.py:12
  99.2 7.1 %fusion.4 = f32[256,1536]{1,0:T(8,128)S(1)} fusion(bf16[256,4096]{0,1:T(8,128)(2,1)} %fusion.10, bf16[4096,2048]{0,1:T(8,128)(2,1)} %all-gather.2.cloned.1.call-done), kind=kOutput, calls=%fused_computation.4 | convolution fusion | flops 3221225472 | bytes 16252928 | tf_op jit(solution)/shard_map/dot_general | solution.py:104
  107.5 2.9 collective-permute-start
  110.6 3.0 copy.162
  113.6 3.0 copy.163
  116.7 3.3 multiply_add_fusion.1
  125.7 5.3 fusion.64
  131.0 3.6 convolution_convert_fusion.2
  134.9 35.3 %all_to_all.51 = bf16[8,256,512]{2,1,0:T(8,128)(2,1)S(1)} all-to-all(bf16[8,256,512]{2,1,0:T(8,128)(2,1)S(1)} %bitcast.181), channel_id=1, replica_groups=mesh['section'=2,'dp'=8,'ctx'=8] {'dp'}, dimensions={0} | all-to-all | bytes 4194304 | tf_op jit(solution)/shard_map/all_to_all | solution.py:49
  172.9 5.2 collective-permute-done.2
  179.7 4.5 all-to-all-start.2
  184.4 28.5 %all-to-all-done.2 = bf16[8,256,512]{1,2,0:T(8,128)(2,1)} async-done(((bf16[8,256,512]{1,2,0:T(8,128)(2,1)}), bf16[8,256,512]{1,2,0:T(8,128)(2,1)}, u32[]{:S(2)}, u32[]{:S(2)}) %all-to-all-start.2) | async-done | bytes 2097184 | tf_op jit(solution)/shard_map/all_to_all | solution.py:28
  214.3 4.3 all-to-all-start.3
  223.4 6.5 %fusion.2 = f32[256,1536]{1,0:T(8,128)S(1)} fusion(bf16[256,4096]{0,1:T(8,128)(2,1)S(1)} %fusion.9, bf16[4096,2048]{0,1:T(8,128)(2,1)} %all-gather.2.cloned.1.call-done), kind=kOutput, calls=%fused_computation.2 | convolution fusion | flops 3221225472 | bytes 16252928 | tf_op jit(solution)/shard_map/dot_general | solution.py:104
  233.0 3.0 copy.171
  236.1 3.0 copy.172
  239.1 4.3 multiply_add_fusion
  243.4 3.9 all-to-all-done.3
  247.3 4.2 bitcast_multiply_fusion.11
  251.5 2.7 collective-permute-start.5
  254.4 3.4 collective-permute-done.5
  257.9 5.3 fusion.32
  267.4 5.3 fusion.49
  276.1 3.6 collective-permute-done.6
  282.0 8.3 %fusion.6 = bf16[256,4096]{1,0:T(8,128)(2,1)S(1)} fusion(bf16[256,1536]{0,1:T(8,128)(2,1)} %bitcast.195, bf16[4096,2048]{0,1:T(8,128)(2,1)} %all-gather.2.cloned.1.call-done), kind=kOutput, calls=%fused_computation.9 | convolution fusion | flops 3222274048 | bytes 15466496 | tf_op jit(solution)/shard_map/dot_general | solution.py:182
  290.5 30.1 %all_to_all.52 = bf16[8,256,512]{2,1,0:T(8,128)(2,1)S(1)} all-to-all(bf16[8,256,512]{2,1,0:T(8,128)(2,1)S(1)} %bitcast.182), channel_id=1, replica_groups=mesh['section'=2,'dp'=8,'ctx'=8] {'dp'}, dimensions={0} | all-to-all | bytes 4194304 | tf_op jit(solution)/shard_map/all_to_all | solution.py:49
  321.7 8.9 %all_to_all.53 = f32[8,1,256]{2,1,0:T(1,128)S(1)} all-to-all(f32[8,1,256]{2,1,0:T(1,128)S(1)} %broadcast_in_dim.75), channel_id=1, replica_groups=mesh['section'=2,'dp'=8,'ctx'=8] {'dp'}, dimensions={0} | all-to-all | bytes 16384 | tf_op jit(solution)/shard_map/all_to_all | solution.py:28
  333.2 8.4 %collective-permute-done.7 = bf16[256,512]{1,0:T(8,128)(2,1)S(1)} collective-permute-done((bf16[256,512]{1,0:T(8,128)(2,1)S(1)}, bf16[256,512]{1,0:T(8,128)(2,1)S(1)}, u32[]{:S(2)}, u32[]{:S(2)}) %collective-permute-start.7) | collective-permute-done | bytes 262176 | tf_op jit(solution)/shard_map/ppermute | solution.py:38
  341.9 30.2 %all_to_all.54 = bf16[8,256,512]{1,2,0:T(8,128)(2,1)S(1)} all-to-all(bf16[8,256,512]{1,2,0:T(8,128)(2,1)S(1)} %broadcast_in_dim.76), channel_id=1, replica_groups=mesh['section'=2,'dp'=8,'ctx'=8] {'dp'}, dimensions={0} | all-to-all | bytes 4194304 | tf_op jit(solution)/shard_map/all_to_all | solution.py:28
  372.1 4.4 fusion.43
  378.0 3.9 collective-permute-start.8
  386.6 5.3 fusion.30
  397.2 3.7 fusion.16
  404.0 8.0 %convolution_convert_fusion = bf16[4096,3,512]{2,0,1:T(8,128)(2,1)} fusion(bf16[256,4096,1]{0,1,2:T(8,128)(2,1)} %bitcast.183, bf16[256,3,512]{0,2,1:T(8,128)(2,1)S(1)} %copy.184), kind=kOutput, calls=%fused_computation.6 | convolution fusion | flops 3227516928 | bytes 15466496 | tf_op jit(solution)/shard_map/dot_general | solution.py:222
  415.0 5.3 fusion.44
  420.6 3.2 copy.192
  425.6 5.3 fusion.46
  432.7 3.2 copy.190
  438.2 3.4 all-to-all-start.9
  441.7 5.6 %all-to-all-done.9 = bf16[8,3,3,512]{3,2,1,0:T(4,128)(2,1)S(1)} async-done(((bf16[8,3,3,512]{3,2,1,0:T(4,128)(2,1)}), bf16[8,3,3,512]{3,2,1,0:T(4,128)(2,1)S(1)}, u32[]{:S(2)}, u32[]{:S(2)}) %all-to-all-start.9) | async-done | bytes 73760 | tf_op jit(solution)/shard_map/all_to_all | solution.py:28
  448.3 4.4 all-to-all-start.8
  460.2 13.5 %all-to-all-done.8 = bf16[8,128,512]{2,1,0:T(8,128)(2,1)S(1)} async-done(((bf16[8,128,512]{2,1,0:T(8,128)(2,1)}), bf16[8,128,512]{2,1,0:T(8,128)(2,1)S(1)}, u32[]{:S(2)}, u32[]{:S(2)}) %all-to-all-start.8) | async-done | bytes 1048608 | tf_op jit(solution)/shard_map/all_to_all | solution.py:28
  473.8 5.5 all-to-all-start.7
  481.8 54.3 %all-to-all-done.7 = bf16[8,512,512]{2,1,0:T(8,128)(2,1)} async-done(((bf16[8,512,512]{2,1,0:T(8,128)(2,1)}), bf16[8,512,512]{2,1,0:T(8,128)(2,1)}, u32[]{:S(2)}, u32[]{:S(2)}) %all-to-all-start.7) | async-done | bytes 4194336 | tf_op jit(solution)/shard_map/all_to_all | solution.py:49
  536.1 3.9 convert_reduce_fusion
  540.0 3.5 bitcast_convert_fusion
  (198 shorter events, 78.2 us)
Async XLA Ops:
  7.2 3.4 copy-start
  7.2 1.9 copy-start.36
  7.2 92.0 %all-gather.2.cloned.1.call-start = ((), (), s32[]{:S(2)}) async-start(), calls=%async_computation.11 | async-start | bytes 18874368 | tf_op jit(solution)/shard_map/all_gather | solution.py:12
  13.2 8.5 %copy-start.44 = (f32[1,512]{1,0:T(1,128)S(1)}, f32[1,512]{1,0:T(1,128)}, u32[]{:S(2)}) copy-start(f32[1,512]{1,0:T(1,128)} %param.13) | copy-start | bytes 6148
  13.2 8.5 %copy-start.41 = (f32[1,3,3,512]{3,0,2,1:T(1,128)S(1)}, f32[1,3,3,512]{3,0,2,1:T(1,128)}, u32[]{:S(2)}) copy-start(f32[1,3,3,512]{3,0,2,1:T(1,128)} %param.11) | copy-start | bytes 55300
  13.2 8.5 %copy-start.20 = (f32[1,128,512]{2,1,0:T(8,128)S(1)}, f32[1,128,512]{2,1,0:T(8,128)}, u32[]{:S(2)}) copy-start(f32[1,128,512]{2,1,0:T(8,128)} %param.12) | copy-start | bytes 786436
  13.2 37.1 %all-to-all-start = ((bf16[8,256,512]{1,2,0:T(8,128)(2,1)}), bf16[8,256,512]{1,2,0:T(8,128)(2,1)S(1)}, u32[]{:S(2)}, u32[]{:S(2)}) async-start(bf16[8,256,512]{1,2,0:T(8,128)(2,1)} %broadcast_in_dim.68), calls=%async_computation | async-start | bytes 4194304 | tf_op jit(solution)/shard_map/all_to_all | solution.py:28
  21.7 232.5 %copy-start.39 = (f32[1,512]{1,0:T(1,128)}, f32[1,512]{1,0:T(1,128)S(1)}, u32[]{:S(2)}) copy-start(f32[1,512]{1,0:T(1,128)S(1)} %neg.14) | copy-start | bytes 6148
  21.7 232.5 %copy-start.42 = (f32[128]{0:T(128)}, f32[128]{0:T(128)S(1)}, u32[]{:S(2)}) copy-start(f32[128]{0:T(128)S(1)} %iota_convert_fusion) | copy-start | bytes 1540
  107.5 9.1 %collective-permute-start = (f32[2,3,512]{2,0,1:T(2,128)S(1)}, f32[2,3,512]{2,0,1:T(2,128)S(1)}, u32[]{:S(2)}, u32[]{:S(2)}) collective-permute-start(f32[2,3,512]{2,0,1:T(2,128)S(1)} %bitcast.214), channel_id=1, source_target_pairs={{0,1},{1,2},{2,3},{3,4},{4,5},{5,6},{6,7},{8,9},{9,10},{10,11},{11... | collective-permute-start | bytes 36872 | tf_op jit(solution)/shard_map/ppermute | solution.py:38
  119.9 11.1 %copy-start.2 = (f32[256,3,512]{2,0,1:T(8,128)}, f32[256,3,512]{2,0,1:T(8,128)S(1)}, u32[]{:S(2)}) copy-start(f32[256,3,512]{2,0,1:T(8,128)S(1)} %multiply_add_fusion.1) | copy-start | bytes 4718596
  120.1 4.1 collective-permute-start.1
  131.0 3.7 copy-start.24
  170.6 7.5 %collective-permute-start.2 = (bf16[256,512]{1,0:T(8,128)(2,1)S(1)}, bf16[256,512]{1,0:T(8,128)(2,1)S(1)}, u32[]{:S(2)}, u32[]{:S(2)}) collective-permute-start(bf16[256,512]{1,0:T(8,128)(2,1)S(1)} %add_convert_fusion), channel_id=1, source_target_pairs={{0,64},{1,65},{2,66},{3,67},{4,68},{5,69},{6,70},{7,71},{8,72},{9,... | collective-permute-start | bytes 786440 | tf_op jit(solution)/shard_map/ppermute | solution.py:38
  179.7 4.5 copy-start.27
  179.7 33.1 %all-to-all-start.2 = ((bf16[8,256,512]{1,2,0:T(8,128)(2,1)}), bf16[8,256,512]{1,2,0:T(8,128)(2,1)}, u32[]{:S(2)}, u32[]{:S(2)}) async-start(bf16[8,256,512]{1,2,0:T(8,128)(2,1)} %broadcast_in_dim.71), calls=%async_computation.2 | async-start | bytes 4194304 | tf_op jit(solution)/shard_map/all_to_all | solution.py:28
  214.3 33.0 %all-to-all-start.3 = ((bf16[8,256,512]{1,2,0:T(8,128)(2,1)}), bf16[8,256,512]{1,2,0:T(8,128)(2,1)}, u32[]{:S(2)}, u32[]{:S(2)}) async-start(bf16[8,256,512]{1,2,0:T(8,128)(2,1)} %broadcast_in_dim.72), calls=%async_computation.3 | async-start | bytes 4194304 | tf_op jit(solution)/shard_map/all_to_all | solution.py:28
  218.7 321.3 %reduce-scatter.2.cloned.1.call-start = ((), (), s32[]{:S(2)}) async-start(), calls=%async_computation.12 | async-start | bytes 14155776 | tf_op jit(solution)/shard_map/reduce_scatter | solution.py:221
  231.1 8.0 %collective-permute-start.3 = (f32[2,3,512]{2,0,1:T(2,128)S(1)}, f32[2,3,512]{2,0,1:T(2,128)S(1)}, u32[]{:S(2)}, u32[]{:S(2)}) collective-permute-start(f32[2,3,512]{2,0,1:T(2,128)S(1)} %bitcast.215), channel_id=1, source_target_pairs={{0,1},{1,2},{2,3},{3,4},{4,5},{5,6},{6,7},{8,9},{9,10},{10,11},{11... | collective-permute-start | bytes 36872 | tf_op jit(solution)/shard_map/ppermute | solution.py:38
  251.5 11.8 %copy-start.28 = (f32[256,512]{1,0:T(8,128)}, f32[256,512]{1,0:T(8,128)S(1)}, u32[]{:S(2)}) copy-start(f32[256,512]{1,0:T(8,128)S(1)} %get-tuple-element.38) | copy-start | bytes 1572868
  251.5 6.3 %collective-permute-start.5 = (bf16[127,512]{1,0:T(8,128)(2,1)S(1)}, bf16[127,512]{1,0:T(8,128)(2,1)S(1)}, u32[]{:S(2)}, u32[]{:S(2)}) collective-permute-start(bf16[127,512]{1,0:T(8,128)(2,1)S(1)} %slice.267), channel_id=1, source_target_pairs={{1,0},{2,1},{3,2},{4,3},{5,4},{6,5},{7,6},{9,8},{10,9},{11,10},{12... | collective-permute-start | bytes 390152 | tf_op jit(solution)/shard_map/ppermute | solution.py:38
  254.3 3.5 copy-start.37
  257.9 5.3 copy-start.8
  263.4 3.9 collective-permute-start.4
  267.4 5.3 copy-start.32
  273.7 2.4 copy-start.14
  273.7 6.2 %copy-start.6 = (f32[256,3,512]{2,0,1:T(8,128)S(1)}, f32[256,3,512]{2,0,1:T(8,128)}, u32[]{:S(2)}) copy-start(f32[256,3,512]{2,0,1:T(8,128)} %copy.172) | copy-start | bytes 4718596
  273.7 6.0 %collective-permute-start.6 = (f32[2,3,512]{2,0,1:T(2,128)S(1)}, f32[2,3,512]{2,0,1:T(2,128)S(1)}, u32[]{:S(2)}, u32[]{:S(2)}) collective-permute-start(f32[2,3,512]{2,0,1:T(2,128)S(1)} %slice.161), channel_id=1, source_target_pairs={{1,0},{2,1},{3,2},{4,3},{5,4},{6,5},{7,6},{9,8},{10,9},{11,10},{12... | collective-permute-start | bytes 36872 | tf_op jit(solution)/shard_map/ppermute | solution.py:38
  331.9 9.7 %collective-permute-start.7 = (bf16[256,512]{1,0:T(8,128)(2,1)S(1)}, bf16[256,512]{1,0:T(8,128)(2,1)S(1)}, u32[]{:S(2)}, u32[]{:S(2)}) collective-permute-start(bf16[256,512]{1,0:T(8,128)(2,1)S(1)} %fusion.37), channel_id=1, source_target_pairs={{64,0},{65,1},{66,2},{67,3},{68,4},{69,5},{70,6},{71,7},{72,8},{73... | collective-permute-start | bytes 786440 | tf_op jit(solution)/shard_map/ppermute | solution.py:38
  341.9 30.2 %copy-start.25 = (f32[1,256,512]{2,0,1:T(1,128)S(1)}, f32[1,256,512]{2,0,1:T(1,128)}, u32[]{:S(2)}) copy-start(f32[1,256,512]{2,0,1:T(1,128)} %copy-done.24) | copy-start | bytes 1572868
  372.1 4.4 copy-start.7
  378.0 6.6 %collective-permute-start.8 = (bf16[127,512]{1,0:T(8,128)(2,1)}, bf16[127,512]{1,0:T(8,128)(2,1)}, u32[]{:S(2)}, u32[]{:S(2)}) collective-permute-start(bf16[127,512]{1,0:T(8,128)(2,1)} %slice.266), channel_id=1, source_target_pairs={{1,0},{2,1},{3,2},{4,3},{5,4},{6,5},{7,6},{9,8},{10,9},{11,10},{12... | collective-permute-start | bytes 390152 | tf_op jit(solution)/shard_map/ppermute | solution.py:38
  381.9 4.7 copy-start.38
  386.6 5.3 copy-start.3
  395.1 5.8 %collective-permute-start.9 = (f32[2,3,512]{2,0,1:T(2,128)S(1)}, f32[2,3,512]{2,0,1:T(2,128)S(1)}, u32[]{:S(2)}, u32[]{:S(2)}) collective-permute-start(f32[2,3,512]{2,0,1:T(2,128)S(1)} %slice.165), channel_id=1, source_target_pairs={{1,0},{2,1},{3,2},{4,3},{5,4},{6,5},{7,6},{9,8},{10,9},{11,10},{12... | collective-permute-start | bytes 36872 | tf_op jit(solution)/shard_map/ppermute | solution.py:38
  420.6 3.2 copy-start.13
  425.6 5.5 copy-start.17
  432.7 3.2 copy-start.11
  438.2 9.1 %all-to-all-start.9 = ((bf16[8,3,3,512]{3,2,1,0:T(4,128)(2,1)}), bf16[8,3,3,512]{3,2,1,0:T(4,128)(2,1)S(1)}, u32[]{:S(2)}, u32[]{:S(2)}) async-start(bf16[8,3,3,512]{3,2,1,0:T(4,128)(2,1)} %broadcast_in_dim.84), calls=%async_computation.10 | async-start | bytes 196608 | tf_op jit(solution)/shard_map/all_to_all | solution.py:28
  448.3 25.4 %all-to-all-start.8 = ((bf16[8,128,512]{2,1,0:T(8,128)(2,1)}), bf16[8,128,512]{2,1,0:T(8,128)(2,1)S(1)}, u32[]{:S(2)}, u32[]{:S(2)}) async-start(bf16[8,128,512]{2,1,0:T(8,128)(2,1)} %broadcast_in_dim.83), calls=%async_computation.9 | async-start | bytes 2097152 | tf_op jit(solution)/shard_map/all_to_all | solution.py:28
  452.8 2.8 copy-start.4
  452.8 3.3 copy-start.9
  452.8 3.4 copy-start.19
  452.8 3.6 copy-start.26
  473.8 6.3 %copy-start.40 = (f32[1,512]{1,0:T(1,128)S(1)}, f32[1,512]{1,0:T(1,128)}, u32[]{:S(2)}) copy-start(f32[1,512]{1,0:T(1,128)} %copy-done.39) | copy-start | bytes 6148
  473.8 6.3 %copy-start.43 = (f32[128]{0:T(128)S(1)}, f32[128]{0:T(128)}, u32[]{:S(2)}) copy-start(f32[128]{0:T(128)} %copy-done.42) | copy-start | bytes 1540
  473.8 62.3 %all-to-all-start.7 = ((bf16[8,512,512]{2,1,0:T(8,128)(2,1)}), bf16[8,512,512]{2,1,0:T(8,128)(2,1)}, u32[]{:S(2)}, u32[]{:S(2)}) async-start(bf16[8,512,512]{2,1,0:T(8,128)(2,1)} %bitcast.178), calls=%async_computation.8 | async-start | bytes 8388608 | tf_op jit(solution)/shard_map/all_to_all | solution.py:49
  536.1 7.4 %copy-start.1 = (bf16[512,512]{1,0:T(8,128)(2,1)S(1)}, bf16[512,512]{1,0:T(8,128)(2,1)}, u32[]{:S(2)}) copy-start(bf16[512,512]{1,0:T(8,128)(2,1)} %param.9) | copy-start | bytes 1572868
  (16 other events, 19.9 us)
Sparse Core Ops, SparseCore 0:
  10.7 88.4 all-gather.1
  412.1 95.6 reduce-scatter.1
where the time goes:
time: 560 us; the launch traced here: 551 us
  waiting for transfers between devices  208 us (37%)
  blocking collectives  105 us (19%)
  matrix products  75.8 us (14%)
  starting transfers between devices  54.7 us (10%)
  local copies, waits for them, and re-layouts  49.2 us (9%)
  other arithmetic  43.2 us (8%)
  between operations  15.2 us (3%)
    all_to_all x5, waiting for transfers between devices, from_everyone(): return lax.all_to_all(copies, axis, split_axis=0, concat_axis=0, tiled=True)  79.9 us
    all_to_all x2, blocking collectives, summed_on_arrival(): lax.all_to_all(cut_along(shard, dim, peers), axis, 0, 0, tiled=True)  65.4 us
    all_to_all x1, waiting for transfers between devices, summed_on_arrival(): lax.all_to_all(cut_along(shard, dim, peers), axis, 0, 0, tiled=True)  54.3 us
    all_gather x1, waiting for transfers between devices, gather_turned(): lax.all_gather(both, axis, axis=0, tiled=True)  46.5 us
    all_to_all x2, blocking collectives, from_everyone(): return lax.all_to_all(copies, axis, split_axis=0, concat_axis=0, tiled=True)  39.1 us
    conv_general_dilated x6, matrix products, correlate(): lax.conv_general_dilated(signal[None], kernel[:, None, :], (1,), 'VALID',...  31.8 us
    ppermute x10, waiting for transfers between devices, from_behind(): lax.ppermute(value, axis, [(source, source + steps) for source in range(i...  27 us
    all_to_all x5, starting transfers between devices, from_everyone(): return lax.all_to_all(copies, axis, split_axis=0, concat_axis=0, tiled=True)  25.1 us
  transfers between devices with their start and end apart: 18, of which 14 were waited for; matrix products, arithmetic and copies ran while one was open for 13% of the time, Pallas kernels for 0%

commit v1 on v0

v1 whole, which is shorter than its diff:
```python
import functools

import jax
import jax.numpy as jnp
from jax import lax
from jax.experimental import pallas as pl
from jax.experimental.pallas import tpu as pltpu
from jax.sharding import PartitionSpec as P

EPSILON = 1e-06
F32 = jnp.float32
BF16 = jnp.bfloat16
MESH = pl.DeviceIdType.MESH
BACK = 136
AHEAD = 1184
KEPT = 1040
RING = 4


class Group:
    def __init__(self, axis):
        self.axis = axis
        me = lax.axis_index(axis)
        if axis == "ctx":
            self.ring, self.pair = me // 2, me % 2
        else:
            self.ring, self.pair = me % RING, me // RING
        self.right = (self.ring + 1) % RING
        self.left = (self.ring + RING - 1) % RING
        self.across = (self.ring + 2) % RING
        self.mate = 1 - self.pair

    def slot(self, ring, pair):
        return ring * 2 + pair if self.axis == "ctx" else pair * RING + ring

    def at(self, ring, pair):
        return {self.axis: self.slot(ring, pair)}

    def neighbours(self):
        return [
            self.at(self.right, self.pair),
            self.at(self.left, self.pair),
            self.at(self.ring, self.mate),
        ]


class Pool:
    def __init__(self, send, recv):
        self.send, self.recv, self.count = send, recv, 0

    def take(self, k):
        first = self.count
        self.count += k
        return [(self.send.at[first + i], self.recv.at[first + i]) for i in range(k)]


def remote(src, dst, sems, device):
    copy = pltpu.make_async_remote_copy(
        src_ref=src,
        dst_ref=dst,
        send_sem=sems[0],
        recv_sem=sems[1],
        device_id=device,
        device_id_type=MESH,
    )
    copy.start()
    return copy


def greet(devices, barrier):
    for device in devices:
        pl.semaphore_signal(barrier, inc=1, device_id=device, device_id_type=MESH)


class Gather:
    def __init__(self, group, src, out, pool, pair_first):
        self.g, self.src, self.out, self.pair_first = group, src, out, pair_first
        self.sems = pool.take(9)
        self.own = pool.take(1)[0]
        self.half = out.shape[1] // 2

    def block(self, ring, pair):
        return self.out.at[self.g.slot(ring, pair)]

    def part(self, ring, pair, second):
        return self.out.at[self.g.slot(ring, pair), pl.ds(self.half * second, self.half)]

    def start(self):
        g, s = self.g, self.sems
        mine = self.block(g.ring, g.pair)
        right, left, mate = g.neighbours()
        self.local = pltpu.make_async_copy(self.src, mine, self.own[0])
        self.local.start()
        first = remote(self.src, mine, s[0], mate)
        self.copies = [first, remote(self.src, mine, s[1], right), remote(self.src, mine, s[2], left)]

    def turn(self, pair, a, b, c, d):
        g, s = self.g, self.sems
        right, left, mate = g.neighbours()
        more = []
        a.wait_recv()
        part = self.part(g.left, pair, 0)
        more.append(remote(part, part, s[c], right))
        if not self.pair_first:
            block = self.block(g.left, pair)
            more.append(remote(block, block, s[5], mate))
        b.wait_recv()
        part = self.part(g.right, pair, 1)
        more.append(remote(part, part, s[d], left))
        if not self.pair_first:
            block = self.block(g.right, pair)
            more.append(remote(block, block, s[6], mate))
        return more

    def middle(self):
        g, s = self.g, self.sems
        right, left, mate = g.neighbours()
        mate_copy, to_right, to_left = self.copies
        rest = self.turn(g.pair, to_right, to_left, 3, 4)
        self.sent = list(self.copies) + rest
        if self.pair_first:
            self.late = list(rest)
            mate_copy.wait_recv()
            block = self.block(g.ring, g.mate)
            a = remote(block, block, s[5], right)
            b = remote(block, block, s[6], left)
            more = self.turn(g.mate, a, b, 7, 8)
            self.sent += [a, b] + more
            self.late += more
        else:
            rest[0].wait_recv()
            rest[2].wait_recv()
            block = self.block(g.across, g.pair)
            last = remote(block, block, s[7], mate)
            self.sent.append(last)
            self.late = [mate_copy, rest[1], rest[3], last]

    def finish(self):
        for copy in self.late:
            copy.wait_recv()
        for copy in self.sent:
            copy.wait_send()
        self.local.wait()


def add_into(out, terms, rows=64):
    @pl.loop(0, out.shape[0] // rows)
    def _(step):
        here = pl.ds(pl.multiple_of(step * rows, rows), rows)
        total = terms[0][here].astype(F32)
        for term in terms[1:]:
            total = total + term[here].astype(F32)
        out[here] = total.astype(out.dtype)


def rows_step(count):
    for rows in (64, 48, 37 * 16, 32, 16):
        if count % rows == 0:
            return rows if rows != 37 * 16 else 16
    return 16


class Around:
    def __init__(self, group, pool, bufs):
        self.g = group
        self.s = pool.take(6)
        self.rel, self.merged, self.came = bufs
        self.half = self.rel.shape[1]

    @staticmethod
    def scratch(rows, lanes):
        half = rows // 2
        return [
            pltpu.VMEM((2, half, lanes), BF16),
            pltpu.VMEM((2, half, lanes), BF16),
            pltpu.VMEM((2, 2, half, lanes), BF16),
        ]

    def halves(self, ref):
        return ref.at[pl.ds(0, self.half)], ref.at[pl.ds(self.half, self.half)]

    def send_across(self, block):
        right, left, _ = self.g.neighbours()
        a, b = self.halves(block)
        self.copies = [remote(a, self.rel.at[0], self.s[0], right), remote(b, self.rel.at[1], self.s[1], left)]

    def send_near(self, to_right, to_left):
        right, left, _ = self.g.neighbours()
        self.to_right, self.to_left = to_right, to_left
        b = self.halves(to_right)[1]
        a = self.halves(to_left)[0]
        self.copies += [
            remote(b, self.came.at[0, 1], self.s[2], right),
            remote(a, self.came.at[1, 0], self.s[3], left),
        ]

    def merge(self):
        right, left, _ = self.g.neighbours()
        step = rows_step(self.half)
        self.copies[0].wait_recv()
        add_into(self.merged.at[0], [self.halves(self.to_right)[0], self.rel.at[0]], step)
        self.copies.append(remote(self.merged.at[0], self.came.at[0, 0], self.s[4], right))
        self.copies[1].wait_recv()
        add_into(self.merged.at[1], [self.halves(self.to_left)[1], self.rel.at[1]], step)
        self.copies.append(remote(self.merged.at[1], self.came.at[1, 1], self.s[5], left))

    def collect(self, out, own):
        step = rows_step(self.half)
        for copy in self.copies[2:]:
            copy.wait_recv()
        for h in range(2):
            piece = pl.ds(h * self.half, self.half)
            add_into(
                out.at[piece],
                [ref.at[piece] for ref in own] + [self.came.at[0, h], self.came.at[1, h]],
                step,
            )

    def finish(self):
        for copy in self.copies:
            copy.wait_send()


class PairThenRing:
    def __init__(self, group, inp, pool, bufs):
        self.g, self.inp = group, inp
        self.got, self.sums = bufs[:2]
        self.ring = Around(group, pool, bufs[2:])
        self.s = pool.take(4)

    @staticmethod
    def scratch(rows, lanes):
        return [pltpu.VMEM((4, rows, lanes), BF16), pltpu.VMEM((4, rows, lanes), BF16)] + Around.scratch(rows, lanes)

    def run(self, out):
        g = self.g
        mate = g.at(g.ring, g.mate)
        order = [g.across, g.right, g.left, g.ring]
        copies = [
            remote(self.inp.at[g.slot(r, g.mate)], self.got.at[k], self.s[k], mate) for k, r in enumerate(order)
        ]
        step = rows_step(self.inp.shape[1])

        def pair_sum(k):
            copies[k].wait_recv()
            add_into(self.sums.at[k], [self.inp.at[g.slot(order[k], g.pair)], self.got.at[k]], step)

        pair_sum(0)
        self.ring.send_across(self.sums.at[0])
        pair_sum(1)
        pair_sum(2)
        self.ring.send_near(self.sums.at[1], self.sums.at[2])
        copies[3].wait_recv()
        self.ring.merge()
        self.ring.collect(out, [self.inp.at[g.slot(g.ring, g.pair)], self.got.at[3]])
        self.ring.finish()
        for copy in copies:
            copy.wait_send()


class RingThenPair:
    def __init__(self, group, inp, pool, bufs):
        self.g, self.inp = group, inp
        self.far, self.got = bufs[:2]
        self.rings = [Around(group, pool, bufs[2:5]), Around(group, pool, bufs[5:8])]
        self.s = pool.take(1)[0]

    @staticmethod
    def scratch(rows, lanes):
        return (
            [pltpu.VMEM((rows, lanes), BF16), pltpu.VMEM((rows, lanes), BF16)]
            + Around.scratch(rows, lanes)
            + Around.scratch(rows, lanes)
        )

    def run(self, out, extra=()):
        g = self.g
        pairs = [g.mate, g.pair]
        blocks = lambda ring, pair: self.inp.at[g.slot(ring, pair)]
        for ring, pair in zip(self.rings, pairs):
            ring.send_across(blocks(g.across, pair))
            ring.send_near(blocks(g.right, pair), blocks(g.left, pair))
        self.rings[0].merge()
        self.rings[1].merge()
        self.rings[0].collect(self.far, [blocks(g.ring, g.mate)])
        copy = remote(self.far, self.got, self.s, g.at(g.ring, g.mate))
        self.rings[1].collect(out, [blocks(g.ring, g.pair)])
        copy.wait_recv()
        add_into(out, [out, self.got] + list(extra), rows_step(out.shape[0]))
        copy.wait_send()
        for ring in self.rings:
            ring.finish()


ANY = pl.BlockSpec(memory_space=pl.ANY)
VMEM = pl.BlockSpec(memory_space=pltpu.VMEM)


def call(body, ident, outs, scratch, sems, *args, in_specs=None, out_specs=None, name=None):
    return pl.pallas_call(
        body,
        out_shape=[jax.ShapeDtypeStruct(shape, dtype) for shape, dtype in outs],
        in_specs=in_specs or [VMEM] * len(args),
        out_specs=out_specs or [VMEM] * len(outs),
        scratch_shapes=list(scratch)
        + [pltpu.SemaphoreType.DMA((sems,)), pltpu.SemaphoreType.DMA((sems,))],
        compiler_params=pltpu.CompilerParams(
            collective_id=ident, has_side_effects=True, vmem_limit_bytes=60 * 1024 * 1024
        ),
        name=name,
    )(*args)


def section_is(k):
    return lax.axis_index("section") == k


def crossing():
    i, j = lax.axis_index("dp"), lax.axis_index("ctx")
    return {"dp": j, "ctx": i}, i != j


def other_section():
    i, j = lax.axis_index("dp"), lax.axis_index("ctx")
    return {"section": 1 - lax.axis_index("section"), "dp": j, "ctx": i}


def begin_kernel(
    emb_ref, w_ref, w_far, cot_ref, tok_ref,
    emb_out, table_out, inv_out, tok_out, w_out, e1_out,
    parts, crossed, half_out, *rest,
):
    bufs, (send, recv) = rest[:-2], rest[-2:]
    barrier = pltpu.get_barrier_semaphore()
    ctx, dp = Group("ctx"), Group("dp")
    partner, apart = crossing()
    greet(ctx.neighbours() + dp.neighbours(), barrier)

    @pl.when(apart)
    def _():
        greet([partner], barrier)

    pl.semaphore_wait(barrier, 6 + jnp.where(apart, 1, 0))

    lane = 128
    strips = RING
    pool = Pool(send, recv)
    cross_sem = pool.take(1)[0]
    same_sem = pool.take(1)[0]
    pair_sems = pool.take(2)

    def cross(src, dst):
        @pl.when(apart)
        def _():
            remote(src, dst, cross_sem, partner).wait()

        @pl.when(jnp.logical_not(apart))
        def _():
            copy = pltpu.make_async_copy(src, dst, same_sem[0])
            copy.start()
            copy.wait()

    @pl.when(section_is(0))
    def _():
        mine = Pool(send, recv)
        mine.count = pool.count
        tokens = Gather(ctx, tok_ref, tok_out, mine, False)
        tokens.start()
        cross(emb_ref, emb_out)
        tokens.middle()
        vocab, width = emb_ref.shape
        hold = vocab // 2
        for core in range(2):
            rows = pl.ds(core * hold, hold)
            values = emb_out[rows].astype(F32)
            square = jnp.broadcast_to(jnp.sum(values * values, axis=1, keepdims=True), (hold, lane)).astype(BF16)
            for strip in range(strips):
                parts[strip * 2 + core, :, 3 * lane :] = square

        @pl.loop(0, 3 * strips)
        def _(k):
            strip, m = k // 3, k % 3
            columns = pl.ds(pl.multiple_of(m * strips * lane + strip * lane, lane), lane)
            product = jnp.dot(emb_out[...], w_ref[:, columns], preferred_element_type=F32).astype(BF16)
            to = pl.ds(pl.multiple_of(m * lane, lane), lane)
            parts[strip * 2, :, to] = product[:hold]
            parts[strip * 2 + 1, :, to] = product[hold:]

        PairThenRing(ctx, parts, mine, bufs).run(half_out)
        here = pl.ds(pl.multiple_of(ctx.pair * hold, hold), hold)
        total = half_out[...]
        inv = lax.rsqrt(total[:, 3 * lane :] / (width * 2 * RING) + EPSILON)
        inv_out[here] = inv
        for m in range(3):
            table_out[here, m * lane : (m + 1) * lane] = (total[:, m * lane : (m + 1) * lane] * inv).astype(BF16)
        mate = ctx.at(ctx.ring, ctx.mate)
        a = remote(inv_out.at[here], inv_out.at[here], pair_sems[0], mate)
        b = remote(table_out.at[here], table_out.at[here], pair_sems[1], mate)
        tokens.finish()
        a.wait()
        b.wait()

    @pl.when(section_is(1))
    def _():
        mine = Pool(send, recv)
        mine.count = pool.count
        weights = Gather(ctx, w_far, w_out, mine, False)
        weights.start()
        cross(cot_ref, crossed)
        cots = Gather(dp, crossed, e1_out, mine, True)
        cots.start()
        cots.middle()
        cots.finish()
        weights.middle()
        weights.finish()


def relay_barrier():
    barrier = pltpu.get_barrier_semaphore()
    dp = Group("dp")
    greet(dp.neighbours() + [other_section()], barrier)
    pl.semaphore_wait(barrier, 4)
    return dp


def forth_kernel(part_ref, first_ref, all_ref, arrived_ref, total, block, *rest):
    bufs, (send, recv) = rest[:-2], rest[-2:]
    dp = relay_barrier()
    pool = Pool(send, recv)
    relay = pool.take(1)[0]

    @pl.when(section_is(0))
    def _():
        RingThenPair(dp, part_ref, pool, bufs).run(total, [first_ref])
        block[...] = total[...].astype(BF16)
        remote(block, arrived_ref, relay, other_section()).wait_send()

    @pl.when(section_is(1))
    def _():
        mine = Pool(send, recv)
        mine.count = 1
        pltpu.make_async_remote_copy(
            src_ref=block, dst_ref=arrived_ref, send_sem=relay[0], recv_sem=relay[1],
            device_id=other_section(), device_id_type=MESH,
        ).wait_recv()
        rows = Gather(dp, arrived_ref, all_ref, mine, True)
        rows.start()
        rows.middle()
        rows.finish()


def back_kernel(
    part_ref, stat_ref, inv_ref, cot_ref, x_ref, all_ref, stats, arrived, total, block, *rest
):
    bufs, (send, recv) = rest[:-2], rest[-2:]
    dp = relay_barrier()
    pool = Pool(send, recv)
    relay = pool.take(1)[0]

    @pl.when(section_is(1))
    def _():
        stat = Gather(dp, stat_ref, stats, pool, True)
        stat.start()
        stat.middle()
        RingThenPair(dp, part_ref, pool, bufs).run(total)
        stat.finish()
        rows, width = total.shape
        lane = 128
        summed = stats[0]
        for k in range(1, 8):
            summed = summed + stats[k]
        eye = lax.broadcasted_iota(jnp.int32, (lane, lane), 0) == lax.broadcasted_iota(jnp.int32, (lane, lane), 1)
        for k in range(rows // lane):
            here = pl.ds(k * lane, lane)
            line = jnp.broadcast_to(summed[k : k + 1], (lane, lane))
            scalar = jnp.sum(jnp.where(eye, line, 0.0), axis=1, keepdims=True)
            inv = inv_ref[here]
            block[here] = (
                cot_ref[here].astype(F32)
                + inv * total[here]
                - x_ref[here].astype(F32) * (inv * inv * scalar / (width * 2 * RING))
            ).astype(BF16)
        remote(block, arrived, relay, other_section()).wait_send()

    @pl.when(section_is(0))
    def _():
        mine = Pool(send, recv)
        mine.count = 1
        pltpu.make_async_remote_copy(
            src_ref=block, dst_ref=arrived, send_sem=relay[0], recv_sem=relay[1],
            device_id=other_section(), device_id_type=MESH,
        ).wait_recv()
        rows = Gather(dp, arrived, all_ref, mine, True)
        rows.start()
        rows.middle()
        rows.finish()


REACH = 128


def lanes_at(first):
    return pl.ds(pl.multiple_of(first, 128), 128)


def shifted(shifts, ref, start, rows, lanes):
    for r in range(8):
        for a in range(0, rows, 64):
            count = min(64, rows - a)
            shifts[r, a : a + count] = ref[start + r + a : start + r + a + count, lanes]


def fir(shifts, kern, lanes, out, out_lanes, tiles, block, backwards):
    @pl.loop(0, tiles // block)
    def _(b):
        first = pl.multiple_of(b * block * 8, 8)

        def step(r, totals):
            totals = list(totals)
            taps = []
            for q in range(REACH // 8):
                u = 8 * q + r
                taps.append(kern[pl.ds(REACH - 1 - u if backwards else u, 8, stride=0), lanes])
            for i in range(block + REACH // 8 - 1):
                x = shifts[r, pl.ds(first + 8 * i, 8)]
                for o in range(block):
                    if 0 <= i - o < REACH // 8:
                        totals[o] = totals[o] + taps[i - o] * x
            return tuple(totals)

        totals = lax.fori_loop(0, 8, step, tuple(jnp.zeros((8, 128), F32) for _ in range(block)))
        for o in range(block):
            out[pl.ds(first + 8 * o, 8), out_lanes] = totals[o]


def lags(shifts, ref, lanes, out, out_lanes, tiles):
    for r in range(8):

        def step(b, totals):
            totals = list(totals)
            first = pl.multiple_of(b * 32, 8)
            own = [ref[pl.ds(first + 8 * o, 8), lanes] for o in range(4)]
            for i in range(4 + REACH // 8 - 1):
                x = shifts[r, pl.ds(first + 8 * i, 8)]
                for o in range(4):
                    if 0 <= i - o < REACH // 8:
                        totals[i - o] = totals[i - o] + own[o] * x
            return tuple(totals)

        totals = lax.fori_loop(0, tiles // 4, step, tuple(jnp.zeros((8, 128), F32) for _ in range(REACH // 8)))
        for q in range(REACH // 8):
            row = REACH - 1 - (8 * q + r)
            out[row : row + 1, out_lanes] = jnp.sum(totals[q], axis=0, keepdims=True)


def chunks(first, last, size):
    for a in range(first, last, size):
        yield a, min(size, last - a)


def short_rows(ref, taps, m, a, count, lanes, tap_lanes):
    total = taps[m : m + 1, tap_lanes] * ref[a : a + count, lanes]
    for j in (1, 2):
        total = total + taps[3 * j + m : 3 * j + m + 1, tap_lanes] * ref[a - j : a - j + count, lanes]
    return total


ALL = slice(0, 128)


def stream(m):
    return slice(m * 128, (m + 1) * 128)


def mix_first(proj, taps, kern, filtered, prod, shifts, gated, part):
    for a, count in chunks(8, BACK + part, 64):
        prod[a : a + count] = short_rows(proj, taps, 1, a, count, stream(1), ALL) * short_rows(
            proj, taps, 2, a, count, stream(2), ALL
        )
    for a, count in chunks(BACK + part, BACK + AHEAD, 64):
        prod[a : a + count] = short_rows(proj, taps, 1, a, count, stream(1), ALL) * short_rows(
            proj, taps, 2, a, count, stream(2), ALL
        )
    shifted(shifts, prod, BACK - REACH + 1, KEPT + REACH, ALL)
    fir(shifts, kern, ALL, filtered, ALL, KEPT // 8, 10, True)
    for a, count in chunks(0, part, 64):
        query = short_rows(proj, taps, 0, BACK + a, count, stream(0), ALL)
        gated[a : a + count] = (query * filtered[a : a + count]).astype(BF16)


def mix_back(gg, proj, taps, kern, filtered, gf, gprod, gs, shifts, gp, part):
    for a, count in chunks(0, AHEAD, 64):
        gf[a : a + count] = gg[a : a + count] * short_rows(proj, taps, 0, BACK + a, count, stream(0), ALL)
    shifted(shifts, gf, 0, KEPT + REACH, ALL)
    fir(shifts, kern, ALL, gprod, ALL, KEPT // 8, 10, False)
    for a, count in chunks(0, KEPT, 64):
        here = slice(a, a + count)
        gs[0, here] = gg[here] * filtered[here]
        gs[1, here] = gprod[here] * short_rows(proj, taps, 2, BACK + a, count, stream(2), ALL)
        gs[2, here] = gprod[here] * short_rows(proj, taps, 1, BACK + a, count, stream(1), ALL)
    for m in range(3):
        for a, count in chunks(0, part, 64):
            total = taps[m : m + 1] * gs[m, a : a + count]
            for j in (1, 2):
                total = total + taps[3 * j + m : 3 * j + m + 1] * gs[m, a + j : a + j + count]
            gp[a : a + count, stream(m)] = total.astype(BF16)


def mix_sums(gf, proj, taps, gs, prod, shifts, out, part):
    for a, count in chunks(8, BACK + part + 8, 64):
        prod[a : a + count] = short_rows(proj, taps, 1, a, count, stream(1), ALL) * short_rows(
            proj, taps, 2, a, count, stream(2), ALL
        )
    shifted(shifts, prod, BACK - REACH + 1, part + REACH, ALL)
    lags(shifts, gf, ALL, out, ALL, part // 8)
    out[REACH:] = jnp.zeros((16, 128), F32)
    for m in range(3):
        for j in range(3):
            total = jnp.zeros((8, 128), F32)
            for a, count in chunks(0, part, 64):
                term = gs[m, a : a + count] * proj[BACK - j + a : BACK - j + a + count, stream(m)]
                total = total + jnp.sum(term.reshape(count // 8, 8, 128), axis=0)
            row = REACH + 3 * j + m
            out[row : row + 1] = jnp.sum(total, axis=0, keepdims=True)


def second_kernel(proj, taps, kern, part_ref, all_ref, gg_ref, filtered, prod, shifts, gated, *rest):
    bufs, (send, recv) = rest[:-2], rest[-2:]
    barrier = pltpu.get_barrier_semaphore()
    ctx = Group("ctx")
    greet(ctx.neighbours(), barrier)
    pl.semaphore_wait(barrier, 3)
    part = gated.shape[0]

    @pl.when(section_is(0))
    def _():
        mix_first(proj, taps, kern, filtered, prod, shifts, gated, part)
        job = Gather(ctx, gated, all_ref, Pool(send, recv), False)
        job.block = lambda ring, pair: all_ref.at[
            pl.ds(pl.multiple_of(pair * part, part), part), lanes_at(ring * 128)
        ]
        job.half = part // 2
        job.part = lambda ring, pair, second: all_ref.at[
            pl.ds(pl.multiple_of(pair * part + second * job.half, job.half), job.half), lanes_at(ring * 128)
        ]
        job.start()
        job.middle()
        job.finish()

    @pl.when(section_is(1))
    def _():
        PairThenRing(ctx, part_ref, Pool(send, recv), bufs).run(gg_ref)


def last_kernel(
    gg, proj, taps, kern, filtered, looked, gtab_all, taps_all,
    gf, gprod, gs, prod, shifts, gp, gtab, sums, got, block, send, recv,
):
    barrier = pltpu.get_barrier_semaphore()
    ctx = Group("ctx")
    greet(ctx.neighbours(), barrier)
    pl.semaphore_wait(barrier, 3)

    @pl.when(section_is(0))
    def _():
        pool = Pool(send, recv)
        sem = pool.take(1)[0]
        hold = got.shape[0]
        part = gp.shape[0]
        mix_back(gg, proj, taps, kern, filtered, gf, gprod, gs, shifts, gp, part)

        @pl.loop(0, 4)
        def _(k):
            here = pl.ds(pl.multiple_of(k * 128, 128), 128)
            gtab[here] = jnp.dot(looked[here], gp[...], preferred_element_type=F32).astype(BF16)

        halves = lambda p: gtab.at[pl.ds(pl.multiple_of(p * hold, hold), hold)]
        copy = remote(halves(ctx.mate), got, sem, ctx.at(ctx.ring, ctx.mate))
        copy.wait()
        add_into(block, [halves(ctx.pair), got])
        table = Gather(ctx, block, gtab_all, pool, False)
        table.start()
        mix_sums(gf, proj, taps, gs, prod, shifts, sums, part)
        job = Gather(ctx, sums, taps_all, pool, False)
        job.start()
        table.middle()
        job.middle()
        table.finish()
        job.finish()


def middle_kernel(
    proj, gg, taps, kern, gp_out, gated_out, stat_out, sums_out, gf, prod,
    kg, pp, query, filtered, gprod, gs, shifts, ptail, qtail, ghead, gfar, sfar, gfpad, row_sum, qsend, gsend, send, recv,
):
    n = 2 * RING
    me = lax.axis_index("ctx")
    after, before = {"ctx": (me + 1) % n}, {"ctx": (me + n - 1) % n}
    barrier = pltpu.get_barrier_semaphore()
    greet([after, before], barrier)
    pl.semaphore_wait(barrier, 2)
    rows, width = gg.shape

    @pl.when(section_is(1))
    def _():
        pool = Pool(send, recv)
        sems = pool.take(4)
        first = (me > 0).astype(F32)
        final = (me < n - 1).astype(F32)
        a_copy = remote(proj.at[pl.ds(rows - 8, 8)], ptail, sems[0], after)
        for a, count in chunks(0, rows, 32):
            pp[8 + a : 8 + a + count] = proj[a : a + count]

        def products(a, count, group):
            tl = lanes_at(group * 128)
            k = short_rows(pp, taps, 1, a, count, lanes_at(width + group * 128), tl)
            v = short_rows(pp, taps, 2, a, count, lanes_at(2 * width + group * 128), tl)
            return k * v

        @pl.loop(0, 4)
        def _(group):
            tl = lanes_at(group * 128)
            for a, count in chunks(rows // 2, rows, 64):
                value = products(8 + a, count, group)
                prod[REACH + a : REACH + a + count, tl] = value
                qsend[a - rows // 2 : a - rows // 2 + count, tl] = value.astype(BF16)

        b_copy = remote(qsend, qtail, sems[1], after)
        a_copy.wait_recv()
        pp[0:8] = jnp.where(me > 0, ptail[...], 0.0)

        @pl.loop(0, 4)
        def _(group):
            tl = lanes_at(group * 128)
            for a, count in chunks(0, rows, 64):
                value = short_rows(pp, taps, 0, 8 + a, count, tl, tl)
                query[a : a + count, tl] = value
                value = value * gg[a : a + count, tl]
                gf[a : a + count, tl] = value
                gfpad[a : a + count, tl] = value
                if a < REACH:
                    ghead[a : a + count, tl] = value.astype(BF16)
            for a, count in chunks(0, rows // 2, 64):
                prod[REACH + a : REACH + a + count, tl] = products(8 + a, count, group)

        c_copy = remote(ghead, gfar, sems[2], before)
        b_copy.wait_recv()
        for a, count in chunks(0, REACH, 32):
            prod[a : a + count] = jnp.where(me > 0, qtail[a : a + count].astype(F32), 0.0)

        @pl.loop(0, 4)
        def _(group):
            tl = lanes_at(group * 128)
            shifted(shifts, prod, 1, rows + REACH - 8, tl)
            kg[...] = kern[:, tl]
            fir(shifts, kg, ALL, filtered, tl, rows // 8, 8, True)
            for a, count in chunks(0, rows, 64):
                gated_out[a : a + count, tl] = (query[a : a + count, tl] * filtered[a : a + count, tl]).astype(BF16)

        c_copy.wait_recv()
        for a, count in chunks(0, REACH, 32):
            gfpad[rows + a : rows + a + count] = jnp.where(me < n - 1, gfar[a : a + count].astype(F32), 0.0)

        @pl.loop(0, 4)
        def _(group):
            tl = lanes_at(group * 128)
            shifted(shifts, gfpad, 0, rows + REACH - 8, tl)
            kg[...] = kern[:, tl]
            fir(shifts, kg, ALL, gprod, tl, rows // 8, 8, False)
            for a, count in chunks(0, rows, 64):
                here = slice(a, a + count)
                gs[here, tl] = gg[here, tl] * filtered[here, tl]
                k = short_rows(pp, taps, 1, 8 + a, count, lanes_at(width + group * 128), tl)
                v = short_rows(pp, taps, 2, 8 + a, count, lanes_at(2 * width + group * 128), tl)
                gs[here, lanes_at(width + group * 128)] = gprod[here, tl] * v
                gs[here, lanes_at(2 * width + group * 128)] = gprod[here, tl] * k

        for m in range(3):
            gsend[:, m * width : (m + 1) * width] = gs[0:8, m * width : (m + 1) * width]
        d_copy = remote(gsend, sfar, sems[3], before)
        d_copy.wait_recv()
        gs[rows : rows + 8] = jnp.where(me < n - 1, sfar[...], 0.0)
        row_sum[...] = jnp.zeros_like(row_sum)

        @pl.loop(0, 4)
        def _(group):
            tl = lanes_at(group * 128)
            for m in range(3):
                ml = lanes_at(m * width + group * 128)
                sums = [jnp.zeros((8, 128), F32) for _ in range(3)]
                for a, count in chunks(0, rows, 64):
                    total = taps[m : m + 1, tl] * gs[a : a + count, ml]
                    for j in (1, 2):
                        total = total + taps[3 * j + m : 3 * j + m + 1, tl] * gs[a + j : a + j + count, ml]
                    gp_out[a : a + count, ml] = total.astype(BF16)
                    row_sum[a : a + count] += total * pp[8 + a : 8 + a + count, ml]
                    for j in range(3):
                        term = gs[a : a + count, ml] * pp[8 - j + a : 8 - j + a + count, ml]
                        sums[j] = sums[j] + jnp.sum(term.reshape(count // 8, 8, 128), axis=0)
                for j in range(3):
                    sums_out[3 * j + m : 3 * j + m + 1, tl] = jnp.sum(sums[j], axis=0, keepdims=True)

        eye = lax.broadcasted_iota(jnp.int32, (128, 128), 0) == lax.broadcasted_iota(jnp.int32, (128, 128), 1)
        stat_out[...] = jnp.zeros_like(stat_out)
        for k in range(rows // 128):
            column = jnp.sum(row_sum[k * 128 : (k + 1) * 128], axis=1, keepdims=True)
            line = jnp.sum(jnp.where(eye, jnp.broadcast_to(column, (128, 128)), 0.0), axis=0, keepdims=True)
            stat_out[k : k + 1] = line
        for copy in (a_copy, b_copy, c_copy, d_copy):
            copy.wait_send()


def late_kernel(
    part_ref, gp_ref, gated_ref, normed_ref, gf, prod, sums_ref,
    gg_ref, gp_all, gated_all, normed_all, taps_all, shifts, taps_own, *rest,
):
    bufs, (send, recv) = rest[:-2], rest[-2:]
    barrier = pltpu.get_barrier_semaphore()
    ctx = Group("ctx")
    me = lax.axis_index("ctx")
    everyone = [{"ctx": (me + k) % (2 * RING)} for k in range(1, 2 * RING)]
    greet(everyone, barrier)
    pl.semaphore_wait(barrier, 2 * RING - 1)

    @pl.when(section_is(0))
    def _():
        PairThenRing(ctx, part_ref, Pool(send, recv), bufs).run(gg_ref)

    @pl.when(section_is(1))
    def _():
        pool = Pool(send, recv)
        jobs = [
            Gather(ctx, gp_ref, gp_all, pool, False),
            Gather(ctx, gated_ref, gated_all, pool, False),
        ]
        for job in jobs:
            job.start()
        sems = pool.take(8)
        width = normed_all.shape[2]
        columns = lambda k: pl.ds(pl.multiple_of(k * width, width), width)
        own = pltpu.make_async_copy(normed_ref.at[:, columns(me)], normed_all.at[me], sems[7][0])
        own.start()
        sends = []
        for k, device in enumerate(everyone):
            target = (me + k + 1) % (2 * RING)
            sends.append(remote(normed_ref.at[:, columns(target)], normed_all.at[me], sems[k], device))

        @pl.loop(0, 4)
        def _(group):
            tl = lanes_at(group * 128)
            shifted(shifts, prod, 1, gf.shape[0] + REACH - 8, tl)
            lags(shifts, gf, tl, taps_own, tl, gf.shape[0] // 8)

        taps_own[REACH:] = sums_ref[...]
        jobs.append(Gather(ctx, taps_own, taps_all, pool, False))
        jobs[-1].start()
        for job in jobs:
            job.middle()
        for job in jobs:
            job.finish()
        own.wait()
        for copy in sends:
            copy.wait()


def dot(a, b, dims=(((1,), (0,)), ((), ()))):
    return lax.dot_general(a, b, dims, preferred_element_type=F32)


TRANS_B = (((1,), (1,)), ((), ()))
TRANS_A = (((0,), (0,)), ((), ()))


def onehot(ids, count):
    return (ids[:, None] == jnp.arange(count, dtype=jnp.int32)[None, :]).astype(BF16)


def local(
    token_ids, embedding, project_in, short_taps, filter_taps, decay_rates, project_out, cotangent
):
    section_zero = lax.axis_index("section") == 0
    n = lax.axis_size("ctx")
    vocab = embedding.shape[0]
    rows = token_ids.shape[0]
    seq = rows * n
    part = seq // 2
    width = embedding.shape[1]
    chans = project_in.shape[3]
    lane = chans // RING
    taps_all = short_taps[0]
    filter_all = filter_taps[0]
    tap_count = filter_all.shape[0]
    place = lax.axis_index("ctx")
    core, strip = place % 2, place // 2
    base = core * part

    w_flat = project_in[0].reshape(width, 3 * chans)
    w_out = project_out[0]
    positions = jnp.arange(tap_count).astype(F32)
    damping_all = jnp.exp(-decay_rates[0][None, :] * positions[:, None] / tap_count)
    kernel_all = filter_all * damping_all

    own_tokens = jnp.tile(token_ids.reshape(rows // lane, lane), (16 * lane // rows, 1))
    emb, table, inv_table, tokens, w_full, e1 = call(
        begin_kernel,
        1,
        [
            ((vocab, width), BF16),
            ((vocab, 3 * lane), BF16),
            ((vocab, lane), F32),
            ((n, 16, lane), jnp.int32),
            ((n, width, 3 * chans), BF16),
            ((n, rows, width), BF16),
        ],
        [
            pltpu.VMEM((n, vocab // 2, 4 * lane), BF16),
            pltpu.VMEM((rows, width), BF16),
            pltpu.VMEM((vocab // 2, 4 * lane), F32),
        ]
        + PairThenRing.scratch(vocab // 2, 4 * lane),
        32,
        embedding, w_flat, w_flat, cotangent, own_tokens,
        in_specs=[VMEM, VMEM, ANY, VMEM, VMEM],
        out_specs=[VMEM, VMEM, VMEM, VMEM, ANY, VMEM],
        name="begin",
    )
    tokens = tokens[:, : rows // lane].reshape(seq)
    w_full = w_full.reshape(n * width, 3 * chans)

    def strip_of(a):
        return lax.dynamic_slice_in_dim(a, strip * lane, lane, a.ndim - 1)

    taps0, kernel0 = strip_of(taps_all), strip_of(kernel_all)
    at = BACK - 2

    taps0 = taps0.reshape(9, lane)
    taps1 = taps_all.reshape(9, chans)
    rows_id = jnp.arange(vocab, dtype=jnp.int32)

    def own_block0():
        padded = jnp.concatenate(
            [jnp.full((BACK,), -1, jnp.int32), tokens, jnp.full((AHEAD - part,), -1, jnp.int32)]
        )
        seen = lax.dynamic_slice_in_dim(padded, base, BACK + AHEAD, 0)
        proj = dot(onehot(seen, vocab), table)
        mine = lax.dynamic_slice_in_dim(tokens, lax.axis_index("dp") * rows, rows, 0)
        first = dot(onehot(mine, vocab), emb).astype(BF16)
        looked = (rows_id[:, None] == lax.dynamic_slice_in_dim(tokens, base, part, 0)[None, :]).astype(BF16)
        return proj, first, looked, e1

    def own_block1():
        shapes = jax.eval_shape(own_block0)
        blank = jax.tree.map(lambda s: jnp.zeros(s.shape, s.dtype), shapes[:-1])
        grad_part = dot(e1.reshape(seq, width), w_out, TRANS_B).astype(BF16)
        return *blank, grad_part.reshape(n, rows, chans)

    proj0, first, looked, gg1_part = lax.cond(section_zero, own_block0, own_block1)
    gated0_all, gg1, filtered0 = call(
        second_kernel,
        2,
        [((seq, chans), BF16), ((rows, chans), F32), ((KEPT, lane), F32)],
        [
            pltpu.VMEM((BACK + AHEAD, lane), F32),
            pltpu.VMEM((8, KEPT + REACH, lane), F32),
            pltpu.VMEM((part, lane), BF16),
        ]
        + PairThenRing.scratch(rows, chans),
        16,
        proj0, taps0, kernel0, gg1_part,
        name="second",
    )
    out_part = dot(gated0_all, w_out).astype(BF16)
    rows_all, arrived = call(
        forth_kernel,
        3,
        [((n, rows, width), BF16), ((rows, width), BF16)],
        [pltpu.VMEM((rows, width), F32), pltpu.VMEM((rows, width), BF16)]
        + RingThenPair.scratch(rows, width),
        24,
        out_part.reshape(n, rows, width), first,
        name="forth",
    )

    rows_all = jnp.transpose(rows_all, (1, 0, 2)).reshape(rows, n * width)
    rows_float = rows_all.astype(F32)
    inv_rms = lax.rsqrt(jnp.mean(rows_float * rows_float, axis=1, keepdims=True) + EPSILON)
    normed = (rows_float * inv_rms).astype(BF16)
    proj1 = dot(normed, w_full)
    gp1, gated1, stat, sums1, gf1, prod1 = call(
        middle_kernel,
        7,
        [
            ((rows, 3 * chans), BF16),
            ((rows, chans), BF16),
            ((16, lane), F32),
            ((16, chans), F32),
            ((rows, chans), F32),
            ((rows + REACH, chans), F32),
        ],
        [
            pltpu.VMEM((REACH, 128), F32),
            pltpu.VMEM((rows + 8, 3 * chans), F32),
            pltpu.VMEM((rows, chans), F32),
            pltpu.VMEM((rows, chans), F32),
            pltpu.VMEM((rows, chans), F32),
            pltpu.VMEM((rows + 8, 3 * chans), F32),
            pltpu.VMEM((8, rows + REACH, 128), F32),
            pltpu.VMEM((8, 3 * chans), F32),
            pltpu.VMEM((REACH, chans), BF16),
            pltpu.VMEM((REACH, chans), BF16),
            pltpu.VMEM((REACH, chans), BF16),
            pltpu.VMEM((8, 3 * chans), F32),
            pltpu.VMEM((rows + REACH, chans), F32),
            pltpu.VMEM((rows, 128), F32),
            pltpu.VMEM((REACH, chans), BF16),
            pltpu.VMEM((8, 3 * chans), F32),
        ],
        4,
        proj1, gg1, taps1, kernel_all,
        name="middle",
    )
    back_part = dot(gp1, w_full, TRANS_B).astype(BF16)
    back_part = jnp.transpose(back_part.reshape(rows, n, width), (1, 0, 2))
    (e0,) = call(
        back_kernel,
        4,
        [((n, rows, width), BF16)],
        [
            pltpu.VMEM((n, 16, lane), F32),
            pltpu.VMEM((rows, width), BF16),
            pltpu.VMEM((rows, width), F32),
            pltpu.VMEM((rows, width), BF16),
        ]
        + RingThenPair.scratch(rows, width),
        32,
        back_part, stat, inv_rms, cotangent, arrived,
        name="back",
    )
    e0_all = e0.reshape(seq, width)

    gg0_part = dot(e0_all, w_out, TRANS_B).astype(BF16)
    gg0_part = jnp.concatenate([gg0_part, jnp.zeros((AHEAD - part, chans), BF16)], axis=0)
    blocks = jnp.stack(
        [
            gg0_part[c * part : c * part + AHEAD, s * lane : (s + 1) * lane]
            for s in range(RING)
            for c in range(2)
        ]
    )
    gg0, gp1_all, gated1_all, normed1, taps1_all = call(
        late_kernel,
        5,
        [
            ((AHEAD, lane), F32),
            ((n, rows, 3 * chans), BF16),
            ((n, rows, chans), BF16),
            ((n, rows, width), BF16),
            ((n, 144, chans), F32),
        ],
        [pltpu.VMEM((8, rows + REACH, 128), F32), pltpu.VMEM((144, chans), F32)]
        + PairThenRing.scratch(AHEAD, lane),
        40,
        blocks, gp1, gated1, normed, gf1, prod1, sums1,
        in_specs=[VMEM, ANY, ANY, ANY, VMEM, VMEM, VMEM],
        out_specs=[VMEM, ANY, ANY, ANY, VMEM],
        name="late",
    )
    gtab, sums0 = call(
        last_kernel,
        6,
        [((n, vocab // 2, 3 * lane), BF16), ((n, 144, lane), F32)],
        [
            pltpu.VMEM((AHEAD, lane), F32),
            pltpu.VMEM((KEPT, lane), F32),
            pltpu.VMEM((3, KEPT, lane), F32),
            pltpu.VMEM((BACK + AHEAD, lane), F32),
            pltpu.VMEM((8, KEPT + REACH, lane), F32),
            pltpu.VMEM((part, 3 * lane), BF16),
            pltpu.VMEM((vocab, 3 * lane), BF16),
            pltpu.VMEM((144, lane), F32),
            pltpu.VMEM((vocab // 2, 3 * lane), BF16),
            pltpu.VMEM((vocab // 2, 3 * lane), BF16),
        ],
        24,
        gg0, proj0, taps0, kernel0, filtered0, looked,
        name="last",
    )

    def end0():
        table_rows = jnp.transpose(gtab.reshape(RING, 2, vocab // 2, 3, lane), (1, 2, 3, 0, 4))
        normed_table = (emb.astype(F32) * inv_table[:, :1]).astype(BF16)
        sums = sums0.reshape(RING, 2, 144, lane).sum(axis=1)
        return (
            dot(normed_table, table_rows.reshape(vocab, 3 * chans), TRANS_A),
            dot(gated0_all, e0_all, TRANS_A),
            jnp.transpose(sums, (1, 0, 2)).reshape(144, chans),
        )

    def end1():
        return (
            dot(normed1.reshape(seq, width), gp1_all.reshape(seq, 3 * chans), TRANS_A),
            dot(gated1_all.reshape(seq, chans), e1.reshape(seq, width), TRANS_A),
            taps1_all.sum(axis=0),
        )

    grad_in, grad_out, sums = lax.cond(section_zero, end0, end1)
    grad_in = grad_in.reshape(width, 3, chans)
    gk, gt = sums[:tap_count], sums[tap_count : tap_count + 9].reshape(3, 3, chans)
    grad_filter = gk * damping_all
    grad_decay = -jnp.sum(gk * kernel_all * positions[:, None], axis=0) / tap_count
    return (grad_in[None], grad_out[None], grad_filter[None], grad_decay[None], gt[None])


def solution(mesh):
    return jax.shard_map(
        local,
        mesh=mesh,
        in_specs=(
            P("ctx"),
            P(None, "dp"),
            P("section", "ctx", None, "dp"),
            P("section", None, None, "dp"),
            P("section", None, "dp"),
            P("section", "dp"),
            P("section", "dp", "ctx"),
            P("ctx", "dp"),
        ),
        out_specs=(
            P("section", "ctx", None, "dp"),
            P("section", "dp", "ctx"),
            P("section", None, "dp"),
            P("section", "dp"),
            P("section", None, None, "dp"),
        ),
        check_vma=False,
    )
```

time: 560 us -> 421 us (0.75); the launches traced: 551 us -> 418 us
  Pallas kernels: 0 us -> 335 us
  waiting for transfers between devices: 208 us -> 0 us
  blocking collectives: 105 us -> 0 us
  starting transfers between devices: 54.7 us -> 0 us
  matrix products: 75.8 us -> 37.5 us
  other arithmetic: 43.2 us -> 11 us
  local copies, waits for them, and re-layouts: 49.2 us -> 33.4 us
  between operations: 15.2 us -> 0.83 us
    pallas_call x0 -> x7, Pallas kernels: none -> 335 us  [call(): pl.pallas_call(body, out_shape=[jax.ShapeDtypeStruct(shape, dtype) for sh...]
    all_to_all x6 -> x0, waiting for transfers between devices: 134 us -> none  [the longest x5 79.9 us: from_everyone(): return lax.all_to_all(copies, axis, split_axis=0, concat_axis=0, tiled=True)]
    all_to_all x4 -> x0, blocking collectives: 105 us -> none  [the longest x2 65.4 us: summed_on_arrival(): lax.all_to_all(cut_along(shard, dim, peers), axis, 0, 0, tiled=True)]
    all_gather x1 -> x0, waiting for transfers between devices: 46.5 us -> none  [gather_turned(): lax.all_gather(both, axis, axis=0, tiled=True)]
    conv_general_dilated x6 -> x0, matrix products: 31.8 us -> none  [correlate(): lax.conv_general_dilated(signal[None], kernel[:, None, :], (1,), 'VALID',...]
    all_to_all x6 -> x0, starting transfers between devices: 30.6 us -> none  [the longest x5 25.1 us: from_everyone(): return lax.all_to_all(copies, axis, split_axis=0, concat_axis=0, tiled=True)]
    ppermute x10 -> x0, waiting for transfers between devices: 27 us -> none  [from_behind(): lax.ppermute(value, axis, [(source, source + steps) for source in range(i...]
    ppermute x10 -> x0, starting transfers between devices: 23.6 us -> none  [from_behind(): lax.ppermute(value, axis, [(source, source + steps) for source in range(i...]
  transfers between devices with their start and end apart: 18 -> 0, of which waited for: 14 -> 0; matrix products, arithmetic and copies ran while one was open for 13% -> 0% of each run, Pallas kernels for 0% -> 0%
where the time goes in v1:
time: 421 us; the launch traced here: 418 us
  Pallas kernels  335 us (80%)
  matrix products  37.5 us (9%)
  local copies, waits for them, and re-layouts  33.4 us (8%)
  other arithmetic  11 us (3%)
    pallas_call x7, Pallas kernels, call(): pl.pallas_call(body, out_shape=[jax.ShapeDtypeStruct(shape, dtype) for sh...  335 us
    dot_general x8, matrix products, dot(): return lax.dot_general(a, b, dims, preferred_element_type=F32)  37.5 us

profile of v1, /device:TPU:1, one launch (start us, length us, event | category | flops | bytes accessed | tf_op | source)
XLA Modules:
  0.0 418.4 jit_solution(1674942069658216266)
XLA Ops:
  0.7 0.7 neg.14
  1.4 0.7 dynamic-slice_reduce_fusion
  2.7 1.3 tile.11
  3.9 0.8 reduce.3
  5.3 1.1 bitcast_multiply_fusion.kern
  6.4 0.7 constant_dynamic-slice_fusion.kern
  7.1 1.7 copy.101
  8.8 1.6 copy.102.w_ref.w_far
  10.4 57.0 %begin.1 = (bf16[512,512]{1,0:T(8,128)(2,1)}, bf16[512,384]{1,0:T(8,128)(2,1)}, f32[512,128]{1,0:T(8,128)}, s32[8,16,128]{2,1,0:T(8,128)S(1)}, bf16[8,512,1536]{...) custom-call(bf16[512,512]{1,0:T(8,128)(2,1)} %emb_ref.1, bf16[512,1536]{1,0:T(8,128)(2,1)} %copy.102.w_ref.w_far, ...), custom_call_target="tpu_custom_call" | custom-call | tf_op jit(solution)/shard_map/begin/pallas_call | solution.py:300
  67.4 6.9 %conditional.2 = (f32[1320,384]{1,0:T(8,128)S(1)}, bf16[256,512]{1,0:T(8,128)(2,1)S(1)}, bf16[512,1024]{1,0:T(8,128)(2,1)S(1)}, bf16[8,256,512]{2,1,0:T(8,128)(2,1)}) conditional(s32[]{:T(128)} %convert_element_type.66, (bf16[8,256,512]{2,1,0:T(8,128)(2,1)}, bf16[512,512]{1,0:T(8,128)(2,1)S(1)}) %tuple.83, (s32[8,16,128]{2,1,0:T(8,128)S(1)}, ...), branch_computations={%region_0.1_spmd, %region_1.2_spmd} | conditional | flops 1074790400 | bytes 8519863 | solution.py:957
  67.5 1.4 convolution_convert_fusion.1
  69.4 1.9 fusion
  71.3 3.0 copy.134
  74.3 25.9 %second.1 = (bf16[2048,512]{1,0:T(8,128)(2,1)}, f32[256,512]{1,0:T(8,128)}, f32[1040,128]{1,0:T(8,128)}) custom-call(f32[1320,384]{1,0:T(8,128)S(1)} %get-tuple-element.179.proj, f32[9,128]{1,0:T(8,128)} %reshape.123.taps, f32[128,128]{1,0:T(8,128)} %constant_dynamic-slice_fusion.kern, bf16[8,256,512]{2,1,0:T(8,128)(2,1)} %get-tuple-element.180.part_ref), custom_call_target="tpu_custom_call" | custom-call | tf_op jit(solution)/shard_map/second/pallas_call | solution.py:300
  100.3 4.2 convolution_convert_fusion.4
  104.4 74.9 %forth.1 = (bf16[8,256,512]{2,1,0:T(8,128)(2,1)}, bf16[256,512]{1,0:T(8,128)(2,1)}) custom-call(bf16[8,256,512]{2,1,0:T(8,128)(2,1)} %bitcast.116, bf16[256,512]{1,0:T(8,128)(2,1)S(1)} %get-tuple-element.182.first_ref), custom_call_target="tpu_custom_call" | custom-call | tf_op jit(solution)/shard_map/forth/pallas_call | solution.py:300
  179.3 2.1 fusion.6
  181.4 0.8 copy.106.inv_ref
  182.2 9.8 %convolution_bitcast_fusion.3.proj = f32[256,1536]{1,0:T(8,128)} fusion(bf16[8,512,1536]{2,1,0:T(8,128)(2,1)} %get-tuple-element.184, bf16[8,256,512]{2,1,0:T(8,128)(2,1)} %get-tuple-element.183, f32[256]{0:T(256)S(1)} %add_rsqrt_fusion), kind=kOutput, calls=%fused_computation.24 | convolution fusion | flops 3224371200 | bytes 16253952 | tf_op jit(solution)/shard_map/dot_general | solution.py:867
  192.0 3.1 middle.1
  195.2 9.6 %convolution_convert_fusion.2 = bf16[256,4096]{1,0:T(8,128)(2,1)} fusion(bf16[256,1536]{1,0:T(8,128)(2,1)} %get-tuple-element.186.gp_ref, bf16[4096,1536]{1,0:T(8,128)(2,1)} %bitcast.131), kind=kOutput, calls=%fused_computation.18 | convolution fusion | flops 3222274048 | bytes 15466496 | tf_op jit(solution)/shard_map/dot_general | solution.py:867
  204.8 4.1 copy.104
  208.8 3.9 copy.105
  212.7 118.7 %back.1 = bf16[8,256,512]{2,1,0:T(8,128)(2,1)} custom-call(bf16[8,256,512]{2,1,0:T(8,128)(2,1)} %bitcast.107, f32[16,128]{1,0:T(8,128)} %get-tuple-element.187.stat_ref, f32[256,1]{1,0:T(8,128)} %copy.106.inv_ref, bf16[256,512]{1,0:T(8,128)(2,1)} %cot_ref.3, bf16[256,512]{1,0:T(8,128)(2,1)} %get-tuple-element.188.x_ref), custom_call_target="tpu_custom_call" | custom-call | tf_op jit(solution)/shard_map/back/pallas_call | solution.py:300
  331.5 3.0 convolution_convert_fusion.3
  335.1 0.6 copy.126
  335.7 1.9 multiply_convert_fusion.1.normed_ref
  337.6 0.8 fusion.22
  338.4 0.8 fusion.12
  339.1 0.8 fusion.21
  339.9 0.8 fusion.14
  340.6 0.8 fusion.20
  341.4 0.8 fusion.16
  342.1 0.8 fusion.19
  342.9 0.8 fusion.18.part_ref
  343.6 23.3 %late.1 = (f32[1184,128]{1,0:T(8,128)}, bf16[8,256,1536]{2,1,0:T(8,128)(2,1)}, bf16[8,256,512]{2,1,0:T(8,128)(2,1)}, bf16[8,256,512]{2,1,0:T(8,128)(2,1)}, f32[8,144,512]{2,1,0:T(8,128)}) custom-call(bf16[8,1184,128]{2,1,0:T(8,128)(2,1)} %fusion.18.part_ref, bf16[256,1536]{1,0:T(8,128)(2,1)} %get-tuple-element.186.gp_ref, ...), custom_call_target="tpu_custom_call" | custom-call | tf_op jit(solution)/shard_map/late/pallas_call | solution.py:300
  366.9 32.3 %last.1 = (bf16[8,256,384]{2,1,0:T(8,128)(2,1)}, f32[8,144,128]{2,1,0:T(8,128)}) custom-call(f32[1184,128]{1,0:T(8,128)} %get-tuple-element.198.gg, f32[1320,384]{1,0:T(8,128)S(1)} %get-tuple-element.179.proj, f32[9,128]{1,0:T(8,128)} %reshape.123.taps, f32[128,128]{1,0:T(8,128)} %constant_dynamic-slice_fusion.kern, ...), custom_call_target="tpu_custom_call" | custom-call | tf_op jit(solution)/shard_map/last/pallas_call | solution.py:300
  399.3 16.7 %conditional.3 = (f32[1,512,3,512]{3,1,2,0:T(8,128)}, f32[1,512,512]{2,1,0:T(8,128)}, f32[128,512]{1,0:T(8,128)}, f32[1,3,3,512]{3,0,2,1:T(1,128)S(1)}) conditional(s32[]{:T(128)} %convert_element_type.66, (bf16[8,256,512]{2,1,0:T(8,128)(2,1)}, bf16[8,256,1536]{2,1,0:T(8,128)(2,1)}, bf16[8,256,512]{2,1,0:T(8,128)(2,1)}, ...), branch_computations={%region_3.5_spmd, %region_5.7_spmd} | conditional | flops 4295483392 | bytes 59875420 | solution.py:1106
  399.6 1.3 bitcast_reduce_fusion
  401.1 0.8 copy.121
  401.9 1.1 copy.111
  403.0 1.0 copy.110
  404.0 3.8 convolution_bitcast_fusion.2
  407.9 1.7 copy.112
  409.6 1.3 copy.97
  411.5 0.7 copy.98
  412.3 3.7 convolution_bitcast_fusion.1
  416.0 1.8 multiply_reduce_fusion
  (42 shorter events, 3.7 us)
Async XLA Ops:
  6.4 4.0 copy-start.2
  10.4 57.0 %copy-start.9 = (bf16[1,512,512]{2,1,0:T(8,128)(2,1)S(1)}, bf16[1,512,512]{2,1,0:T(8,128)(2,1)}, u32[]{:S(2)}) copy-start(bf16[1,512,512]{2,1,0:T(8,128)(2,1)} %param.18) | copy-start | bytes 1572868
  74.3 25.9 %copy-start.10 = (bf16[1,512,512]{2,1,0:T(8,128)(2,1)S(1)}, bf16[1,512,512]{2,1,0:T(8,128)(2,1)}, u32[]{:S(2)}) copy-start(bf16[1,512,512]{2,1,0:T(8,128)(2,1)} %param.18) | copy-start | bytes 1572868
  212.7 118.7 %copy-start.11 = (bf16[1,512,512]{2,1,0:T(8,128)(2,1)S(1)}, bf16[1,512,512]{2,1,0:T(8,128)(2,1)}, u32[]{:S(2)}) copy-start(bf16[1,512,512]{2,1,0:T(8,128)(2,1)} %param.18) | copy-start | bytes 1572868
  331.5 3.0 copy-start
  399.3 16.7 %copy-start.3 = (f32[1,128,512]{2,1,0:T(8,128)S(1)}, f32[1,128,512]{2,1,0:T(8,128)}, u32[]{:S(2)}) copy-start(f32[1,128,512]{2,1,0:T(8,128)} %param.16) | copy-start | bytes 786436
  399.6 3.4 copy-start.4
  399.6 4.5 %copy-start.1 = (bf16[2048,512]{1,0:T(8,128)(2,1)S(1)}, bf16[2048,512]{1,0:T(8,128)(2,1)}, u32[]{:S(2)}) copy-start(bf16[2048,512]{1,0:T(8,128)(2,1)} %get-tuple-element.136) | copy-start | bytes 6291460 | tf_op jit(solution)/shard_map/cond
  403.0 4.9 %copy-start.5 = (f32[512,128]{0,1:T(8,128)}, f32[512,128]{0,1:T(8,128)S(1)}, u32[]{:S(2)}) copy-start(f32[512,128]{0,1:T(8,128)S(1)} %copy.111) | copy-start | bytes 786436 | tf_op jit(solution)/shard_map/cond
  411.5 0.7 slice-start
  416.0 2.4 copy-start.6

commit v2 on v1

--- a/solution.py
+++ b/solution.py
@@ -328,20 +328,22 @@
 def begin_kernel(
     emb_ref, w_ref, w_far, cot_ref, tok_ref,
     emb_out, table_out, inv_out, tok_out, w_out, e1_out,
-    parts, crossed, half_out, *rest,
+    parts, crossed, half_out, piece, *rest,
 ):
     bufs, (send, recv) = rest[:-2], rest[-2:]
     barrier = pltpu.get_barrier_semaphore()
     ctx, dp = Group("ctx"), Group("dp")
     partner, apart = crossing()
-    greet(ctx.neighbours() + dp.neighbours(), barrier)
+    n = 2 * RING
+    me = lax.axis_index("dp")
+    others = [{"dp": (me + k) % n} for k in range(1, n)]
+    greet(ctx.neighbours() + others, barrier)
 
     @pl.when(apart)
     def _():
         greet([partner], barrier)
 
-    pl.semaphore_wait(barrier, 6 + jnp.where(apart, 1, 0))
-
+    pl.semaphore_wait(barrier, n + 2 + jnp.where(apart, 1, 0))
     lane = 128
     strips = RING
     pool = Pool(send, recv)
@@ -349,30 +351,50 @@
     same_sem = pool.take(1)[0]
     pair_sems = pool.take(2)
 
-    def cross(src, dst):
-        @pl.when(apart)
-        def _():
-            remote(src, dst, cross_sem, partner).wait()
-
-        @pl.when(jnp.logical_not(apart))
-        def _():
-            copy = pltpu.make_async_copy(src, dst, same_sem[0])
-            copy.start()
-            copy.wait()
-
     @pl.when(section_is(0))
     def _():
         mine = Pool(send, recv)
         mine.count = pool.count
         tokens = Gather(ctx, tok_ref, tok_out, mine, False)
         tokens.start()
-        cross(emb_ref, emb_out)
+        spread = mine.take(n - 1)
+        share = piece.shape[0]
+        share_of = lambda k: emb_ref.at[pl.ds(pl.multiple_of(k * share, share), share)]
+        keep = pltpu.make_async_copy(share_of(me), piece, same_sem[0])
+        copies = [
+            pltpu.make_async_remote_copy(
+                src_ref=share_of((me + k + 1) % n), dst_ref=piece, send_sem=spread[k][0],
+                recv_sem=cross_sem[1], device_id=device, device_id_type=MESH,
+            )
+            for k, device in enumerate(others)
+        ]
+
+        @pl.when(jnp.logical_not(apart))
+        def _():
+            for copy in copies:
+                copy.start()
+            keep.start()
+            keep.wait()
+
+        @pl.when(apart)
+        def _():
+            copies[0].wait_recv()
+
+        table_rows = Gather(dp, piece, emb_out, mine, True)
+        table_rows.start()
         tokens.middle()
+        table_rows.middle()
+        table_rows.finish()
+
+        @pl.when(jnp.logical_not(apart))
+        def _():
+            for copy in copies:
+                copy.wait_send()
+
         vocab, width = emb_ref.shape
         hold = vocab // 2
         for core in range(2):
-            rows = pl.ds(core * hold, hold)
-            values = emb_out[rows].astype(F32)
+            values = emb_out[core * RING : (core + 1) * RING].reshape(hold, width).astype(F32)
             square = jnp.broadcast_to(jnp.sum(values * values, axis=1, keepdims=True), (hold, lane)).astype(BF16)
             for strip in range(strips):
                 parts[strip * 2 + core, :, 3 * lane :] = square
@@ -381,7 +403,7 @@
         def _(k):
             strip, m = k // 3, k % 3
             columns = pl.ds(pl.multiple_of(m * strips * lane + strip * lane, lane), lane)
-            product = jnp.dot(emb_out[...], w_ref[:, columns], preferred_element_type=F32).astype(BF16)
+            product = jnp.dot(emb_out[...].reshape(vocab, width), w_ref[:, columns], preferred_element_type=F32).astype(BF16)
             to = pl.ds(pl.multiple_of(m * lane, lane), lane)
             parts[strip * 2, :, to] = product[:hold]
             parts[strip * 2 + 1, :, to] = product[hold:]
@@ -406,12 +428,20 @@
         mine.count = pool.count
         weights = Gather(ctx, w_far, w_out, mine, False)
         weights.start()
-        cross(cot_ref, crossed)
+        there = pltpu.make_async_remote_copy(
+            src_ref=cot_ref, dst_ref=crossed, send_sem=cross_sem[0], recv_sem=cross_sem[1],
+            device_id=partner, device_id_type=MESH,
+        )
+        here = pltpu.make_async_copy(cot_ref, crossed, same_sem[0])
+        pl.when(apart)(there.start)
+        pl.when(jnp.logical_not(apart))(here.start)
+        weights.middle()
+        pl.when(apart)(there.wait)
+        pl.when(jnp.logical_not(apart))(here.wait)
         cots = Gather(dp, crossed, e1_out, mine, True)
         cots.start()
         cots.middle()
         cots.finish()
-        weights.middle()
         weights.finish()
 
 
@@ -423,27 +453,37 @@
     return dp
 
 
-def forth_kernel(part_ref, first_ref, all_ref, arrived_ref, total, block, *rest):
+def reduce_kernel(part_ref, first_ref, out_ref, total, *rest):
     bufs, (send, recv) = rest[:-2], rest[-2:]
+    barrier = pltpu.get_barrier_semaphore()
+    dp = Group("dp")
+
+    @pl.when(section_is(0))
+    def _():
+        greet(dp.neighbours(), barrier)
+        pl.semaphore_wait(barrier, 3)
+        RingThenPair(dp, part_ref, Pool(send, recv), bufs).run(total, [first_ref])
+        out_ref[...] = total[...].astype(BF16)
+
+
+def forth_kernel(block, all_ref, arrived_ref, send, recv):
     dp = relay_barrier()
     pool = Pool(send, recv)
     relay = pool.take(1)[0]
+    copy = pltpu.make_async_remote_copy(
+        src_ref=block, dst_ref=arrived_ref, send_sem=relay[0], recv_sem=relay[1],
+        device_id=other_section(), device_id_type=MESH,
+    )
 
     @pl.when(section_is(0))
     def _():
-        RingThenPair(dp, part_ref, pool, bufs).run(total, [first_ref])
-        block[...] = total[...].astype(BF16)
-        remote(block, arrived_ref, relay, other_section()).wait_send()
+        copy.start()
+        copy.wait_send()
 
     @pl.when(section_is(1))
     def _():
-        mine = Pool(send, recv)
-        mine.count = 1
-        pltpu.make_async_remote_copy(
-            src_ref=block, dst_ref=arrived_ref, send_sem=relay[0], recv_sem=relay[1],
-            device_id=other_section(), device_id_type=MESH,
-        ).wait_recv()
-        rows = Gather(dp, arrived_ref, all_ref, mine, True)
+        copy.wait_recv()
+        rows = Gather(dp, arrived_ref, all_ref, pool, True)
         rows.start()
         rows.middle()
         rows.finish()
@@ -811,8 +851,8 @@
 
 
 def late_kernel(
-    part_ref, gp_ref, gated_ref, normed_ref, gf, prod, sums_ref,
-    gg_ref, gp_all, gated_all, normed_all, taps_all, shifts, taps_own, *rest,
+    e0_ref, w_ref, gp_ref, gated_ref, normed_ref, gf, prod, sums_ref,
+    gg_ref, gp_all, gated_all, normed_all, taps_all, shifts, taps_own, part_ref, *rest,
 ):
     bufs, (send, recv) = rest[:-2], rest[-2:]
     barrier = pltpu.get_barrier_semaphore()
@@ -824,6 +864,18 @@
 
     @pl.when(section_is(0))
     def _():
+        count, rows, _ = e0_ref.shape
+        for k in range(count):
+            product = dot(e0_ref[k], w_ref[...], TRANS_B).astype(BF16)
+            core, first = divmod(k * rows, count // 2 * rows)
+            for strip in range(RING):
+                part = product[:, strip * 128 : (strip + 1) * 128]
+                part_ref[strip * 2 + core, first : first + rows] = part
+                if core == 1 and first == 0:
+                    part_ref[strip * 2, count // 2 * rows : AHEAD] = part[: AHEAD - count // 2 * rows]
+        over = AHEAD - count // 2 * rows
+        for strip in range(RING):
+            part_ref[strip * 2 + 1, count // 2 * rows : AHEAD] = jnp.zeros((over, 128), BF16)
         PairThenRing(ctx, part_ref, Pool(send, recv), bufs).run(gg_ref)
 
     @pl.when(section_is(1))
@@ -905,7 +957,7 @@
         begin_kernel,
         1,
         [
-            ((vocab, width), BF16),
+            ((n, vocab // n, width), BF16),
             ((vocab, 3 * lane), BF16),
             ((vocab, lane), F32),
             ((n, 16, lane), jnp.int32),
@@ -916,9 +968,10 @@
             pltpu.VMEM((n, vocab // 2, 4 * lane), BF16),
             pltpu.VMEM((rows, width), BF16),
             pltpu.VMEM((vocab // 2, 4 * lane), F32),
+            pltpu.VMEM((vocab // n, width), BF16),
         ]
         + PairThenRing.scratch(vocab // 2, 4 * lane),
-        32,
+        48,
         embedding, w_flat, w_flat, cotangent, own_tokens,
         in_specs=[VMEM, VMEM, ANY, VMEM, VMEM],
         out_specs=[VMEM, VMEM, VMEM, VMEM, ANY, VMEM],
@@ -926,6 +979,7 @@
     )
     tokens = tokens[:, : rows // lane].reshape(seq)
     w_full = w_full.reshape(n * width, 3 * chans)
+    emb = emb.reshape(vocab, width)
 
     def strip_of(a):
         return lax.dynamic_slice_in_dim(a, strip * lane, lane, a.ndim - 1)
@@ -970,14 +1024,22 @@
         name="second",
     )
     out_part = dot(gated0_all, w_out).astype(BF16)
+    (second,) = call(
+        reduce_kernel,
+        3,
+        [((rows, width), BF16)],
+        [pltpu.VMEM((rows, width), F32)] + RingThenPair.scratch(rows, width),
+        24,
+        out_part.reshape(n, rows, width), first,
+        name="reduce",
+    )
     rows_all, arrived = call(
         forth_kernel,
-        3,
+        8,
         [((n, rows, width), BF16), ((rows, width), BF16)],
-        [pltpu.VMEM((rows, width), F32), pltpu.VMEM((rows, width), BF16)]
-        + RingThenPair.scratch(rows, width),
+        [],
         24,
-        out_part.reshape(n, rows, width), first,
+        second,
         name="forth",
     )
 
@@ -1038,15 +1100,6 @@
     )
     e0_all = e0.reshape(seq, width)
 
-    gg0_part = dot(e0_all, w_out, TRANS_B).astype(BF16)
-    gg0_part = jnp.concatenate([gg0_part, jnp.zeros((AHEAD - part, chans), BF16)], axis=0)
-    blocks = jnp.stack(
-        [
-            gg0_part[c * part : c * part + AHEAD, s * lane : (s + 1) * lane]
-            for s in range(RING)
-            for c in range(2)
-        ]
-    )
     gg0, gp1_all, gated1_all, normed1, taps1_all = call(
         late_kernel,
         5,
@@ -1057,11 +1110,11 @@
             ((n, rows, width), BF16),
             ((n, 144, chans), F32),
         ],
-        [pltpu.VMEM((8, rows + REACH, 128), F32), pltpu.VMEM((144, chans), F32)]
+        [pltpu.VMEM((8, rows + REACH, 128), F32), pltpu.VMEM((144, chans), F32), pltpu.VMEM((n, AHEAD, lane), BF16)]
         + PairThenRing.scratch(AHEAD, lane),
         40,
-        blocks, gp1, gated1, normed, gf1, prod1, sums1,
-        in_specs=[VMEM, ANY, ANY, ANY, VMEM, VMEM, VMEM],
+        e0, w_out, gp1, gated1, normed, gf1, prod1, sums1,
+        in_specs=[VMEM, VMEM, ANY, ANY, ANY, VMEM, VMEM, VMEM],
         out_specs=[VMEM, ANY, ANY, ANY, VMEM],
         name="late",
     )

time: 421 us -> 387 us (0.919)
  Pallas kernels: 335 us -> 310 us
  local copies, waits for them, and re-layouts: 33.4 us -> 27.4 us
    pallas_call x7 -> x8, Pallas kernels: 335 us -> 310 us  [call(): pl.pallas_call(body, out_shape=[jax.ShapeDtypeStruct(shape, dtype) for sh...]
    unnamed x22 -> x13, local copies, waits for them, and re-layouts: 7.02 us -> 1.74 us
    dot_general x8 -> x7, matrix products: 37.5 us -> 34.4 us  [dot(): return lax.dot_general(a, b, dims, preferred_element_type=F32)]
where the time goes in v2:
time: 387 us; the launch traced here: 386 us
  Pallas kernels  310 us (80%)
  matrix products  34.4 us (9%)
  local copies, waits for them, and re-layouts  27.4 us (7%)
  other arithmetic  12.5 us (3%)
    pallas_call x8, Pallas kernels, call(): pl.pallas_call(body, out_shape=[jax.ShapeDtypeStruct(shape, dtype) for sh...  310 us
    dot_general x7, matrix products, dot(): return lax.dot_general(a, b, dims, preferred_element_type=F32)  34.4 us

profile of v2, /device:TPU:1, one launch (start us, length us, event | category | flops | bytes accessed | tf_op | source)
XLA Modules:
  0.0 386.1 jit_solution(17737367646606870216)
XLA Ops:
  0.7 0.7 neg.14
  1.4 0.7 dynamic-slice_reduce_fusion
  2.1 0.6 reshape.129.taps
  2.7 1.3 tile.11
  4.0 0.8 reduce.4
  4.7 0.6 reshape_squeeze.7.taps
  5.3 1.1 bitcast_multiply_fusion.kern
  6.4 0.7 constant_dynamic-slice_fusion.kern
  7.1 1.7 copy.101
  8.8 1.6 copy.102.w_ref.w_far
  10.4 45.1 %begin.1 = (bf16[8,64,512]{2,1,0:T(8,128)(2,1)}, bf16[512,384]{1,0:T(8,128)(2,1)}, f32[512,128]{1,0:T(8,128)}, s32[8,16,128]{2,1,0:T(8,128)S(1)}, bf16[8,512,153...) custom-call(bf16[512,512]{1,0:T(8,128)(2,1)} %emb_ref.1, bf16[512,1536]{1,0:T(8,128)(2,1)} %copy.102.w_ref.w_far, ...), custom_call_target="tpu_custom_call" | custom-call | tf_op jit(solution)/shard_map/begin/pallas_call | solution.py:300
  55.5 6.9 %conditional.2 = (f32[1320,384]{1,0:T(8,128)S(1)}, bf16[256,512]{1,0:T(8,128)(2,1)S(1)}, bf16[512,1024]{1,0:T(8,128)(2,1)S(1)}, bf16[8,256,512]{2,1,0:T(8,128)(2,1)}) conditional(s32[]{:T(128)} %convert_element_type.63, (bf16[8,256,512]{2,1,0:T(8,128)(2,1)}, bf16[512,512]{1,0:T(8,128)(2,1)S(1)}) %tuple.82, (s32[8,16,128]{2,1,0:T(8,128)S(1)}, ...), branch_computations={%region_0.1_spmd, %region_1.2_spmd} | conditional | flops 1074790400 | bytes 8519863 | solution.py:1011
  55.6 0.1 dynamic_slice.17
  55.7 1.4 convolution_convert_fusion.1
  57.3 0.2 compare_convert_fusion
  57.5 1.9 fusion
  59.4 3.0 copy.134
  62.5 25.6 %second.1 = (bf16[2048,512]{1,0:T(8,128)(2,1)}, f32[256,512]{1,0:T(8,128)}, f32[1040,128]{1,0:T(8,128)}) custom-call(f32[1320,384]{1,0:T(8,128)S(1)} %get-tuple-element.180.proj, f32[9,128]{1,0:T(8,128)} %reshape.129.taps, f32[128,128]{1,0:T(8,128)} %constant_dynamic-slice_fusion.kern, bf16[8,256,512]{2,1,0:T(8,128)(2,1)} %get-tuple-element.181.part_ref), custom_call_target="tpu_custom_call" | custom-call | tf_op jit(solution)/shard_map/second/pallas_call | solution.py:300
  88.1 4.2 %convolution_convert_fusion.3 = bf16[2048,512]{1,0:T(8,128)(2,1)} fusion(bf16[2048,512]{1,0:T(8,128)(2,1)} %get-tuple-element.182, bf16[1,512,512]{2,1,0:T(8,128)(2,1)S(1)} %copy-done.4), kind=kOutput, calls=%fused_computation.22 | convolution fusion | flops 1074790400 | bytes 4718592 | tf_op jit(solution)/shard_map/dot_general | solution.py:919
  92.3 27.2 %reduce.6.block = bf16[256,512]{1,0:T(8,128)(2,1)} custom-call(bf16[8,256,512]{2,1,0:T(8,128)(2,1)} %bitcast.81, bf16[256,512]{1,0:T(8,128)(2,1)S(1)} %get-tuple-element.183.first_ref), custom_call_target="tpu_custom_call" | custom-call | tf_op jit(solution)/shard_map/reduce/pallas_call | solution.py:300
  119.4 24.6 %forth.1 = (bf16[8,256,512]{2,1,0:T(8,128)(2,1)}, bf16[256,512]{1,0:T(8,128)(2,1)}) custom-call(bf16[256,512]{1,0:T(8,128)(2,1)} %reduce.6.block), custom_call_target="tpu_custom_call" | custom-call | tf_op jit(solution)/shard_map/forth/pallas_call | solution.py:300
  144.0 2.1 fusion.6
  146.1 0.8 copy.106.inv_ref
  146.9 9.8 %convolution_bitcast_fusion.3.proj = f32[256,1536]{1,0:T(8,128)} fusion(bf16[8,512,1536]{2,1,0:T(8,128)(2,1)} %get-tuple-element.185, bf16[8,256,512]{2,1,0:T(8,128)(2,1)} %get-tuple-element.184, f32[256]{0:T(256)S(1)} %add_rsqrt_fusion), kind=kOutput, calls=%fused_computation.23 | convolution fusion | flops 3224371200 | bytes 16253952 | tf_op jit(solution)/shard_map/dot_general | solution.py:919
  156.7 9.0 %middle.1 = (bf16[256,1536]{1,0:T(8,128)(2,1)}, bf16[256,512]{1,0:T(8,128)(2,1)}, f32[16,128]{1,0:T(8,128)}, f32[16,512]{1,0:T(8,128)}, f32[256,512]{1,0:T(8,128)}, /*index=5*/f32[384,512]{1,0:T(8,128)}) custom-call(f32[256,1536]{1,0:T(8,128)} %convolution_bitcast_fusion.3.proj, f32[256,512]{1,0:T(8,128)} %get-tuple-element.186.gg, ...), custom_call_target="tpu_custom_call" | custom-call | tf_op jit(solution)/shard_map/middle/pallas_call | solution.py:300
  165.7 9.6 %convolution_convert_fusion.2 = bf16[256,4096]{1,0:T(8,128)(2,1)} fusion(bf16[256,1536]{1,0:T(8,128)(2,1)} %get-tuple-element.187.gp_ref, bf16[4096,1536]{1,0:T(8,128)(2,1)} %bitcast.100), kind=kOutput, calls=%fused_computation.18 | convolution fusion | flops 3222274048 | bytes 15466496 | tf_op jit(solution)/shard_map/dot_general | solution.py:919
  175.3 4.1 %copy.104 = bf16[256,4096]{0,1:T(8,128)(2,1)} copy(bf16[256,4096]{1,0:T(8,128)(2,1)} %convolution_convert_fusion.2) | data formatting | bytes 4194304 | tf_op jit(solution)/shard_map/convert_element_type | solution.py:1084
  179.4 3.9 %copy.105 = bf16[256,8,512]{2,0,1:T(8,128)(2,1)} copy(bf16[256,8,512]{0,2,1:T(8,128)(2,1)} %bitcast.75) | data formatting | bytes 4194304 | tf_op jit(solution)/shard_map/reshape | solution.py:1085
  183.3 122.1 %back.1.e0_ref = bf16[8,256,512]{2,1,0:T(8,128)(2,1)} custom-call(bf16[8,256,512]{2,1,0:T(8,128)(2,1)} %bitcast.74, f32[16,128]{1,0:T(8,128)} %get-tuple-element.188.stat_ref, f32[256,1]{1,0:T(8,128)} %copy.106.inv_ref, bf16[256,512]{1,0:T(8,128)(2,1)} %cot_ref.3, bf16[256,512]{1,0:T(8,128)(2,1)} %get-tuple-element.189.x_ref), custom_call_target="tpu_custom_call" | custom-call | tf_op jit(solution)/shard_map/back/pallas_call | solution.py:300
  305.5 2.2 convert_bitcast_fusion
  307.6 0.6 copy.126
  308.3 1.8 multiply_convert_fusion.1.normed_ref
  310.1 24.6 %late.1 = (f32[1184,128]{1,0:T(8,128)}, bf16[8,256,1536]{2,1,0:T(8,128)(2,1)}, bf16[8,256,512]{2,1,0:T(8,128)(2,1)}, bf16[8,256,512]{2,1,0:T(8,128)(2,1)}, f32[8,144,512]{2,1,0:T(8,128)}) custom-call(bf16[8,256,512]{2,1,0:T(8,128)(2,1)} %back.1.e0_ref, bf16[512,512]{1,0:T(8,128)(2,1)S(1)} %bitcast.86, bf16[256,1536]{1,0:T(8,128)(2,1)} %get-tuple-element.187.gp_ref, ...), custom_call_target="tpu_custom_call" | custom-call | tf_op jit(solution)/shard_map/late/pallas_call | solution.py:300
  334.6 32.3 %last.1 = (bf16[8,256,384]{2,1,0:T(8,128)(2,1)}, f32[8,144,128]{2,1,0:T(8,128)}) custom-call(f32[1184,128]{1,0:T(8,128)} %get-tuple-element.199.gg, f32[1320,384]{1,0:T(8,128)S(1)} %get-tuple-element.180.proj, f32[9,128]{1,0:T(8,128)} %reshape.129.taps, f32[128,128]{1,0:T(8,128)} %constant_dynamic-slice_fusion.kern, ...), custom_call_target="tpu_custom_call" | custom-call | tf_op jit(solution)/shard_map/last/pallas_call | solution.py:300
  367.0 16.7 %conditional.3 = (f32[1,512,3,512]{3,1,2,0:T(8,128)}, f32[1,512,512]{2,1,0:T(8,128)}, f32[128,512]{1,0:T(8,128)}, f32[1,3,3,512]{3,0,2,1:T(1,128)S(1)}) conditional(s32[]{:T(128)} %convert_element_type.63, (bf16[8,256,512]{2,1,0:T(8,128)(2,1)}, bf16[8,256,1536]{2,1,0:T(8,128)(2,1)}, bf16[8,256,512]{2,1,0:T(8,128)(2,1)}, ...), branch_computations={%region_3.5_spmd, %region_5.7_spmd} | conditional | flops 4295483392 | bytes 59875420 | solution.py:1159
  367.3 1.3 bitcast_reduce_fusion
  368.6 0.1 copy.99
  368.8 0.8 copy.121
  369.6 1.1 copy.111
  370.7 1.0 copy.110
  371.7 3.8 convolution_bitcast_fusion.2
  375.6 1.7 copy.112
  377.3 1.3 copy.97
  378.6 0.6 reshape.120
  379.2 0.7 copy.98
  380.0 3.7 convolution_bitcast_fusion.1
  383.7 1.8 multiply_reduce_fusion
  385.5 0.6 negate_multiply_fusion
  (32 shorter events, 0.3 us)
Async XLA Ops:
  6.4 4.0 %copy-start.1 = (f32[128,512]{1,0:T(8,128)}, f32[128,512]{1,0:T(8,128)S(1)}, u32[]{:S(2)}) copy-start(f32[128,512]{1,0:T(8,128)S(1)} %bitcast_multiply_fusion.kern) | copy-start | bytes 786436
  10.4 45.1 %copy-start.3 = (bf16[1,512,512]{2,1,0:T(8,128)(2,1)S(1)}, bf16[1,512,512]{2,1,0:T(8,128)(2,1)}, u32[]{:S(2)}) copy-start(bf16[1,512,512]{2,1,0:T(8,128)(2,1)} %param.18) | copy-start | bytes 1572868
  62.5 25.6 %copy-start.4 = (bf16[1,512,512]{2,1,0:T(8,128)(2,1)S(1)}, bf16[1,512,512]{2,1,0:T(8,128)(2,1)}, u32[]{:S(2)}) copy-start(bf16[1,512,512]{2,1,0:T(8,128)(2,1)} %param.18) | copy-start | bytes 1572868
  308.3 1.8 copy-start.5
  367.0 16.7 %copy-start.2 = (f32[1,128,512]{2,1,0:T(8,128)S(1)}, f32[1,128,512]{2,1,0:T(8,128)}, u32[]{:S(2)}) copy-start(f32[1,128,512]{2,1,0:T(8,128)} %param.16) | copy-start | bytes 786436
  367.3 3.4 copy-start.6
  367.3 4.5 %copy-start = (bf16[8,256,512]{2,1,0:T(8,128)(2,1)S(1)}, bf16[8,256,512]{2,1,0:T(8,128)(2,1)}, u32[]{:S(2)}) copy-start(bf16[8,256,512]{2,1,0:T(8,128)(2,1)} %get-tuple-element.137) | copy-start | bytes 6291460 | tf_op jit(solution)/shard_map/cond
  370.7 4.9 %copy-start.7 = (f32[512,128]{0,1:T(8,128)}, f32[512,128]{0,1:T(8,128)S(1)}, u32[]{:S(2)}) copy-start(f32[512,128]{0,1:T(8,128)S(1)} %copy.111) | copy-start | bytes 786436 | tf_op jit(solution)/shard_map/cond
  379.2 0.7 slice-start
  383.7 2.4 copy-start.8

commit v3 on v2

--- a/solution.py
+++ b/solution.py
@@ -273,13 +273,17 @@
             + Around.scratch(rows, lanes)
         )
 
-    def run(self, out, extra=()):
+    def run(self, out, extra=(), produce=lambda slot: None):
         g = self.g
         pairs = [g.mate, g.pair]
         blocks = lambda ring, pair: self.inp.at[g.slot(ring, pair)]
         for ring, pair in zip(self.rings, pairs):
+            produce(g.slot(g.across, pair))
             ring.send_across(blocks(g.across, pair))
+            produce(g.slot(g.right, pair))
+            produce(g.slot(g.left, pair))
             ring.send_near(blocks(g.right, pair), blocks(g.left, pair))
+            produce(g.slot(g.ring, pair))
         self.rings[0].merge()
         self.rings[1].merge()
         self.rings[0].collect(self.far, [blocks(g.ring, g.mate)])
@@ -296,14 +300,15 @@
 VMEM = pl.BlockSpec(memory_space=pltpu.VMEM)
 
 
-def call(body, ident, outs, scratch, sems, *args, in_specs=None, out_specs=None, name=None):
+def call(body, ident, outs, scratch, sems, *args, in_specs=None, out_specs=None, name=None, local=0):
     return pl.pallas_call(
         body,
         out_shape=[jax.ShapeDtypeStruct(shape, dtype) for shape, dtype in outs],
         in_specs=in_specs or [VMEM] * len(args),
         out_specs=out_specs or [VMEM] * len(outs),
         scratch_shapes=list(scratch)
-        + [pltpu.SemaphoreType.DMA((sems,)), pltpu.SemaphoreType.DMA((sems,))],
+        + [pltpu.SemaphoreType.DMA((sems,)), pltpu.SemaphoreType.DMA((sems,))]
+        + ([pltpu.SemaphoreType.DMA((local,))] if local else []),
         compiler_params=pltpu.CompilerParams(
             collective_id=ident, has_side_effects=True, vmem_limit_bytes=60 * 1024 * 1024
         ),
@@ -427,7 +432,6 @@
         mine = Pool(send, recv)
         mine.count = pool.count
         weights = Gather(ctx, w_far, w_out, mine, False)
-        weights.start()
         there = pltpu.make_async_remote_copy(
             src_ref=cot_ref, dst_ref=crossed, send_sem=cross_sem[0], recv_sem=cross_sem[1],
             device_id=partner, device_id_type=MESH,
@@ -435,22 +439,15 @@
         here = pltpu.make_async_copy(cot_ref, crossed, same_sem[0])
         pl.when(apart)(there.start)
         pl.when(jnp.logical_not(apart))(here.start)
-        weights.middle()
         pl.when(apart)(there.wait)
         pl.when(jnp.logical_not(apart))(here.wait)
+        weights.start()
         cots = Gather(dp, crossed, e1_out, mine, True)
         cots.start()
         cots.middle()
         cots.finish()
+        weights.middle()
         weights.finish()
-
-
-def relay_barrier():
-    barrier = pltpu.get_barrier_semaphore()
-    dp = Group("dp")
-    greet(dp.neighbours() + [other_section()], barrier)
-    pl.semaphore_wait(barrier, 4)
-    return dp
 
 
 def reduce_kernel(part_ref, first_ref, out_ref, total, *rest):
@@ -464,76 +461,6 @@
         pl.semaphore_wait(barrier, 3)
         RingThenPair(dp, part_ref, Pool(send, recv), bufs).run(total, [first_ref])
         out_ref[...] = total[...].astype(BF16)
-
-
-def forth_kernel(block, all_ref, arrived_ref, send, recv):
-    dp = relay_barrier()
-    pool = Pool(send, recv)
-    relay = pool.take(1)[0]
-    copy = pltpu.make_async_remote_copy(
-        src_ref=block, dst_ref=arrived_ref, send_sem=relay[0], recv_sem=relay[1],
-        device_id=other_section(), device_id_type=MESH,
-    )
-
-    @pl.when(section_is(0))
-    def _():
-        copy.start()
-        copy.wait_send()
-
-    @pl.when(section_is(1))
-    def _():
-        copy.wait_recv()
-        rows = Gather(dp, arrived_ref, all_ref, pool, True)
-        rows.start()
-        rows.middle()
-        rows.finish()
-
-
-def back_kernel(
-    part_ref, stat_ref, inv_ref, cot_ref, x_ref, all_ref, stats, arrived, total, block, *rest
-):
-    bufs, (send, recv) = rest[:-2], rest[-2:]
-    dp = relay_barrier()
-    pool = Pool(send, recv)
-    relay = pool.take(1)[0]
-
-    @pl.when(section_is(1))
-    def _():
-        stat = Gather(dp, stat_ref, stats, pool, True)
-        stat.start()
-        stat.middle()
-        RingThenPair(dp, part_ref, pool, bufs).run(total)
-        stat.finish()
-        rows, width = total.shape
-        lane = 128
-        summed = stats[0]
-        for k in range(1, 8):
-            summed = summed + stats[k]
-        eye = lax.broadcasted_iota(jnp.int32, (lane, lane), 0) == lax.broadcasted_iota(jnp.int32, (lane, lane), 1)
-        for k in range(rows // lane):
-            here = pl.ds(k * lane, lane)
-            line = jnp.broadcast_to(summed[k : k + 1], (lane, lane))
-            scalar = jnp.sum(jnp.where(eye, line, 0.0), axis=1, keepdims=True)
-            inv = inv_ref[here]
-            block[here] = (
-                cot_ref[here].astype(F32)
-                + inv * total[here]
-                - x_ref[here].astype(F32) * (inv * inv * scalar / (width * 2 * RING))
-            ).astype(BF16)
-        remote(block, arrived, relay, other_section()).wait_send()
-
-    @pl.when(section_is(0))
-    def _():
-        mine = Pool(send, recv)
-        mine.count = 1
-        pltpu.make_async_remote_copy(
-            src_ref=block, dst_ref=arrived, send_sem=relay[0], recv_sem=relay[1],
-            device_id=other_section(), device_id_type=MESH,
-        ).wait_recv()
-        rows = Gather(dp, arrived, all_ref, mine, True)
-        rows.start()
-        rows.middle()
-        rows.finish()
 
 
 REACH = 128
@@ -729,27 +656,79 @@
         job.finish()
 
 
-def middle_kernel(
-    proj, gg, taps, kern, gp_out, gated_out, stat_out, sums_out, gf, prod,
-    kg, pp, query, filtered, gprod, gs, shifts, ptail, qtail, ghead, gfar, sfar, gfpad, row_sum, qsend, gsend, send, recv,
+def block1_kernel(
+    x_ref, w_far, gg, cot, taps, kern,
+    all_ref, e0_ref, gp_out, gated_out, sums_out, gf, prod,
+    arrived, returned, wv, square, inv_ref, gpb, part, stats, stat_own, total_ref, block,
+    kg, pp, query, filtered, gprod, gs, shifts, ptail, qtail, ghead, gfar, sfar, gfpad, row_sum, qsend, gsend, *rest,
 ):
+    bufs, (send, recv, local_sem) = rest[:-3], rest[-3:]
     n = 2 * RING
     me = lax.axis_index("ctx")
+    dp = Group("dp")
     after, before = {"ctx": (me + 1) % n}, {"ctx": (me + n - 1) % n}
     barrier = pltpu.get_barrier_semaphore()
-    greet([after, before], barrier)
-    pl.semaphore_wait(barrier, 2)
+    greet([after, before] + dp.neighbours() + [other_section()], barrier)
+    pl.semaphore_wait(barrier, 6)
     rows, width = gg.shape
+    pool = Pool(send, recv)
+    relay = pool.take(2)
+    forth = pltpu.make_async_remote_copy(
+        src_ref=x_ref, dst_ref=arrived, send_sem=relay[0][0], recv_sem=relay[0][1],
+        device_id=other_section(), device_id_type=MESH,
+    )
+    back = pltpu.make_async_remote_copy(
+        src_ref=block, dst_ref=returned, send_sem=relay[1][0], recv_sem=relay[1][1],
+        device_id=other_section(), device_id_type=MESH,
+    )
+
+    @pl.when(section_is(0))
+    def _():
+        mine = Pool(send, recv)
+        mine.count = 2
+        forth.start()
+        back.wait_recv()
+        gather = Gather(dp, returned, e0_ref, mine, True)
+        gather.start()
+        gather.middle()
+        gather.finish()
+        forth.wait_send()
 
     @pl.when(section_is(1))
     def _():
-        pool = Pool(send, recv)
+        load = pltpu.make_async_copy(w_far, wv, local_sem.at[0])
+        load.start()
+        forth.wait_recv()
+        gather = Gather(dp, arrived, all_ref, pool, True)
+        gather.start()
+        load.wait()
+
+        def use(ref, slot, begin=False):
+            values = ref[...]
+            for m in range(3):
+                ml = slice(m * width, (m + 1) * width)
+                term = dot(values, wv[slot, :, ml])
+                pp[8:, ml] = term if begin else pp[8:, ml] + term
+            term = jnp.zeros((rows, 128), F32)
+            for g in range(width // 128):
+                v = values[:, g * 128 : (g + 1) * 128].astype(F32)
+                term = term + v * v
+            square[...] = term if begin else square[...] + term
+
+        use(arrived, dp.slot(dp.ring, dp.pair), True)
+        gather.middle()
+        for ring, pair in ((dp.left, dp.pair), (dp.right, dp.pair), (dp.ring, dp.mate), (dp.left, dp.mate), (dp.right, dp.mate)):
+            use(gather.block(ring, pair), dp.slot(ring, pair))
+        gather.finish()
+        for pair in (dp.pair, dp.mate):
+            use(gather.block(dp.across, pair), dp.slot(dp.across, pair))
+        inv = lax.rsqrt(jnp.sum(square[...], axis=1, keepdims=True) / (width * n) + EPSILON)
+        inv_ref[...] = jnp.broadcast_to(inv, (rows, 128))
+        for a, count in chunks(0, rows, 32):
+            pp[8 + a : 8 + a + count] = pp[8 + a : 8 + a + count] * inv_ref[a : a + count, :1]
+
         sems = pool.take(4)
-        first = (me > 0).astype(F32)
-        final = (me < n - 1).astype(F32)
-        a_copy = remote(proj.at[pl.ds(rows - 8, 8)], ptail, sems[0], after)
-        for a, count in chunks(0, rows, 32):
-            pp[8 + a : 8 + a + count] = proj[a : a + count]
+        a_copy = remote(pp.at[pl.ds(rows, 8)], ptail, sems[0], after)
 
         def products(a, count, group):
             tl = lanes_at(group * 128)
@@ -832,7 +811,8 @@
                     total = taps[m : m + 1, tl] * gs[a : a + count, ml]
                     for j in (1, 2):
                         total = total + taps[3 * j + m : 3 * j + m + 1, tl] * gs[a + j : a + j + count, ml]
-                    gp_out[a : a + count, ml] = total.astype(BF16)
+                    gpb[a : a + count, ml] = total.astype(BF16)
+                    gp_out[a : a + count, ml] = (total * inv_ref[a : a + count]).astype(BF16)
                     row_sum[a : a + count] += total * pp[8 + a : 8 + a + count, ml]
                     for j in range(3):
                         term = gs[a : a + count, ml] * pp[8 - j + a : 8 - j + a + count, ml]
@@ -841,13 +821,37 @@
                     sums_out[3 * j + m : 3 * j + m + 1, tl] = jnp.sum(sums[j], axis=0, keepdims=True)
 
         eye = lax.broadcasted_iota(jnp.int32, (128, 128), 0) == lax.broadcasted_iota(jnp.int32, (128, 128), 1)
-        stat_out[...] = jnp.zeros_like(stat_out)
+        stat_own[...] = jnp.zeros_like(stat_own)
         for k in range(rows // 128):
             column = jnp.sum(row_sum[k * 128 : (k + 1) * 128], axis=1, keepdims=True)
             line = jnp.sum(jnp.where(eye, jnp.broadcast_to(column, (128, 128)), 0.0), axis=0, keepdims=True)
-            stat_out[k : k + 1] = line
+            stat_own[k : k + 1] = line
+        stat = Gather(dp, stat_own, stats, pool, True)
+        stat.start()
+
+        def produce(slot):
+            part[slot] = dot(gpb[...], wv[slot], TRANS_B).astype(BF16)
+
+        RingThenPair(dp, part, pool, bufs).run(total_ref, produce=produce)
+        stat.middle()
+        stat.finish()
+        summed = stats[0]
+        for k in range(1, n):
+            summed = summed + stats[k]
+        for k in range(rows // 128):
+            here = pl.ds(k * 128, 128)
+            line = jnp.broadcast_to(summed[k : k + 1], (128, 128))
+            scalar = jnp.sum(jnp.where(eye, line, 0.0), axis=1, keepdims=True)
+            inv = inv_ref[here, :1]
+            block[here] = (
+                cot[here].astype(F32)
+                + inv * total_ref[here]
+                - arrived[here].astype(F32) * (inv * inv * scalar / (width * n))
+            ).astype(BF16)
+        back.start()
         for copy in (a_copy, b_copy, c_copy, d_copy):
             copy.wait_send()
+        back.wait_send()
 
 
 def late_kernel(
@@ -888,14 +892,12 @@
         for job in jobs:
             job.start()
         sems = pool.take(8)
-        width = normed_all.shape[2]
-        columns = lambda k: pl.ds(pl.multiple_of(k * width, width), width)
-        own = pltpu.make_async_copy(normed_ref.at[:, columns(me)], normed_all.at[me], sems[7][0])
+        own = pltpu.make_async_copy(normed_ref.at[me], normed_all.at[me], sems[7][0])
         own.start()
         sends = []
         for k, device in enumerate(everyone):
             target = (me + k + 1) % (2 * RING)
-            sends.append(remote(normed_ref.at[:, columns(target)], normed_all.at[me], sems[k], device))
+            sends.append(remote(normed_ref.at[target], normed_all.at[me], sems[k], device))
 
         @pl.loop(0, 4)
         def _(group):
@@ -978,7 +980,6 @@
         name="begin",
     )
     tokens = tokens[:, : rows // lane].reshape(seq)
-    w_full = w_full.reshape(n * width, 3 * chans)
     emb = emb.reshape(vocab, width)
 
     def strip_of(a):
@@ -1033,33 +1034,30 @@
         out_part.reshape(n, rows, width), first,
         name="reduce",
     )
-    rows_all, arrived = call(
-        forth_kernel,
-        8,
-        [((n, rows, width), BF16), ((rows, width), BF16)],
-        [],
-        24,
-        second,
-        name="forth",
-    )
-
-    rows_all = jnp.transpose(rows_all, (1, 0, 2)).reshape(rows, n * width)
-    rows_float = rows_all.astype(F32)
-    inv_rms = lax.rsqrt(jnp.mean(rows_float * rows_float, axis=1, keepdims=True) + EPSILON)
-    normed = (rows_float * inv_rms).astype(BF16)
-    proj1 = dot(normed, w_full)
-    gp1, gated1, stat, sums1, gf1, prod1 = call(
-        middle_kernel,
-        7,
+    rows_all, e0, gp1, gated1, sums1, gf1, prod1 = call(
+        block1_kernel,
+        4,
         [
+            ((n, rows, width), BF16),
+            ((n, rows, width), BF16),
             ((rows, 3 * chans), BF16),
             ((rows, chans), BF16),
-            ((16, lane), F32),
             ((16, chans), F32),
             ((rows, chans), F32),
             ((rows + REACH, chans), F32),
         ],
         [
+            pltpu.VMEM((rows, width), BF16),
+            pltpu.VMEM((rows, width), BF16),
+            pltpu.VMEM((n, width, 3 * chans), BF16),
+            pltpu.VMEM((rows, 128), F32),
+            pltpu.VMEM((rows, 128), F32),
+            pltpu.VMEM((rows, 3 * chans), BF16),
+            pltpu.VMEM((n, rows, width), BF16),
+            pltpu.VMEM((n, 16, 128), F32),
+            pltpu.VMEM((16, 128), F32),
+            pltpu.VMEM((rows, width), F32),
+            pltpu.VMEM((rows, width), BF16),
             pltpu.VMEM((REACH, 128), F32),
             pltpu.VMEM((rows + 8, 3 * chans), F32),
             pltpu.VMEM((rows, chans), F32),
@@ -1076,28 +1074,15 @@
             pltpu.VMEM((rows, 128), F32),
             pltpu.VMEM((REACH, chans), BF16),
             pltpu.VMEM((8, 3 * chans), F32),
-        ],
-        4,
-        proj1, gg1, taps1, kernel_all,
-        name="middle",
-    )
-    back_part = dot(gp1, w_full, TRANS_B).astype(BF16)
-    back_part = jnp.transpose(back_part.reshape(rows, n, width), (1, 0, 2))
-    (e0,) = call(
-        back_kernel,
-        4,
-        [((n, rows, width), BF16)],
-        [
-            pltpu.VMEM((n, 16, lane), F32),
-            pltpu.VMEM((rows, width), BF16),
-            pltpu.VMEM((rows, width), F32),
-            pltpu.VMEM((rows, width), BF16),
         ]
         + RingThenPair.scratch(rows, width),
-        32,
-        back_part, stat, inv_rms, cotangent, arrived,
-        name="back",
+        48,
+        second, w_full, gg1, cotangent, taps1, kernel_all,
+        in_specs=[VMEM, ANY, VMEM, VMEM, VMEM, VMEM],
+        local=1,
+        name="block1",
     )
+
     e0_all = e0.reshape(seq, width)
 
     gg0, gp1_all, gated1_all, normed1, taps1_all = call(
@@ -1113,7 +1098,7 @@
         [pltpu.VMEM((8, rows + REACH, 128), F32), pltpu.VMEM((144, chans), F32), pltpu.VMEM((n, AHEAD, lane), BF16)]
         + PairThenRing.scratch(AHEAD, lane),
         40,
-        e0, w_out, gp1, gated1, normed, gf1, prod1, sums1,
+        e0, w_out, gp1, gated1, rows_all, gf1, prod1, sums1,
         in_specs=[VMEM, VMEM, ANY, ANY, ANY, VMEM, VMEM, VMEM],
         out_specs=[VMEM, ANY, ANY, ANY, VMEM],
         name="late",

time: 387 us -> 334 us (0.86)
  matrix products: 34.4 us -> 15 us
  Pallas kernels: 310 us -> 293 us
  local copies, waits for them, and re-layouts: 27.4 us -> 18 us
  other arithmetic: 12.5 us -> 6.44 us
    dot_general x7 -> x5, matrix products: 34.4 us -> 15 us  [dot(): return lax.dot_general(a, b, dims, preferred_element_type=F32)]
    pallas_call x8 -> x6, Pallas kernels: 310 us -> 293 us  [call(): pl.pallas_call(body, out_shape=[jax.ShapeDtypeStruct(shape, dtype) for sh...]
    convert_element_type x2 -> x0, local copies, waits for them, and re-layouts: 4.7 us -> none  [the longest x1 4.06 us: local(): back_part = dot(gp1, w_full, TRANS_B).astype(BF16)]
    reshape x1 -> x0, local copies, waits for them, and re-layouts: 3.92 us -> none  [local(): back_part = jnp.transpose(back_part.reshape(rows, n, width), (1, 0, 2))]
where the time goes in v3:
time: 334 us; the launch traced here: 333 us
  Pallas kernels  293 us (88%)
  local copies, waits for them, and re-layouts  18 us (5%)
  matrix products  15 us (4%)
  other arithmetic  6.44 us (2%)
    pallas_call x6, Pallas kernels, call(): pl.pallas_call(body, out_shape=[jax.ShapeDtypeStruct(shape, dtype) for sh...  293 us
    dot_general x5, matrix products, dot(): return lax.dot_general(a, b, dims, preferred_element_type=F32)  15 us

profile of v3, /device:TPU:1, one launch (start us, length us, event | category | flops | bytes accessed | tf_op | source)
XLA Modules:
  0.0 333.3 jit_solution(5547687239608980604)
XLA Ops:
  0.7 0.7 neg.14
  1.4 0.7 dynamic-slice_reduce_fusion
  2.1 0.6 reshape.93.taps
  2.7 1.3 tile.11
  3.9 0.8 reduce.2
  4.7 0.6 reshape_squeeze.7.taps
  5.3 1.1 bitcast_multiply_fusion.kern
  6.4 0.0 copy-start.1
  6.4 0.7 constant_dynamic-slice_fusion.kern
  7.1 1.7 copy.84
  8.9 1.6 copy.85.w_ref.w_far
  10.4 0.0 copy-done.1
  10.4 45.1 %begin.1 = (bf16[8,64,512]{2,1,0:T(8,128)(2,1)}, bf16[512,384]{1,0:T(8,128)(2,1)}, f32[512,128]{1,0:T(8,128)}, s32[8,16,128]{2,1,0:T(8,128)S(1)}, bf16[8,512,153...) custom-call(bf16[512,512]{1,0:T(8,128)(2,1)} %emb_ref.1, bf16[512,1536]{1,0:T(8,128)(2,1)} %copy.85.w_ref.w_far, ...), custom_call_target="tpu_custom_call" | custom-call | tf_op jit(solution)/shard_map/begin/pallas_call | solution.py:304
  55.6 6.9 %conditional.2 = (f32[1320,384]{1,0:T(8,128)S(1)}, bf16[256,512]{1,0:T(8,128)(2,1)S(1)}, bf16[512,1024]{1,0:T(8,128)(2,1)S(1)}, bf16[8,256,512]{2,1,0:T(8,128)(2,1)}) conditional(s32[]{:T(128)} %convert_element_type.39, (bf16[8,256,512]{2,1,0:T(8,128)(2,1)}, bf16[512,512]{1,0:T(8,128)(2,1)S(1)}) %tuple.82, (s32[8,16,128]{2,1,0:T(8,128)S(1)}, ...), branch_computations={%region_0.1_spmd, %region_1.2_spmd} | conditional | flops 1074790400 | bytes 8519863 | solution.py:1012
  55.6 0.1 dynamic_slice.17
  55.7 1.4 convolution_convert_fusion.1
  57.1 0.1 concatenate.4
  57.2 0.1 dynamic_slice.16
  57.3 0.2 compare_convert_fusion
  57.5 1.9 fusion
  59.5 3.0 copy.112
  62.5 25.6 %second.1 = (bf16[2048,512]{1,0:T(8,128)(2,1)}, f32[256,512]{1,0:T(8,128)}, f32[1040,128]{1,0:T(8,128)}) custom-call(f32[1320,384]{1,0:T(8,128)S(1)} %get-tuple-element.179.proj, f32[9,128]{1,0:T(8,128)} %reshape.93.taps, f32[128,128]{1,0:T(8,128)} %constant_dynamic-slice_fusion.kern, bf16[8,256,512]{2,1,0:T(8,128)(2,1)} %get-tuple-element.180.part_ref), custom_call_target="tpu_custom_call" | custom-call | tf_op jit(solution)/shard_map/second/pallas_call | solution.py:304
  88.1 0.0 copy-done.4
  88.1 4.2 %convolution_convert_fusion.2 = bf16[2048,512]{1,0:T(8,128)(2,1)} fusion(bf16[2048,512]{1,0:T(8,128)(2,1)} %get-tuple-element.181, bf16[1,512,512]{2,1,0:T(8,128)(2,1)S(1)} %copy-done.4), kind=kOutput, calls=%fused_computation.15 | convolution fusion | flops 1074790400 | bytes 4718592 | tf_op jit(solution)/shard_map/dot_general | solution.py:921
  92.3 27.2 %reduce.4.x_ref = bf16[256,512]{1,0:T(8,128)(2,1)} custom-call(bf16[8,256,512]{2,1,0:T(8,128)(2,1)} %bitcast.62, bf16[256,512]{1,0:T(8,128)(2,1)S(1)} %get-tuple-element.182.first_ref), custom_call_target="tpu_custom_call" | custom-call | tf_op jit(solution)/shard_map/reduce/pallas_call | solution.py:304
  119.5 134.1 %block1.1 = (bf16[8,256,512]{2,1,0:T(8,128)(2,1)}, bf16[8,256,512]{2,1,0:T(8,128)(2,1)}, bf16[256,1536]{1,0:T(8,128)(2,1)}, bf16[256,512]{1,0:T(8,128)(2,1)}, f3...) custom-call(bf16[256,512]{1,0:T(8,128)(2,1)} %reduce.4.x_ref, ...), custom_call_target="tpu_custom_call" | custom-call | tf_op jit(solution)/shard_map/block1/pallas_call | solution.py:304
  253.6 26.8 %late.1 = (f32[1184,128]{1,0:T(8,128)}, bf16[8,256,1536]{2,1,0:T(8,128)(2,1)}, bf16[8,256,512]{2,1,0:T(8,128)(2,1)}, bf16[8,256,512]{2,1,0:T(8,128)(2,1)}, f32[8,144,512]{2,1,0:T(8,128)}) custom-call(bf16[8,256,512]{2,1,0:T(8,128)(2,1)} %get-tuple-element.185.e0_ref, bf16[512,512]{1,0:T(8,128)(2,1)S(1)} %bitcast.67, ...), custom_call_target="tpu_custom_call" | custom-call | tf_op jit(solution)/shard_map/late/pallas_call | solution.py:304
  280.4 33.8 %last.1 = (bf16[8,256,384]{2,1,0:T(8,128)(2,1)}, f32[8,144,128]{2,1,0:T(8,128)}) custom-call(f32[1184,128]{1,0:T(8,128)} %get-tuple-element.197.gg, f32[1320,384]{1,0:T(8,128)S(1)} %get-tuple-element.179.proj, f32[9,128]{1,0:T(8,128)} %reshape.93.taps, f32[128,128]{1,0:T(8,128)} %constant_dynamic-slice_fusion.kern, f32[1040,128]{1,0:T(8,128)} %get-tuple-element.198.filtered, ...), custom_call_target="tpu_custom_call" | custom-call | tf_op jit(solution)/shard_map/last/pallas_call | solution.py:304
  314.2 0.0 copy-start.2
  314.2 16.7 %conditional.3 = (f32[1,512,3,512]{3,1,2,0:T(8,128)}, f32[1,512,512]{2,1,0:T(8,128)}, f32[128,512]{1,0:T(8,128)}, f32[1,3,3,512]{3,0,2,1:T(1,128)S(1)}) conditional(s32[]{:T(128)} %convert_element_type.39, (bf16[8,256,512]{2,1,0:T(8,128)(2,1)}, bf16[8,256,1536]{2,1,0:T(8,128)(2,1)}, bf16[8,256,512]{2,1,0:T(8,128)(2,1)}, ...), branch_computations={%region_2.4_spmd, %region_4.6_spmd} | conditional | flops 4295483392 | bytes 59875420 | solution.py:1144
  314.5 1.3 bitcast_reduce_fusion
  315.9 0.1 copy.82
  316.0 0.8 copy.100
  316.8 1.1 copy.90
  317.9 0.0 copy-start.6
  317.9 1.0 copy.89
  319.0 0.0 copy-done
  319.0 3.8 %convolution_bitcast_fusion.2 = f32[1,512,512]{2,1,0:T(8,128)} fusion(bf16[2048,512]{1,0:T(8,128)(2,1)} %get-tuple-element.136, bf16[2048,512]{1,0:T(8,128)(2,1)S(1)} %bitcast.61), kind=kOutput, calls=%fused_computation.10 | convolution fusion | flops 1073741824 | bytes 5242880 | tf_op jit(solution)/shard_map/cond/branch_1_fun/dot_general | solution.py:921
  322.8 1.7 copy.91
  324.5 1.3 copy.80
  325.8 0.6 reshape.86
  326.5 0.0 slice-start
  326.5 0.7 copy.81
  327.2 0.0 slice-done
  327.2 3.7 %convolution_bitcast_fusion.1 = f32[1,512,3,512]{3,1,2,0:T(8,128)} fusion(bf16[3,512,512]{2,1,0:T(8,128)(2,1)S(1)} %bitcast.59, bf16[512,512]{0,1:T(8,128)(2,1)} %copy.89, f32[512]{0:T(512)S(1)} %bitcast.70), kind=kOutput, calls=%fused_computation.9 | convolution fusion | flops 806092800 | bytes 5244928 | tf_op jit(solution)/shard_map/cond/branch_1_fun/dot_general | solution.py:921
  330.9 1.8 multiply_reduce_fusion
  332.7 0.6 negate_multiply_fusion
  333.3 0.0 copy-done.7
  (18 shorter events, 0.1 us)
Async XLA Ops:
  6.4 4.0 %copy-start.1 = (f32[128,512]{1,0:T(8,128)}, f32[128,512]{1,0:T(8,128)S(1)}, u32[]{:S(2)}) copy-start(f32[128,512]{1,0:T(8,128)S(1)} %bitcast_multiply_fusion.kern) | copy-start | bytes 786436
  10.4 45.1 %copy-start.3 = (bf16[1,512,512]{2,1,0:T(8,128)(2,1)S(1)}, bf16[1,512,512]{2,1,0:T(8,128)(2,1)}, u32[]{:S(2)}) copy-start(bf16[1,512,512]{2,1,0:T(8,128)(2,1)} %param.18) | copy-start | bytes 1572868
  62.5 25.6 %copy-start.4 = (bf16[1,512,512]{2,1,0:T(8,128)(2,1)S(1)}, bf16[1,512,512]{2,1,0:T(8,128)(2,1)}, u32[]{:S(2)}) copy-start(bf16[1,512,512]{2,1,0:T(8,128)(2,1)} %param.18) | copy-start | bytes 1572868
  314.2 16.7 %copy-start.2 = (f32[1,128,512]{2,1,0:T(8,128)S(1)}, f32[1,128,512]{2,1,0:T(8,128)}, u32[]{:S(2)}) copy-start(f32[1,128,512]{2,1,0:T(8,128)} %param.16) | copy-start | bytes 786436
  314.5 3.4 %copy-start.5 = (bf16[512,512]{1,0:T(8,128)(2,1)S(1)}, bf16[512,512]{1,0:T(8,128)(2,1)}, u32[]{:S(2)}) copy-start(bf16[512,512]{1,0:T(8,128)(2,1)} %get-tuple-element.315) | copy-start | bytes 1572868 | tf_op jit(solution)/shard_map/cond
  314.5 4.5 %copy-start = (bf16[8,256,512]{2,1,0:T(8,128)(2,1)S(1)}, bf16[8,256,512]{2,1,0:T(8,128)(2,1)}, u32[]{:S(2)}) copy-start(bf16[8,256,512]{2,1,0:T(8,128)(2,1)} %get-tuple-element.137) | copy-start | bytes 6291460 | tf_op jit(solution)/shard_map/cond
  317.9 4.9 %copy-start.6 = (f32[512,128]{0,1:T(8,128)}, f32[512,128]{0,1:T(8,128)S(1)}, u32[]{:S(2)}) copy-start(f32[512,128]{0,1:T(8,128)S(1)} %copy.90) | copy-start | bytes 786436 | tf_op jit(solution)/shard_map/cond
  326.5 0.7 slice-start
  330.9 2.4 copy-start.7

commit v4 on v3

v4 whole, which is shorter than its diff:
```python
import functools

import jax
import jax.numpy as jnp
from jax import lax
from jax.experimental import pallas as pl
from jax.experimental.pallas import tpu as pltpu
from jax.sharding import PartitionSpec as P

EPSILON = 1e-06
F32 = jnp.float32
BF16 = jnp.bfloat16
MESH = pl.DeviceIdType.MESH
BACK = 256
AHEAD = 1184
KEPT = 1040
RING = 4
REACH = 128


class Group:
    def __init__(self, axis):
        self.axis = axis
        me = lax.axis_index(axis)
        if axis == "ctx":
            self.ring, self.pair = me // 2, me % 2
        else:
            self.ring, self.pair = me % RING, me // RING
        self.right = (self.ring + 1) % RING
        self.left = (self.ring + RING - 1) % RING
        self.across = (self.ring + 2) % RING
        self.mate = 1 - self.pair

    def slot(self, ring, pair):
        return ring * 2 + pair if self.axis == "ctx" else pair * RING + ring

    def at(self, ring, pair):
        return {self.axis: self.slot(ring, pair)}

    def neighbours(self):
        return [
            self.at(self.right, self.pair),
            self.at(self.left, self.pair),
            self.at(self.ring, self.mate),
        ]


class Pool:
    def __init__(self, send, recv):
        self.send, self.recv, self.count = send, recv, 0

    def take(self, k):
        first = self.count
        self.count += k
        return [(self.send.at[first + i], self.recv.at[first + i]) for i in range(k)]


def remote(src, dst, sems, device):
    copy = pltpu.make_async_remote_copy(
        src_ref=src,
        dst_ref=dst,
        send_sem=sems[0],
        recv_sem=sems[1],
        device_id=device,
        device_id_type=MESH,
    )
    copy.start()
    return copy


def greet(devices, barrier):
    for device in devices:
        pl.semaphore_signal(barrier, inc=1, device_id=device, device_id_type=MESH)


class Gather:
    def __init__(self, group, src, out, pool, pair_first, place=None):
        self.g, self.src, self.out, self.pair_first = group, src, out, pair_first
        self.sems = pool.take(9)
        self.own = pool.take(1)[0]
        self.rows = src.shape[0]
        self.half = self.rows // 2
        self.place = place or (lambda ring, pair, first, rows: out.at[group.slot(ring, pair), pl.ds(first, rows)])

    def block(self, ring, pair):
        return self.place(ring, pair, 0, self.rows)

    def part(self, ring, pair, second):
        return self.place(ring, pair, self.half * second, self.half)

    def start(self):
        g, s = self.g, self.sems
        mine = self.block(g.ring, g.pair)
        right, left, mate = g.neighbours()
        self.local = pltpu.make_async_copy(self.src, mine, self.own[0])
        self.local.start()
        first = remote(self.src, mine, s[0], mate)
        self.copies = [first, remote(self.src, mine, s[1], right), remote(self.src, mine, s[2], left)]

    def turn(self, pair, a, b, c, d):
        g, s = self.g, self.sems
        right, left, mate = g.neighbours()
        more = []
        a.wait_recv()
        part = self.part(g.left, pair, 0)
        more.append(remote(part, part, s[c], right))
        if not self.pair_first:
            block = self.block(g.left, pair)
            more.append(remote(block, block, s[5], mate))
        b.wait_recv()
        part = self.part(g.right, pair, 1)
        more.append(remote(part, part, s[d], left))
        if not self.pair_first:
            block = self.block(g.right, pair)
            more.append(remote(block, block, s[6], mate))
        return more

    def middle(self):
        g, s = self.g, self.sems
        right, left, mate = g.neighbours()
        mate_copy, to_right, to_left = self.copies
        rest = self.turn(g.pair, to_right, to_left, 3, 4)
        self.sent = list(self.copies) + rest
        if self.pair_first:
            self.late = list(rest)
            mate_copy.wait_recv()
            block = self.block(g.ring, g.mate)
            a = remote(block, block, s[5], right)
            b = remote(block, block, s[6], left)
            more = self.turn(g.mate, a, b, 7, 8)
            self.sent += [a, b] + more
            self.late += more
        else:
            rest[0].wait_recv()
            rest[2].wait_recv()
            block = self.block(g.across, g.pair)
            last = remote(block, block, s[7], mate)
            self.sent.append(last)
            self.late = [mate_copy, rest[1], rest[3], last]

    def finish(self):
        for copy in self.late:
            copy.wait_recv()
        for copy in self.sent:
            copy.wait_send()
        self.local.wait()


def add_into(out, terms, rows=64):
    @pl.loop(0, out.shape[0] // rows)
    def _(step):
        here = pl.ds(pl.multiple_of(step * rows, rows), rows)
        total = terms[0][here].astype(F32)
        for term in terms[1:]:
            total = total + term[here].astype(F32)
        out[here] = total.astype(out.dtype)


def rows_step(count):
    for rows in (64, 48, 37 * 16, 32, 16):
        if count % rows == 0:
            return rows if rows != 37 * 16 else 16
    return 16


class Around:
    def __init__(self, group, pool, bufs):
        self.g = group
        self.s = pool.take(6)
        self.rel, self.merged, self.came = bufs
        self.half = self.rel.shape[1]

    @staticmethod
    def scratch(rows, lanes):
        half = rows // 2
        return [
            pltpu.VMEM((2, half, lanes), BF16),
            pltpu.VMEM((2, half, lanes), BF16),
            pltpu.VMEM((2, 2, half, lanes), BF16),
        ]

    def halves(self, ref):
        return ref.at[pl.ds(0, self.half)], ref.at[pl.ds(self.half, self.half)]

    def send_across(self, block):
        right, left, _ = self.g.neighbours()
        a, b = self.halves(block)
        self.copies = [remote(a, self.rel.at[0], self.s[0], right), remote(b, self.rel.at[1], self.s[1], left)]

    def send_near(self, to_right, to_left):
        right, left, _ = self.g.neighbours()
        self.to_right, self.to_left = to_right, to_left
        b = self.halves(to_right)[1]
        a = self.halves(to_left)[0]
        self.copies += [
            remote(b, self.came.at[0, 1], self.s[2], right),
            remote(a, self.came.at[1, 0], self.s[3], left),
        ]

    def merge(self):
        right, left, _ = self.g.neighbours()
        step = rows_step(self.half)
        self.copies[0].wait_recv()
        add_into(self.merged.at[0], [self.halves(self.to_right)[0], self.rel.at[0]], step)
        self.copies.append(remote(self.merged.at[0], self.came.at[0, 0], self.s[4], right))
        self.copies[1].wait_recv()
        add_into(self.merged.at[1], [self.halves(self.to_left)[1], self.rel.at[1]], step)
        self.copies.append(remote(self.merged.at[1], self.came.at[1, 1], self.s[5], left))

    def collect(self, out, own):
        step = rows_step(self.half)
        for copy in self.copies[2:]:
            copy.wait_recv()
        for h in range(2):
            piece = pl.ds(h * self.half, self.half)
            add_into(
                out.at[piece],
                [ref.at[piece] for ref in own] + [self.came.at[0, h], self.came.at[1, h]],
                step,
            )

    def finish(self):
        for copy in self.copies:
            copy.wait_send()


class PairThenRing:
    def __init__(self, group, inp, pool, bufs):
        self.g, self.inp = group, inp
        self.got, self.sums = bufs[:2]
        self.ring = Around(group, pool, bufs[2:])
        self.s = pool.take(4)

    @staticmethod
    def scratch(rows, lanes):
        return [pltpu.VMEM((4, rows, lanes), BF16), pltpu.VMEM((4, rows, lanes), BF16)] + Around.scratch(rows, lanes)

    def run(self, out):
        g = self.g
        mate = g.at(g.ring, g.mate)
        order = [g.across, g.right, g.left, g.ring]
        copies = [
            remote(self.inp.at[g.slot(r, g.mate)], self.got.at[k], self.s[k], mate) for k, r in enumerate(order)
        ]
        step = rows_step(self.inp.shape[1])

        def pair_sum(k):
            copies[k].wait_recv()
            add_into(self.sums.at[k], [self.inp.at[g.slot(order[k], g.pair)], self.got.at[k]], step)

        pair_sum(0)
        self.ring.send_across(self.sums.at[0])
        pair_sum(1)
        pair_sum(2)
        self.ring.send_near(self.sums.at[1], self.sums.at[2])
        copies[3].wait_recv()
        self.ring.merge()
        self.ring.collect(out, [self.inp.at[g.slot(g.ring, g.pair)], self.got.at[3]])
        self.ring.finish()
        for copy in copies:
            copy.wait_send()


class RingThenPair:
    def __init__(self, group, inp, pool, bufs):
        self.g, self.inp = group, inp
        self.far, self.got = bufs[:2]
        self.rings = [Around(group, pool, bufs[2:5]), Around(group, pool, bufs[5:8])]
        self.s = pool.take(1)[0]

    @staticmethod
    def scratch(rows, lanes):
        return (
            [pltpu.VMEM((rows, lanes), BF16), pltpu.VMEM((rows, lanes), BF16)]
            + Around.scratch(rows, lanes)
            + Around.scratch(rows, lanes)
        )

    def run(self, out, extra=(), produce=lambda slot: None):
        g = self.g
        pairs = [g.mate, g.pair]
        blocks = lambda ring, pair: self.inp.at[g.slot(ring, pair)]
        for ring, pair in zip(self.rings, pairs):
            produce(g.slot(g.across, pair))
            ring.send_across(blocks(g.across, pair))
            produce(g.slot(g.right, pair))
            produce(g.slot(g.left, pair))
            ring.send_near(blocks(g.right, pair), blocks(g.left, pair))
            produce(g.slot(g.ring, pair))
        self.rings[0].merge()
        self.rings[1].merge()
        self.rings[0].collect(self.far, [blocks(g.ring, g.mate)])
        copy = remote(self.far, self.got, self.s, g.at(g.ring, g.mate))
        self.rings[1].collect(out, [blocks(g.ring, g.pair)])
        copy.wait_recv()
        add_into(out, [out, self.got] + list(extra), rows_step(out.shape[0]))
        copy.wait_send()
        for ring in self.rings:
            ring.finish()


ANY = pl.BlockSpec(memory_space=pl.ANY)
VMEM = pl.BlockSpec(memory_space=pltpu.VMEM)


def call(body, ident, outs, scratch, sems, *args, in_specs=None, out_specs=None, name=None, local=0):
    return pl.pallas_call(
        body,
        out_shape=[jax.ShapeDtypeStruct(shape, dtype) for shape, dtype in outs],
        in_specs=in_specs or [VMEM] * len(args),
        out_specs=out_specs or [VMEM] * len(outs),
        scratch_shapes=list(scratch)
        + [pltpu.SemaphoreType.DMA((sems,)), pltpu.SemaphoreType.DMA((sems,))]
        + ([pltpu.SemaphoreType.DMA((local,))] if local else []),
        compiler_params=pltpu.CompilerParams(
            collective_id=ident, has_side_effects=True, vmem_limit_bytes=60 * 1024 * 1024
        ),
        name=name,
    )(*args)


def section_is(k):
    return lax.axis_index("section") == k


def crossing():
    i, j = lax.axis_index("dp"), lax.axis_index("ctx")
    return {"dp": j, "ctx": i}, i != j


def other_section():
    i, j = lax.axis_index("dp"), lax.axis_index("ctx")
    return {"section": 1 - lax.axis_index("section"), "dp": j, "ctx": i}


def lanes_at(first):
    return pl.ds(pl.multiple_of(first, 128), 128)


def shifted(shifts, ref, start, rows, lanes):
    for r in range(8):
        for a in range(0, rows, 64):
            count = min(64, rows - a)
            shifts[r, a : a + count] = ref[start + r + a : start + r + a + count, lanes]


def fir(shifts, kern, lanes, out, out_lanes, tiles, block, backwards):
    @pl.loop(0, tiles // block)
    def _(b):
        first = pl.multiple_of(b * block * 8, 8)

        def step(r, totals):
            totals = list(totals)
            taps = []
            for q in range(REACH // 8):
                u = 8 * q + r
                taps.append(kern[pl.ds(REACH - 1 - u if backwards else u, 8, stride=0), lanes])
            for i in range(block + REACH // 8 - 1):
                x = shifts[r, pl.ds(first + 8 * i, 8)]
                for o in range(block):
                    if 0 <= i - o < REACH // 8:
                        totals[o] = totals[o] + taps[i - o] * x
            return tuple(totals)

        totals = lax.fori_loop(0, 8, step, tuple(jnp.zeros((8, 128), F32) for _ in range(block)))
        for o in range(block):
            out[pl.ds(first + 8 * o, 8), out_lanes] = totals[o]


def lags(shifts, ref, lanes, out, out_lanes, tiles):
    for r in range(8):

        def step(b, totals):
            totals = list(totals)
            first = pl.multiple_of(b * 32, 8)
            own = [ref[pl.ds(first + 8 * o, 8), lanes] for o in range(4)]
            for i in range(4 + REACH // 8 - 1):
                x = shifts[r, pl.ds(first + 8 * i, 8)]
                for o in range(4):
                    if 0 <= i - o < REACH // 8:
                        totals[i - o] = totals[i - o] + own[o] * x
            return tuple(totals)

        totals = lax.fori_loop(0, tiles // 4, step, tuple(jnp.zeros((8, 128), F32) for _ in range(REACH // 8)))
        for q in range(REACH // 8):
            row = REACH - 1 - (8 * q + r)
            out[row : row + 1, out_lanes] = jnp.sum(totals[q], axis=0, keepdims=True)


def chunks(first, last, size):
    for a in range(first, last, size):
        yield a, min(size, last - a)


def short_rows(ref, taps, m, a, count, lanes, tap_lanes):
    total = taps[m : m + 1, tap_lanes] * ref[a : a + count, lanes]
    for j in (1, 2):
        total = total + taps[3 * j + m : 3 * j + m + 1, tap_lanes] * ref[a - j : a - j + count, lanes]
    return total


ALL = slice(0, 128)


def stream(m):
    return slice(m * 128, (m + 1) * 128)


def mix_first(proj, taps, kern, filtered, prod, shifts, gated, part):
    for a, count in chunks(BACK - REACH, BACK + part, 64):
        prod[a : a + count] = short_rows(proj, taps, 1, a, count, stream(1), ALL) * short_rows(
            proj, taps, 2, a, count, stream(2), ALL
        )
    for a, count in chunks(BACK + part, BACK + AHEAD, 64):
        prod[a : a + count] = short_rows(proj, taps, 1, a, count, stream(1), ALL) * short_rows(
            proj, taps, 2, a, count, stream(2), ALL
        )
    shifted(shifts, prod, BACK - REACH + 1, KEPT + REACH, ALL)
    fir(shifts, kern, ALL, filtered, ALL, KEPT // 8, 10, True)
    for a, count in chunks(0, part, 64):
        query = short_rows(proj, taps, 0, BACK + a, count, stream(0), ALL)
        gated[a : a + count] = (query * filtered[a : a + count]).astype(BF16)


def mix_back(gg, proj, taps, kern, filtered, gf, gprod, gs, shifts, gp, part):
    for a, count in chunks(0, AHEAD, 64):
        gf[a : a + count] = gg[a : a + count] * short_rows(proj, taps, 0, BACK + a, count, stream(0), ALL)
    shifted(shifts, gf, 0, KEPT + REACH, ALL)
    fir(shifts, kern, ALL, gprod, ALL, KEPT // 8, 10, False)
    for a, count in chunks(0, KEPT, 64):
        here = slice(a, a + count)
        gs[0, here] = gg[here] * filtered[here]
        gs[1, here] = gprod[here] * short_rows(proj, taps, 2, BACK + a, count, stream(2), ALL)
        gs[2, here] = gprod[here] * short_rows(proj, taps, 1, BACK + a, count, stream(1), ALL)
    for m in range(3):
        for a, count in chunks(0, part, 64):
            total = taps[m : m + 1] * gs[m, a : a + count]
            for j in (1, 2):
                total = total + taps[3 * j + m : 3 * j + m + 1] * gs[m, a + j : a + j + count]
            gp[a : a + count, stream(m)] = total.astype(BF16)


def mix_sums(gf, proj, taps, gs, prod, shifts, out, part):
    for a, count in chunks(BACK - REACH, BACK + part + 8, 64):
        prod[a : a + count] = short_rows(proj, taps, 1, a, count, stream(1), ALL) * short_rows(
            proj, taps, 2, a, count, stream(2), ALL
        )
    shifted(shifts, prod, BACK - REACH + 1, part + REACH, ALL)
    lags(shifts, gf, ALL, out, ALL, part // 8)
    out[REACH:] = jnp.zeros((16, 128), F32)
    for m in range(3):
        for j in range(3):
            total = jnp.zeros((8, 128), F32)
            for a, count in chunks(0, part, 64):
                term = gs[m, a : a + count] * proj[BACK - j + a : BACK - j + a + count, stream(m)]
                total = total + jnp.sum(term.reshape(count // 8, 8, 128), axis=0)
            row = REACH + 3 * j + m
            out[row : row + 1] = jnp.sum(total, axis=0, keepdims=True)


def by_rows(group, out, rows):
    def place(ring, pair, first, count):
        start = group.slot(ring, pair) * rows + first
        return out.at[pl.ds(pl.multiple_of(start, count), count)]

    return place


def by_strip(out, part):
    def place(ring, pair, first, count):
        return out.at[pl.ds(pl.multiple_of(pair * part + first, count), count), lanes_at(ring * 128)]

    return place


def marks(tok, q, vocab):
    inside = jnp.clip(q, 0, 4 * RING - 1)
    ids = tok[inside // 2, pl.ds(inside % 2, 1)]
    ids = jnp.where(q == inside, ids, -1)
    return jnp.where(lax.broadcasted_iota(jnp.int32, (vocab, 128), 0) == ids, 1.0, 0.0).astype(BF16)


def main_kernel(
    emb_ref, w_ref, w_far, cot_ref, tok_ref, w_proj, taps0, kern0, taps1, kern1,
    emb_out, inv_out, tok_out, e_all, gated_all, proj0, filtered0, x_all, gp_all, sums_all,
    part, crossed, half_out, piece, table, prod0, shifts, gated0, first_rows, total, x_block,
    wv, gg, arrived, returned, all_ref, x_col, square, inv_rows, gp_out, gpb, gated_out, stats, stat_own, block, sums_own, gf, prod,
    kg, pp, query, filtered, gprod, gs, ptail, qtail, ghead, gfar, sfar, gfpad, row_sum, qsend, gsend, *rest,
):
    pair_bufs, ring_bufs = rest[: len(PAIR)], rest[len(PAIR) : -2]
    send, recv = rest[-2:]
    barrier = pltpu.get_barrier_semaphore()
    ctx, dp = Group("ctx"), Group("dp")
    partner, apart = crossing()
    n = 2 * RING
    me = lax.axis_index("dp")
    place = lax.axis_index("ctx")
    others = [{"dp": (me + k) % n} for k in range(1, n)]
    after, before = {"ctx": (place + 1) % n}, {"ctx": (place + n - 1) % n}
    beyond = {"ctx": (place + n - 1 + 2 * ctx.pair) % n}
    opposite = {"section": 1 - lax.axis_index("section")}
    greet(ctx.neighbours() + [beyond] + others + [other_section(), opposite], barrier)

    @pl.when(apart)
    def _():
        greet([partner], barrier)

    pl.semaphore_wait(barrier, n + 5 + jnp.where(apart, 1, 0))
    lane = 128
    strips = RING
    common = Pool(send, recv)
    cross_sem = common.take(1)[0]
    same_sem = common.take(1)[0]
    pair_sems = common.take(2)
    relay = common.take(3)
    forth = pltpu.make_async_remote_copy(
        src_ref=x_block, dst_ref=arrived, send_sem=relay[0][0], recv_sem=relay[0][1],
        device_id=other_section(), device_id_type=MESH,
    )
    back = pltpu.make_async_remote_copy(
        src_ref=block, dst_ref=returned, send_sem=relay[1][0], recv_sem=relay[1][1],
        device_id=other_section(), device_id_type=MESH,
    )
    straight = pltpu.make_async_remote_copy(
        src_ref=x_block, dst_ref=x_col, send_sem=relay[2][0], recv_sem=relay[2][1],
        device_id=opposite, device_id_type=MESH,
    )

    @pl.when(section_is(0))
    def _():
        pool = Pool(send, recv)
        pool.count = common.count
        tokens = Gather(ctx, tok_ref, tok_out, pool, False)
        tokens.start()
        spread = pool.take(n - 1)
        share = piece.shape[0]
        share_of = lambda k: emb_ref.at[pl.ds(pl.multiple_of(k * share, share), share)]
        keep = pltpu.make_async_copy(share_of(me), piece, same_sem[0])
        copies = [
            pltpu.make_async_remote_copy(
                src_ref=share_of((me + k + 1) % n), dst_ref=piece, send_sem=spread[k][0],
                recv_sem=cross_sem[1], device_id=device, device_id_type=MESH,
            )
            for k, device in enumerate(others)
        ]

        @pl.when(jnp.logical_not(apart))
        def _():
            for copy in copies:
                copy.start()
            keep.start()
            keep.wait()

        @pl.when(apart)
        def _():
            copies[0].wait_recv()

        table_rows = Gather(dp, piece, emb_out, pool, True)
        table_rows.start()
        tokens.middle()
        table_rows.middle()
        table_rows.finish()

        @pl.when(jnp.logical_not(apart))
        def _():
            for copy in copies:
                copy.wait_send()

        vocab, width = emb_ref.shape
        hold = vocab // 2
        for core in range(2):
            values = emb_out[core * RING : (core + 1) * RING].reshape(hold, width).astype(F32)
            square = jnp.broadcast_to(jnp.sum(values * values, axis=1, keepdims=True), (hold, lane)).astype(BF16)
            for strip in range(strips):
                part[strip * 2 + core, :, 3 * lane :] = square

        @pl.loop(0, 3 * strips)
        def _(k):
            strip, m = k // 3, k % 3
            columns = pl.ds(pl.multiple_of(m * strips * lane + strip * lane, lane), lane)
            product = jnp.dot(emb_out[...].reshape(vocab, width), w_ref[:, columns], preferred_element_type=F32).astype(BF16)
            to = pl.ds(pl.multiple_of(m * lane, lane), lane)
            part[strip * 2, :, to] = product[:hold]
            part[strip * 2 + 1, :, to] = product[hold:]

        PairThenRing(ctx, part, pool, pair_bufs).run(half_out)
        here = pl.ds(pl.multiple_of(ctx.pair * hold, hold), hold)
        whole = half_out[...]
        inv = lax.rsqrt(whole[:, 3 * lane :] / (width * 2 * RING) + EPSILON)
        inv_out[here] = inv
        for m in range(3):
            table[here, m * lane : (m + 1) * lane] = (whole[:, m * lane : (m + 1) * lane] * inv).astype(BF16)
        mate = ctx.at(ctx.ring, ctx.mate)
        a = remote(inv_out.at[here], inv_out.at[here], pair_sems[0], mate)
        b = remote(table.at[here], table.at[here], pair_sems[1], mate)
        tokens.finish()
        a.wait()
        b.wait()


        @pl.loop(0, (BACK + 1280) // 128)
        def _(c):
            hot = marks(tok_out, ctx.pair * (n * 128 // 128) - BACK // 128 + c, vocab)
            proj0[pl.ds(pl.multiple_of(c * 128, 128), 128)] = dot(hot, table[...], TRANS_A)

        for k in range(2):
            hot = marks(tok_out, 2 * me + k, vocab)
            first_rows[k * 128 : (k + 1) * 128] = dot(hot, emb_out[...].reshape(vocab, width), TRANS_A).astype(BF16)
        span = gated0.shape[0]
        mix_first(proj0, taps0, kern0, filtered0, prod0, shifts, gated0, span)
        job = Gather(ctx, gated0, gated_all, pool, False, by_strip(gated_all, span))
        job.start()
        job.middle()
        job.finish()
        rows = x_block.shape[0]

        def produce(slot):
            here = pl.ds(pl.multiple_of(slot * rows, rows), rows)
            part[slot] = dot(gated_all[here], w_proj[...]).astype(BF16)

        RingThenPair(dp, part, pool, ring_bufs).run(total, [first_rows], produce)
        x_block[...] = total[...].astype(BF16)
        forth.start()
        straight.start()
        back.wait_recv()
        gather = Gather(dp, returned, e_all, pool, True)
        gather.start()
        gather.middle()
        gather.finish()
        forth.wait_send()
        straight.wait_send()

    @pl.when(section_is(1))
    def _():
        pool = Pool(send, recv)
        pool.count = common.count
        rows, width = gg.shape
        me = lax.axis_index("ctx")
        cot = cot_ref
        weights = Gather(ctx, w_far, wv, pool, False)
        there = pltpu.make_async_remote_copy(
            src_ref=cot_ref, dst_ref=crossed, send_sem=cross_sem[0], recv_sem=cross_sem[1],
            device_id=partner, device_id_type=MESH,
        )
        here = pltpu.make_async_copy(cot_ref, crossed, same_sem[0])
        pl.when(apart)(there.start)
        pl.when(jnp.logical_not(apart))(here.start)
        pl.when(apart)(there.wait)
        pl.when(jnp.logical_not(apart))(here.wait)
        weights.start()
        cots = Gather(dp, crossed, e_all, pool, True)
        cots.start()
        cots.middle()
        cots.finish()
        weights.middle()
        weights.finish()

        for k in range(n):
            part[k] = dot(e_all[k], w_proj[...], TRANS_B).astype(BF16)
        PairThenRing(ctx, part, pool, pair_bufs).run(gg)
        sums_own[REACH:] = jnp.zeros((16, width), F32)
        forth.wait_recv()
        gather = Gather(dp, arrived, all_ref, pool, True)
        gather.start()

        def use(ref, slot, begin=False):
            values = ref[...]
            for m in range(3):
                ml = slice(m * width, (m + 1) * width)
                term = dot(values, wv[slot, :, ml])
                pp[8:, ml] = term if begin else pp[8:, ml] + term
            term = jnp.zeros((rows, 128), F32)
            for g in range(width // 128):
                v = values[:, g * 128 : (g + 1) * 128].astype(F32)
                term = term + v * v
            square[...] = term if begin else square[...] + term

        use(arrived, dp.slot(dp.ring, dp.pair), True)
        gather.middle()
        for ring, pair in ((dp.left, dp.pair), (dp.right, dp.pair), (dp.ring, dp.mate), (dp.left, dp.mate), (dp.right, dp.mate)):
            use(gather.block(ring, pair), dp.slot(ring, pair))
        gather.finish()
        for pair in (dp.pair, dp.mate):
            use(gather.block(dp.across, pair), dp.slot(dp.across, pair))
        inv = lax.rsqrt(jnp.sum(square[...], axis=1, keepdims=True) / (width * n) + EPSILON)
        inv_rows[...] = jnp.broadcast_to(inv, (rows, 128))
        for a, count in chunks(0, rows, 32):
            pp[8 + a : 8 + a + count] = pp[8 + a : 8 + a + count] * inv_rows[a : a + count, :1]

        sems = pool.take(4)
        a_copy = remote(pp.at[pl.ds(rows, 8)], ptail, sems[0], after)

        def products(a, count, group):
            tl = lanes_at(group * 128)
            k = short_rows(pp, taps1, 1, a, count, lanes_at(width + group * 128), tl)
            v = short_rows(pp, taps1, 2, a, count, lanes_at(2 * width + group * 128), tl)
            return k * v

        @pl.loop(0, 4)
        def _(group):
            tl = lanes_at(group * 128)
            for a, count in chunks(rows // 2, rows, 64):
                value = products(8 + a, count, group)
                prod[REACH + a : REACH + a + count, tl] = value
                qsend[a - rows // 2 : a - rows // 2 + count, tl] = value.astype(BF16)

        b_copy = remote(qsend, qtail, sems[1], after)
        a_copy.wait_recv()
        pp[0:8] = jnp.where(me > 0, ptail[...], 0.0)

        @pl.loop(0, 4)
        def _(group):
            tl = lanes_at(group * 128)
            for a, count in chunks(0, rows, 64):
                value = short_rows(pp, taps1, 0, 8 + a, count, tl, tl)
                query[a : a + count, tl] = value
                value = value * gg[a : a + count, tl]
                gf[a : a + count, tl] = value
                gfpad[a : a + count, tl] = value
                if a < REACH:
                    ghead[a : a + count, tl] = value.astype(BF16)
            for a, count in chunks(0, rows // 2, 64):
                prod[REACH + a : REACH + a + count, tl] = products(8 + a, count, group)

        c_copy = remote(ghead, gfar, sems[2], before)
        b_copy.wait_recv()
        for a, count in chunks(0, REACH, 32):
            prod[a : a + count] = jnp.where(me > 0, qtail[a : a + count].astype(F32), 0.0)

        @pl.loop(0, 4)
        def _(group):
            tl = lanes_at(group * 128)
            shifted(shifts, prod, 1, rows + REACH - 8, tl)
            kg[...] = kern1[:, tl]
            fir(shifts, kg, ALL, filtered, tl, rows // 8, 8, True)
            for a, count in chunks(0, rows, 64):
                gated_out[a : a + count, tl] = (query[a : a + count, tl] * filtered[a : a + count, tl]).astype(BF16)

        near = Gather(ctx, gated_out, gated_all, pool, False, by_rows(ctx, gated_all, rows))
        near.start()
        c_copy.wait_recv()
        for a, count in chunks(0, REACH, 32):
            gfpad[rows + a : rows + a + count] = jnp.where(me < n - 1, gfar[a : a + count].astype(F32), 0.0)

        @pl.loop(0, 4)
        def _(group):
            tl = lanes_at(group * 128)
            shifted(shifts, gfpad, 0, rows + REACH - 8, tl)
            kg[...] = kern1[:, tl]
            fir(shifts, kg, ALL, gprod, tl, rows // 8, 8, False)
            for a, count in chunks(0, rows, 64):
                here = slice(a, a + count)
                gs[here, tl] = gg[here, tl] * filtered[here, tl]
                k = short_rows(pp, taps1, 1, 8 + a, count, lanes_at(width + group * 128), tl)
                v = short_rows(pp, taps1, 2, 8 + a, count, lanes_at(2 * width + group * 128), tl)
                gs[here, lanes_at(width + group * 128)] = gprod[here, tl] * v
                gs[here, lanes_at(2 * width + group * 128)] = gprod[here, tl] * k

        for m in range(3):
            gsend[:, m * width : (m + 1) * width] = gs[0:8, m * width : (m + 1) * width]
        d_copy = remote(gsend, sfar, sems[3], before)
        d_copy.wait_recv()
        gs[rows : rows + 8] = jnp.where(me < n - 1, sfar[...], 0.0)
        row_sum[...] = jnp.zeros_like(row_sum)

        @pl.loop(0, 4)
        def _(group):
            tl = lanes_at(group * 128)
            for m in range(3):
                ml = lanes_at(m * width + group * 128)
                sums = [jnp.zeros((8, 128), F32) for _ in range(3)]
                for a, count in chunks(0, rows, 64):
                    grad = taps1[m : m + 1, tl] * gs[a : a + count, ml]
                    for j in (1, 2):
                        grad = grad + taps1[3 * j + m : 3 * j + m + 1, tl] * gs[a + j : a + j + count, ml]
                    gpb[a : a + count, ml] = grad.astype(BF16)
                    gp_out[a : a + count, ml] = (grad * inv_rows[a : a + count]).astype(BF16)
                    row_sum[a : a + count] += grad * pp[8 + a : 8 + a + count, ml]
                    for j in range(3):
                        term = gs[a : a + count, ml] * pp[8 - j + a : 8 - j + a + count, ml]
                        sums[j] = sums[j] + jnp.sum(term.reshape(count // 8, 8, 128), axis=0)
                for j in range(3):
                    sums_own[REACH + 3 * j + m : REACH + 3 * j + m + 1, tl] = jnp.sum(sums[j], axis=0, keepdims=True)

        eye = lax.broadcasted_iota(jnp.int32, (128, 128), 0) == lax.broadcasted_iota(jnp.int32, (128, 128), 1)
        stat_own[...] = jnp.zeros_like(stat_own)
        for k in range(rows // 128):
            column = jnp.sum(row_sum[k * 128 : (k + 1) * 128], axis=1, keepdims=True)
            line = jnp.sum(jnp.where(eye, jnp.broadcast_to(column, (128, 128)), 0.0), axis=0, keepdims=True)
            stat_own[k : k + 1] = line
        grads = Gather(ctx, gp_out, gp_all, pool, False)
        grads.start()
        stat = Gather(dp, stat_own, stats, pool, True)
        stat.start()

        def produce(slot):
            part[slot] = dot(gpb[...], wv[slot], TRANS_B).astype(BF16)

        RingThenPair(dp, part, pool, ring_bufs).run(total, produce=produce)
        stat.middle()
        stat.finish()
        summed = stats[0]
        for k in range(1, n):
            summed = summed + stats[k]
        for k in range(rows // 128):
            here = pl.ds(k * 128, 128)
            line = jnp.broadcast_to(summed[k : k + 1], (128, 128))
            scalar = jnp.sum(jnp.where(eye, line, 0.0), axis=1, keepdims=True)
            inv = inv_rows[here, :1]
            block[here] = (
                cot[here].astype(F32)
                + inv * total[here]
                - arrived[here].astype(F32) * (inv * inv * scalar / (width * n))
            ).astype(BF16)
        back.start()
        straight.wait_recv()
        columns = Gather(dp, x_col, x_all, pool, True)
        columns.start()
        near.middle()

        @pl.loop(0, 4)
        def _(group):
            tl = lanes_at(group * 128)
            shifted(shifts, prod, 1, rows + REACH - 8, tl)
            lags(shifts, gf, tl, sums_own, tl, rows // 8)

        taps_job = Gather(ctx, sums_own, sums_all, pool, False)
        taps_job.start()
        jobs = [columns, grads, taps_job]
        for job in jobs:
            job.middle()
        for job in [near] + jobs:
            job.finish()
        for copy in (a_copy, b_copy, c_copy, d_copy):
            copy.wait_send()
        back.wait_send()


PAIR = (None,) * 5


def end_kernel(
    e_all, w_proj, gated_all, proj, taps, kern, filtered, tok, gtab_all, taps_all, grad_out,
    part_ref, gg, gf, gprod, gs, prod, shifts, gp, sum_ref, gtab, sums, got, block, *rest,
):
    bufs, (send, recv) = rest[:-2], rest[-2:]
    barrier = pltpu.get_barrier_semaphore()
    ctx = Group("ctx")

    def outer():
        count, rows, _ = e_all.shape
        grad_out[...] = jnp.zeros_like(grad_out)

        @pl.loop(0, count)
        def _(k):
            here = pl.ds(pl.multiple_of(k * rows, rows), rows)
            grad_out[...] += dot(gated_all[here], e_all[k], TRANS_A)

    @pl.when(section_is(0))
    def _():
        greet(ctx.neighbours(), barrier)
        pl.semaphore_wait(barrier, 3)
        pool = Pool(send, recv)
        count, rows, _ = e_all.shape
        for k in range(count):
            product = dot(e_all[k], w_proj[...], TRANS_B).astype(BF16)
            core, first = divmod(k * rows, count // 2 * rows)
            for strip in range(RING):
                part = product[:, strip * 128 : (strip + 1) * 128]
                part_ref[strip * 2 + core, first : first + rows] = part
                if core == 1 and first == 0:
                    part_ref[strip * 2, count // 2 * rows : AHEAD] = part[: AHEAD - count // 2 * rows]
        over = AHEAD - count // 2 * rows
        for strip in range(RING):
            part_ref[strip * 2 + 1, count // 2 * rows : AHEAD] = jnp.zeros((over, 128), BF16)
        PairThenRing(ctx, part_ref, pool, bufs).run(gg)

        sem = pool.take(1)[0]
        hold = got.shape[0]
        part = gp.shape[0]
        mix_back(gg, proj, taps, kern, filtered, gf, gprod, gs, shifts, gp, part)

        sum_ref[...] = jnp.zeros_like(sum_ref)

        @pl.loop(0, part // 128)
        def _(c):
            hot = marks(tok, ctx.pair * (part // 128) + c, sum_ref.shape[0])
            sum_ref[...] += dot(hot, gp[pl.ds(pl.multiple_of(c * 128, 128), 128)])

        gtab[...] = sum_ref[...].astype(BF16)

        halves = lambda p: gtab.at[pl.ds(pl.multiple_of(p * hold, hold), hold)]
        copy = remote(halves(ctx.mate), got, sem, ctx.at(ctx.ring, ctx.mate))
        copy.wait()
        add_into(block, [halves(ctx.pair), got])
        table = Gather(ctx, block, gtab_all, pool, False)
        table.start()
        outer()
        mix_sums(gf, proj, taps, gs, prod, shifts, sums, part)
        job = Gather(ctx, sums, taps_all, pool, False)
        job.start()
        table.middle()
        job.middle()
        table.finish()
        job.finish()

    @pl.when(section_is(1))
    def _():
        outer()


def dot(a, b, dims=(((1,), (0,)), ((), ()))):
    return lax.dot_general(a, b, dims, preferred_element_type=F32)


TRANS_B = (((1,), (1,)), ((), ()))
TRANS_A = (((0,), (0,)), ((), ()))


def local(
    token_ids, embedding, project_in, short_taps, filter_taps, decay_rates, project_out, cotangent
):
    section_zero = lax.axis_index("section") == 0
    n = lax.axis_size("ctx")
    vocab = embedding.shape[0]
    rows = token_ids.shape[0]
    seq = rows * n
    part = seq // 2
    width = embedding.shape[1]
    chans = project_in.shape[3]
    lane = chans // RING
    taps_all = short_taps[0]
    filter_all = filter_taps[0]
    tap_count = filter_all.shape[0]
    strip = lax.axis_index("ctx") // 2

    w_flat = project_in[0].reshape(width, 3 * chans)
    w_out = project_out[0]
    positions = jnp.arange(tap_count).astype(F32)
    damping_all = jnp.exp(-decay_rates[0][None, :] * positions[:, None] / tap_count)
    kernel_all = filter_all * damping_all

    def strip_of(a):
        return lax.dynamic_slice_in_dim(a, strip * lane, lane, a.ndim - 1)

    taps0, kernel0 = strip_of(taps_all), strip_of(kernel_all)

    taps0 = taps0.reshape(9, lane)
    taps1 = taps_all.reshape(9, chans)
    own_tokens = jnp.tile(token_ids.reshape(rows // lane, lane), (16 * lane // rows, 1))
    emb, inv_table, tokens, e_all, gated_all, proj0, filtered0, x_all, gp_all, sums1 = call(
        main_kernel,
        1,
        [
            ((n, vocab // n, width), BF16),
            ((vocab, lane), F32),
            ((n, 16, lane), jnp.int32),
            ((n, rows, width), BF16),
            ((seq, chans), BF16),
            ((BACK + 1280, 3 * lane), F32),
            ((KEPT, lane), F32),
            ((n, rows, width), BF16),
            ((n, rows, 3 * chans), BF16),
            ((n, 144, chans), F32),
        ],
        [
            pltpu.VMEM(shape, dtype)
            for shape, dtype in (
                ((n, rows, width), BF16),
                ((rows, width), BF16),
                ((vocab // 2, 4 * lane), F32),
                ((vocab // n, width), BF16),
                ((vocab, 3 * lane), BF16),
                ((BACK + AHEAD, lane), F32),
                ((8, KEPT + REACH, lane), F32),
                ((part, lane), BF16),
                ((rows, width), BF16),
                ((rows, width), F32),
                ((rows, width), BF16),
                ((n, width, 3 * chans), BF16),
                ((rows, chans), F32),
                ((rows, width), BF16),
                ((rows, width), BF16),
                ((n, rows, width), BF16),
                ((rows, width), BF16),
                ((rows, 128), F32),
                ((rows, 128), F32),
                ((rows, 3 * chans), BF16),
                ((rows, 3 * chans), BF16),
                ((rows, chans), BF16),
                ((n, 16, 128), F32),
                ((16, 128), F32),
                ((rows, width), BF16),
                ((144, chans), F32),
                ((rows, chans), F32),
                ((rows + REACH, chans), F32),
                ((REACH, 128), F32),
                ((rows + 8, 3 * chans), F32),
                ((rows, chans), F32),
                ((rows, chans), F32),
                ((rows, chans), F32),
                ((rows + 8, 3 * chans), F32),
                ((8, 3 * chans), F32),
                ((REACH, chans), BF16),
                ((REACH, chans), BF16),
                ((REACH, chans), BF16),
                ((8, 3 * chans), F32),
                ((rows + REACH, chans), F32),
                ((rows, 128), F32),
                ((REACH, chans), BF16),
                ((8, 3 * chans), F32),
            )
        ]
        + PairThenRing.scratch(rows, width)
        + RingThenPair.scratch(rows, width),
        128,
        embedding, w_flat, w_flat, cotangent, own_tokens, w_out, taps0, kernel0, taps1, kernel_all,
        in_specs=[VMEM, VMEM, ANY] + [VMEM] * 7,
        out_specs=[VMEM] * 8 + [ANY] * 2,
        name="main",
    )
    emb = emb.reshape(vocab, width)
    gtab, sums0, grad_out = call(
        end_kernel,
        2,
        [((n, vocab // 2, 3 * lane), BF16), ((n, 144, lane), F32), ((chans, width), F32)],
        [
            pltpu.VMEM((n, AHEAD, lane), BF16),
            pltpu.VMEM((AHEAD, lane), F32),
            pltpu.VMEM((AHEAD, lane), F32),
            pltpu.VMEM((KEPT, lane), F32),
            pltpu.VMEM((3, KEPT, lane), F32),
            pltpu.VMEM((BACK + AHEAD, lane), F32),
            pltpu.VMEM((8, KEPT + REACH, lane), F32),
            pltpu.VMEM((part, 3 * lane), BF16),
            pltpu.VMEM((vocab, 3 * lane), F32),
            pltpu.VMEM((vocab, 3 * lane), BF16),
            pltpu.VMEM((144, lane), F32),
            pltpu.VMEM((vocab // 2, 3 * lane), BF16),
            pltpu.VMEM((vocab // 2, 3 * lane), BF16),
        ]
        + PairThenRing.scratch(AHEAD, lane),
        40,
        e_all, w_out, gated_all, proj0, taps0, kernel0, filtered0, tokens,
        name="end",
    )

    def end0():
        table_rows = jnp.transpose(gtab.reshape(RING, 2, vocab // 2, 3, lane), (1, 2, 3, 0, 4))
        normed_table = (emb.astype(F32) * inv_table[:, :1]).astype(BF16)
        sums = sums0.reshape(RING, 2, 144, lane).sum(axis=1)
        return (
            dot(normed_table, table_rows.reshape(vocab, 3 * chans), TRANS_A),
            jnp.transpose(sums, (1, 0, 2)).reshape(144, chans),
        )

    def end1():
        return (
            dot(x_all.reshape(seq, width), gp_all.reshape(seq, 3 * chans), TRANS_A),
            sums1.sum(axis=0),
        )

    grad_in, sums = lax.cond(section_zero, end0, end1)
    grad_in = grad_in.reshape(width, 3, chans)
    gk, gt = sums[:tap_count], sums[tap_count : tap_count + 9].reshape(3, 3, chans)
    grad_filter = gk * damping_all
    grad_decay = -jnp.sum(gk * kernel_all * positions[:, None], axis=0) / tap_count
    return (grad_in[None], grad_out[None], grad_filter[None], grad_decay[None], gt[None])


def solution(mesh):
    return jax.shard_map(
        local,
        mesh=mesh,
        in_specs=(
            P("ctx"),
            P(None, "dp"),
            P("section", "ctx", None, "dp"),
            P("section", None, None, "dp"),
            P("section", None, "dp"),
            P("section", "dp"),
            P("section", "dp", "ctx"),
            P("ctx", "dp"),
        ),
        out_specs=(
            P("section", "ctx", None, "dp"),
            P("section", "dp", "ctx"),
            P("section", None, "dp"),
            P("section", "dp"),
            P("section", None, None, "dp"),
        ),
        check_vma=False,
    )
```

time: 334 us -> 305 us (0.913)
  Pallas kernels: 293 us -> 278 us
  matrix products: 15 us -> 3.74 us
  local copies, waits for them, and re-layouts: 18 us -> 14.1 us
    pallas_call x6 -> x2, Pallas kernels: 293 us -> 278 us  [call(): pl.pallas_call(body, out_shape=[jax.ShapeDtypeStruct(shape, dtype) for sh...]
    dot_general x5 -> x1, matrix products: 15 us -> 3.74 us  [dot(): return lax.dot_general(a, b, dims, preferred_element_type=F32)]
where the time goes in v4:
time: 305 us; the launch traced here: 304 us
  Pallas kernels  278 us (91%)
  local copies, waits for them, and re-layouts  14.1 us (5%)
  other arithmetic  7.17 us (2%)
  matrix products  3.74 us (1%)
    pallas_call x2, Pallas kernels, call(): pl.pallas_call(body, out_shape=[jax.ShapeDtypeStruct(shape, dtype) for sh...  278 us

profile of v4, /device:TPU:1, one launch (start us, length us, event | category | flops | bytes accessed | tf_op | source)
XLA Modules:
  0.0 304.1 jit_solution(18056711833594245023)
XLA Ops:
  0.7 0.7 neg.14
  1.3 0.7 dynamic-slice_reduce_fusion
  2.1 0.6 reshape.72.taps0.taps
  2.7 1.3 tile.11
  3.9 0.8 reduce.2
  4.7 0.6 reshape_squeeze.7.taps1
  5.3 1.1 bitcast_multiply_fusion.kern1
  6.4 0.0 copy-start.1
  6.4 0.7 constant_dynamic-slice_fusion.kern0.kern
  7.1 1.7 copy.81
  8.9 1.6 copy.82.w_ref.w_far
  10.4 0.0 copy-done.1
  10.4 220.6 %main.1 = (bf16[8,64,512]{2,1,0:T(8,128)(2,1)}, f32[512,128]{1,0:T(8,128)}, s32[8,16,128]{2,1,0:T(8,128)}, bf16[8,256,512]{2,1,0:T(8,128)(2,1)}, bf16[2048,512]{...) custom-call(bf16[512,512]{1,0:T(8,128)(2,1)} %emb_ref.1, ...), custom_call_target="tpu_custom_call" | custom-call | tf_op jit(solution)/shard_map/main/pallas_call | solution.py:307
  231.0 57.7 %end.1 = (bf16[8,256,384]{2,1,0:T(8,128)(2,1)}, f32[8,144,128]{2,1,0:T(8,128)}, f32[512,512]{1,0:T(8,128)}) custom-call(bf16[8,256,512]{2,1,0:T(8,128)(2,1)} %get-tuple-element.64.e_all, bf16[512,512]{1,0:T(8,128)(2,1)} %bitcast.42, bf16[2048,512]{1,0:T(8,128)(2,1)} %get-tuple-element.65.gated_all, f32[1536,384]{1,0:T(8,128)} %get-tuple-element.66.proj, ...), custom_call_target="tpu_custom_call" | custom-call | tf_op jit(solution)/shard_map/end/pallas_call | solution.py:307
  288.7 0.0 copy-start.2
  288.8 10.7 %conditional.1 = (f32[1,512,3,512]{3,1,2,0:T(8,128)}, f32[128,512]{1,0:T(8,128)}, f32[1,3,3,512]{3,0,2,1:T(1,128)S(1)}) conditional(s32[]{:T(128)} %convert_element_type.24, (bf16[8,256,512]{2,1,0:T(8,128)(2,1)}, bf16[8,256,1536]{2,1,0:T(8,128)(2,1)}, f32[8,144,512]{2,1,0:T(8,128)S(1)}) %tuple.24, (bf16[8,64,512]{2,1,0:T(8,128)(2,1)}, ...), branch_computations={%region_0.2_spmd, %region_2.4_spmd} | conditional | flops 3221741568 | bytes 31377516 | solution.py:1063
  288.8 0.0 copy-start.4
  288.8 0.0 copy-start.3
  288.8 0.0 copy-start
  288.8 1.3 bitcast_reduce_fusion
  290.2 0.1 copy.79
  290.3 0.8 copy.96
  291.1 0.0 copy-done.4
  291.1 0.1 copy.85
  291.3 0.1 mul.8
  291.4 0.0 copy-done.3
  291.4 1.0 multiply_convert_fusion
  292.3 0.0 copy-done
  292.3 0.7 copy.86
  293.1 1.3 copy.76
  294.4 0.6 reshape.69
  295.0 0.7 copy.77
  295.7 3.7 %convolution_bitcast_fusion = f32[1,512,3,512]{3,1,2,0:T(8,128)} fusion(bf16[512,512,1]{1,0,2:T(8,128)(2,1)} %bitcast.40, bf16[3,512,512]{2,1,0:T(8,128)(2,1)S(1)} %bitcast.38), kind=kOutput, calls=%fused_computation | convolution fusion | flops 805306368 | bytes 5242880 | tf_op jit(solution)/shard_map/cond/branch_1_fun/dot_general | solution.py:913
  299.5 0.0 copy-start.5
  299.5 0.0 copy-done.2
  299.5 1.8 multiply_reduce_fusion
  301.3 0.6 negate_multiply_fusion
  301.9 2.3 copy.108
  304.1 0.0 copy-done.5
  (5 shorter events, 0.1 us)
Async XLA Ops:
  6.4 4.0 %copy-start.1 = (f32[128,512]{1,0:T(8,128)}, f32[128,512]{1,0:T(8,128)S(1)}, u32[]{:S(2)}) copy-start(f32[128,512]{1,0:T(8,128)S(1)} %bitcast_multiply_fusion.kern1) | copy-start | bytes 786436
  288.7 10.8 %copy-start.2 = (f32[1,128,512]{2,1,0:T(8,128)S(1)}, f32[1,128,512]{2,1,0:T(8,128)}, u32[]{:S(2)}) copy-start(f32[1,128,512]{2,1,0:T(8,128)} %param.14) | copy-start | bytes 786436
  288.8 2.4 copy-start.4
  288.8 2.6 copy-start.3
  288.8 3.5 %copy-start = (bf16[8,256,384]{2,1,0:T(8,128)(2,1)S(1)}, bf16[8,256,384]{2,1,0:T(8,128)(2,1)}, u32[]{:S(2)}) copy-start(bf16[8,256,384]{2,1,0:T(8,128)(2,1)} %get-tuple-element.158) | copy-start | bytes 4718596 | tf_op jit(solution)/shard_map/cond
  299.5 4.7 %copy-start.5 = (f32[1,3,3,512]{3,0,2,1:T(1,128)}, f32[1,3,3,512]{3,0,2,1:T(1,128)S(1)}, u32[]{:S(2)}) copy-start(f32[1,3,3,512]{3,0,2,1:T(1,128)S(1)} %get-tuple-element.184) | copy-start | bytes 55300

commit v5 on v4

--- a/solution.py
+++ b/solution.py
@@ -115,11 +115,18 @@
             more.append(remote(block, block, s[6], mate))
         return more
 
+    def pass_on(self):
+        self.passed = self.turn(self.g.pair, self.copies[1], self.copies[2], 3, 4)
+
+    passed = None
+
     def middle(self):
         g, s = self.g, self.sems
         right, left, mate = g.neighbours()
         mate_copy, to_right, to_left = self.copies
-        rest = self.turn(g.pair, to_right, to_left, 3, 4)
+        if self.passed is None:
+            self.pass_on()
+        rest = self.passed
         self.sent = list(self.copies) + rest
         if self.pair_first:
             self.late = list(rest)
@@ -480,11 +487,50 @@
     return jnp.where(lax.broadcasted_iota(jnp.int32, (vocab, 128), 0) == ids, 1.0, 0.0).astype(BF16)
 
 
+def sems_of(send, recv, k):
+    return recv.at[k]
+
+
+def use_rows(out, blocks, weights, gather, dp, own):
+    term = lambda ref, slot: dot(ref[...], weights[slot], TRANS_B)
+    slot = dp.slot(dp.ring, dp.pair)
+    out[...] = term(own, slot)
+    gather.middle()
+    near = ((dp.left, dp.pair), (dp.right, dp.pair), (dp.ring, dp.mate), (dp.left, dp.mate), (dp.right, dp.mate))
+    for ring, pair in near:
+        slot = dp.slot(ring, pair)
+        out[...] += term(blocks.at[slot], slot)
+    gather.finish()
+    for pair in (dp.pair, dp.mate):
+        slot = dp.slot(dp.across, pair)
+        out[...] += term(blocks.at[slot], slot)
+
+
+def swap(pieces, sems, me):
+    for k, (src, dst, to, sem, when) in enumerate(pieces):
+        far = jnp.logical_and(when, to != me)
+        near = jnp.logical_and(when, to == me)
+        away = pltpu.make_async_remote_copy(
+            src_ref=src, dst_ref=dst, send_sem=sems[k][0], recv_sem=sem, device_id={"ctx": to}, device_id_type=MESH
+        )
+        here = pltpu.make_async_copy(src, dst, sem)
+        pl.when(far)(away.start)
+        pl.when(near)(here.start)
+
+
+def swapped(pieces, sems, me):
+    for k, (src, dst, to, sem, when) in enumerate(pieces):
+        away = pltpu.make_async_remote_copy(
+            src_ref=src, dst_ref=dst, send_sem=sems[k][0], recv_sem=sem, device_id={"ctx": to}, device_id_type=MESH
+        )
+        pl.when(jnp.logical_and(when, to != me))(away.wait_send)
+
+
 def main_kernel(
-    emb_ref, w_ref, w_far, cot_ref, tok_ref, w_proj, taps0, kern0, taps1, kern1,
-    emb_out, inv_out, tok_out, e_all, gated_all, proj0, filtered0, x_all, gp_all, sums_all,
+    emb_ref, w_ref, w_far, cot_ref, tok_ref, w_proj, wo_far, taps0, kern0, taps1, kern1,
+    emb_out, inv_out, tok_out, e_all, gated_all, proj0, filtered0, x_all, gp_all, sums_all, gg_rows, e_col,
     part, crossed, half_out, piece, table, prod0, shifts, gated0, first_rows, total, x_block,
-    wv, gg, arrived, returned, all_ref, x_col, square, inv_rows, gp_out, gpb, gated_out, stats, stat_own, block, sums_own, gf, prod,
+    wv, wo, gated_own, gg, arrived, returned, all_ref, x_col, square, inv_rows, gp_out, gpb, gated_out, stats, stat_own, block, sums_own, gf, prod,
     kg, pp, query, filtered, gprod, gs, ptail, qtail, ghead, gfar, sfar, gfpad, row_sum, qsend, gsend, *rest,
 ):
     pair_bufs, ring_bufs = rest[: len(PAIR)], rest[len(PAIR) : -2]
@@ -497,34 +543,33 @@
     place = lax.axis_index("ctx")
     others = [{"dp": (me + k) % n} for k in range(1, n)]
     after, before = {"ctx": (place + 1) % n}, {"ctx": (place + n - 1) % n}
-    beyond = {"ctx": (place + n - 1 + 2 * ctx.pair) % n}
+    along = [{"ctx": (place + k) % n} for k in range(1, n)]
     opposite = {"section": 1 - lax.axis_index("section")}
-    greet(ctx.neighbours() + [beyond] + others + [other_section(), opposite], barrier)
+    greet(along + others + [other_section(), opposite], barrier)
 
     @pl.when(apart)
     def _():
         greet([partner], barrier)
 
-    pl.semaphore_wait(barrier, n + 5 + jnp.where(apart, 1, 0))
+    pl.semaphore_wait(barrier, 2 * n + jnp.where(apart, 1, 0))
     lane = 128
     strips = RING
     common = Pool(send, recv)
     cross_sem = common.take(1)[0]
     same_sem = common.take(1)[0]
     pair_sems = common.take(2)
-    relay = common.take(3)
-    forth = pltpu.make_async_remote_copy(
-        src_ref=x_block, dst_ref=arrived, send_sem=relay[0][0], recv_sem=relay[0][1],
-        device_id=other_section(), device_id_type=MESH,
-    )
-    back = pltpu.make_async_remote_copy(
-        src_ref=block, dst_ref=returned, send_sem=relay[1][0], recv_sem=relay[1][1],
-        device_id=other_section(), device_id_type=MESH,
-    )
-    straight = pltpu.make_async_remote_copy(
-        src_ref=x_block, dst_ref=x_col, send_sem=relay[2][0], recv_sem=relay[2][1],
-        device_id=opposite, device_id_type=MESH,
-    )
+    relay = common.take(4)
+
+    def handed(src, dst, k, device):
+        return pltpu.make_async_remote_copy(
+            src_ref=src, dst_ref=dst, send_sem=relay[k][0], recv_sem=relay[k][1],
+            device_id=device, device_id_type=MESH,
+        )
+
+    forth = handed(x_block, arrived, 0, opposite)
+    back = handed(block, returned, 1, opposite)
+    x_over = handed(x_block, x_col, 2, other_section())
+    e_over = handed(block, e_col, 3, other_section())
 
     @pl.when(section_is(0))
     def _():
@@ -532,6 +577,8 @@
         pool.count = common.count
         tokens = Gather(ctx, tok_ref, tok_out, pool, False)
         tokens.start()
+        outs = Gather(ctx, wo_far, wo, pool, False)
+        outs.start()
         spread = pool.take(n - 1)
         share = piece.shape[0]
         share_of = lambda k: emb_ref.at[pl.ds(pl.multiple_of(k * share, share), share)]
@@ -583,7 +630,9 @@
             part[strip * 2, :, to] = product[:hold]
             part[strip * 2 + 1, :, to] = product[hold:]
 
+        outs.pass_on()
         PairThenRing(ctx, part, pool, pair_bufs).run(half_out)
+        outs.middle()
         here = pl.ds(pl.multiple_of(ctx.pair * hold, hold), hold)
         whole = half_out[...]
         inv = lax.rsqrt(whole[:, 3 * lane :] / (width * 2 * RING) + EPSILON)
@@ -604,31 +653,51 @@
             proj0[pl.ds(pl.multiple_of(c * 128, 128), 128)] = dot(hot, table[...], TRANS_A)
 
         for k in range(2):
-            hot = marks(tok_out, 2 * me + k, vocab)
-            first_rows[k * 128 : (k + 1) * 128] = dot(hot, emb_out[...].reshape(vocab, width), TRANS_A).astype(BF16)
+            hot = marks(tok_out, 2 * place + k, vocab)
+            first_rows[k * 128 : (k + 1) * 128] = dot(hot, emb_ref[...], TRANS_A).astype(BF16)
         span = gated0.shape[0]
         mix_first(proj0, taps0, kern0, filtered0, prod0, shifts, gated0, span)
+        rows = x_block.shape[0]
+        sems = pool.take(RING)
+        yes = place >= 0
+        pieces = [
+            (
+                gated0.at[pl.ds(k * rows, rows)],
+                gated_own.at[:, lanes_at(ctx.ring * 128)],
+                ctx.pair * RING + k,
+                sems_of(send, recv, pool.count + ctx.ring),
+                yes,
+            )
+            for k in range(RING)
+        ]
+        pool.count += RING
+        swap(pieces, sems, place)
+        outs.finish()
+        for k in range(RING):
+            pltpu.make_async_copy(
+                gated0.at[pl.ds(0, rows)], gated_own.at[:, lanes_at(k * 128)], sems_of(send, recv, pool.count - RING + k)
+            ).wait()
+        swapped(pieces, sems, place)
+
+        def produce(slot):
+            part[slot] = dot(gated_own[...], wo[slot]).astype(BF16)
+
+        RingThenPair(dp, part, pool, ring_bufs).run(total, [first_rows], produce)
+        x_block[...] = total[...].astype(BF16)
+        forth.start()
+        forth.wait_send()
+        x_over.start()
         job = Gather(ctx, gated0, gated_all, pool, False, by_strip(gated_all, span))
         job.start()
         job.middle()
         job.finish()
-        rows = x_block.shape[0]
-
-        def produce(slot):
-            here = pl.ds(pl.multiple_of(slot * rows, rows), rows)
-            part[slot] = dot(gated_all[here], w_proj[...]).astype(BF16)
-
-        RingThenPair(dp, part, pool, ring_bufs).run(total, [first_rows], produce)
-        x_block[...] = total[...].astype(BF16)
-        forth.start()
-        straight.start()
+        x_over.wait_send()
         back.wait_recv()
-        gather = Gather(dp, returned, e_all, pool, True)
+        gather = Gather(dp, returned, all_ref, pool, True)
         gather.start()
-        gather.middle()
-        gather.finish()
-        forth.wait_send()
-        straight.wait_send()
+        use_rows(gg, all_ref, wo, gather, dp, returned)
+        gg_rows[...] = gg[...].astype(BF16)
+        e_over.wait_recv()
 
     @pl.when(section_is(1))
     def _():
@@ -637,7 +706,10 @@
         rows, width = gg.shape
         me = lax.axis_index("ctx")
         cot = cot_ref
+        outs = Gather(ctx, wo_far, wo, pool, False)
         weights = Gather(ctx, w_far, wv, pool, False)
+        outs.start()
+        weights.start()
         there = pltpu.make_async_remote_copy(
             src_ref=cot_ref, dst_ref=crossed, send_sem=cross_sem[0], recv_sem=cross_sem[1],
             device_id=partner, device_id_type=MESH,
@@ -645,19 +717,25 @@
         here = pltpu.make_async_copy(cot_ref, crossed, same_sem[0])
         pl.when(apart)(there.start)
         pl.when(jnp.logical_not(apart))(here.start)
+        turned = Gather(dp, cot_ref, part, pool, True)
+        turned.start()
+        turned.middle()
+        turned.finish()
+        outs.pass_on()
         pl.when(apart)(there.wait)
         pl.when(jnp.logical_not(apart))(here.wait)
-        weights.start()
         cots = Gather(dp, crossed, e_all, pool, True)
         cots.start()
+        weights.pass_on()
+        outs.middle()
         cots.middle()
+        outs.finish()
+        gg[...] = jnp.zeros_like(gg)
+        for k in range(n):
+            gg[...] += dot(part[k], wo[k], TRANS_B)
         cots.finish()
         weights.middle()
         weights.finish()
-
-        for k in range(n):
-            part[k] = dot(e_all[k], w_proj[...], TRANS_B).astype(BF16)
-        PairThenRing(ctx, part, pool, pair_bufs).run(gg)
         sums_own[REACH:] = jnp.zeros((16, width), F32)
         forth.wait_recv()
         gather = Gather(dp, arrived, all_ref, pool, True)
@@ -813,7 +891,8 @@
                 - arrived[here].astype(F32) * (inv * inv * scalar / (width * n))
             ).astype(BF16)
         back.start()
-        straight.wait_recv()
+        e_over.start()
+        x_over.wait_recv()
         columns = Gather(dp, x_col, x_all, pool, True)
         columns.start()
         near.middle()
@@ -834,20 +913,23 @@
         for copy in (a_copy, b_copy, c_copy, d_copy):
             copy.wait_send()
         back.wait_send()
+        e_over.wait_send()
 
 
 PAIR = (None,) * 5
 
 
 def end_kernel(
-    e_all, w_proj, gated_all, proj, taps, kern, filtered, tok, gtab_all, taps_all, grad_out,
-    part_ref, gg, gf, gprod, gs, prod, shifts, gp, sum_ref, gtab, sums, got, block, *rest,
+    gg_rows, e_col, e_all, gated_all, proj, taps, kern, filtered, tok, gtab_all, taps_all, grad_out,
+    e_got, gg, gf, gprod, gs, prod, shifts, gp, sum_ref, gtab, sums, got, block, *rest,
 ):
-    bufs, (send, recv) = rest[:-2], rest[-2:]
+    send, recv = rest
     barrier = pltpu.get_barrier_semaphore()
-    ctx = Group("ctx")
-
-    def outer():
+    ctx, dp = Group("ctx"), Group("dp")
+    n = 2 * RING
+    place = lax.axis_index("ctx")
+
+    def outer(e_all):
         count, rows, _ = e_all.shape
         grad_out[...] = jnp.zeros_like(grad_out)
 
@@ -858,27 +940,62 @@
 
     @pl.when(section_is(0))
     def _():
-        greet(ctx.neighbours(), barrier)
-        pl.semaphore_wait(barrier, 3)
+        greet([{"ctx": (place + k) % n} for k in range(1, n)] + dp.neighbours(), barrier)
+        pl.semaphore_wait(barrier, n + 2)
         pool = Pool(send, recv)
-        count, rows, _ = e_all.shape
-        for k in range(count):
-            product = dot(e_all[k], w_proj[...], TRANS_B).astype(BF16)
-            core, first = divmod(k * rows, count // 2 * rows)
-            for strip in range(RING):
-                part = product[:, strip * 128 : (strip + 1) * 128]
-                part_ref[strip * 2 + core, first : first + rows] = part
-                if core == 1 and first == 0:
-                    part_ref[strip * 2, count // 2 * rows : AHEAD] = part[: AHEAD - count // 2 * rows]
-        over = AHEAD - count // 2 * rows
-        for strip in range(RING):
-            part_ref[strip * 2 + 1, count // 2 * rows : AHEAD] = jnp.zeros((over, 128), BF16)
-        PairThenRing(ctx, part_ref, pool, bufs).run(gg)
-
+        rows = gg_rows.shape[0]
+        over = AHEAD - RING * rows
+        sems = pool.take(2 * RING)
+        start = pool.count
+        pool.count += RING + 1
+        spot = place % RING
+        yes = place >= 0
+        strip_at = lambda x: slice(x * 128, (x + 1) * 128)
+        pieces = [
+            (
+                gg_rows.at[:, strip_at(x)],
+                gg.at[pl.ds(pl.multiple_of(spot * rows, rows), rows)],
+                2 * x + place // RING,
+                sems_of(send, recv, start + spot),
+                yes,
+            )
+            for x in range(RING)
+        ] + [
+            (
+                gg_rows.at[pl.ds(0, over), strip_at(x)],
+                gg.at[pl.ds(RING * rows, over)],
+                2 * x,
+                sems_of(send, recv, start + RING),
+                place == RING,
+            )
+            for x in range(RING)
+        ]
+
+        @pl.when(ctx.pair == 1)
+        def _():
+            gg[pl.ds(RING * rows, over)] = jnp.zeros((over, 128), BF16)
+
+        swap(pieces, sems, place)
+        for k in range(RING):
+            pltpu.make_async_copy(
+                gg_rows.at[:, strip_at(0)], gg.at[pl.ds(k * rows, rows)], sems_of(send, recv, start + k)
+            ).wait()
+
+        @pl.when(ctx.pair == 0)
+        def _():
+            pltpu.make_async_copy(
+                gg_rows.at[pl.ds(0, over), strip_at(0)],
+                gg.at[pl.ds(RING * rows, over)],
+                sems_of(send, recv, start + RING),
+            ).wait()
+
+        columns = Gather(dp, e_col, e_got, pool, True)
+        columns.start()
         sem = pool.take(1)[0]
         hold = got.shape[0]
         part = gp.shape[0]
         mix_back(gg, proj, taps, kern, filtered, gf, gprod, gs, shifts, gp, part)
+        columns.middle()
 
         sum_ref[...] = jnp.zeros_like(sum_ref)
 
@@ -895,7 +1012,8 @@
         add_into(block, [halves(ctx.pair), got])
         table = Gather(ctx, block, gtab_all, pool, False)
         table.start()
-        outer()
+        columns.finish()
+        outer(e_got)
         mix_sums(gf, proj, taps, gs, prod, shifts, sums, part)
         job = Gather(ctx, sums, taps_all, pool, False)
         job.start()
@@ -903,10 +1021,11 @@
         job.middle()
         table.finish()
         job.finish()
+        swapped(pieces, sems, place)
 
     @pl.when(section_is(1))
     def _():
-        outer()
+        outer(e_all)
 
 
 def dot(a, b, dims=(((1,), (0,)), ((), ()))):
@@ -948,7 +1067,7 @@
     taps0 = taps0.reshape(9, lane)
     taps1 = taps_all.reshape(9, chans)
     own_tokens = jnp.tile(token_ids.reshape(rows // lane, lane), (16 * lane // rows, 1))
-    emb, inv_table, tokens, e_all, gated_all, proj0, filtered0, x_all, gp_all, sums1 = call(
+    emb, inv_table, tokens, e_all, gated_all, proj0, filtered0, x_all, gp_all, sums1, gg_rows, e_col = call(
         main_kernel,
         1,
         [
@@ -962,6 +1081,8 @@
             ((n, rows, width), BF16),
             ((n, rows, 3 * chans), BF16),
             ((n, 144, chans), F32),
+            ((rows, chans), BF16),
+            ((rows, width), BF16),
         ],
         [
             pltpu.VMEM(shape, dtype)
@@ -978,6 +1099,8 @@
                 ((rows, width), F32),
                 ((rows, width), BF16),
                 ((n, width, 3 * chans), BF16),
+                ((n, chans, width), BF16),
+                ((rows, chans), BF16),
                 ((rows, chans), F32),
                 ((rows, width), BF16),
                 ((rows, width), BF16),
@@ -1014,9 +1137,9 @@
         + PairThenRing.scratch(rows, width)
         + RingThenPair.scratch(rows, width),
         128,
-        embedding, w_flat, w_flat, cotangent, own_tokens, w_out, taps0, kernel0, taps1, kernel_all,
-        in_specs=[VMEM, VMEM, ANY] + [VMEM] * 7,
-        out_specs=[VMEM] * 8 + [ANY] * 2,
+        embedding, w_flat, w_flat, cotangent, own_tokens, w_out, w_out, taps0, kernel0, taps1, kernel_all,
+        in_specs=[VMEM, VMEM, ANY] + [VMEM] * 3 + [ANY] + [VMEM] * 4,
+        out_specs=[VMEM] * 8 + [ANY] * 2 + [VMEM] * 2,
         name="main",
     )
     emb = emb.reshape(vocab, width)
@@ -1025,8 +1148,8 @@
         2,
         [((n, vocab // 2, 3 * lane), BF16), ((n, 144, lane), F32), ((chans, width), F32)],
         [
-            pltpu.VMEM((n, AHEAD, lane), BF16),
-            pltpu.VMEM((AHEAD, lane), F32),
+            pltpu.VMEM((n, rows, width), BF16),
+            pltpu.VMEM((AHEAD, lane), BF16),
             pltpu.VMEM((AHEAD, lane), F32),
             pltpu.VMEM((KEPT, lane), F32),
             pltpu.VMEM((3, KEPT, lane), F32),
@@ -1038,10 +1161,9 @@
             pltpu.VMEM((144, lane), F32),
             pltpu.VMEM((vocab // 2, 3 * lane), BF16),
             pltpu.VMEM((vocab // 2, 3 * lane), BF16),
-        ]
-        + PairThenRing.scratch(AHEAD, lane),
-        40,
-        e_all, w_out, gated_all, proj0, taps0, kernel0, filtered0, tokens,
+        ],
+        56,
+        gg_rows, e_col, e_all, gated_all, proj0, taps0, kernel0, filtered0, tokens,
         name="end",
     )
 

time: 305 us -> 297 us (0.974)
  Pallas kernels: 278 us -> 271 us
    pallas_call x2, Pallas kernels: 278 us -> 271 us  [call(): pl.pallas_call(body, out_shape=[jax.ShapeDtypeStruct(shape, dtype) for sh...]
where the time goes in v5:
time: 297 us
  Pallas kernels  271 us (91%)
  local copies, waits for them, and re-layouts  14.1 us (5%)
  other arithmetic  7.17 us (2%)
  matrix products  3.74 us (1%)
    pallas_call x2, Pallas kernels, call(): pl.pallas_call(body, out_shape=[jax.ShapeDtypeStruct(shape, dtype) for sh...  271 us

profile of v5, /device:TPU:1, one launch (start us, length us, event | category | flops | bytes accessed | tf_op | source)
XLA Modules:
  0.0 296.8 jit_solution(7975739292188367063)
XLA Ops:
  0.7 0.7 neg.14
  1.3 0.7 dynamic-slice_reduce_fusion
  2.1 0.6 reshape.72.taps0.taps
  2.7 1.3 tile.11
  3.9 0.8 reduce.2
  4.7 0.6 reshape_squeeze.7.taps1
  5.3 1.1 bitcast_multiply_fusion.kern1
  6.4 0.0 copy-start.1
  6.4 0.7 constant_dynamic-slice_fusion.kern0.kern
  7.1 1.7 copy.81
  8.9 1.6 copy.82.w_ref.w_far
  10.4 0.0 copy-done.1
  10.4 207.8 %main.1 = (bf16[8,64,512]{2,1,0:T(8,128)(2,1)}, f32[512,128]{1,0:T(8,128)}, s32[8,16,128]{2,1,0:T(8,128)}, bf16[8,256,512]{2,1,0:T(8,128)(2,1)}, bf16[2048,512]{...) custom-call(bf16[512,512]{1,0:T(8,128)(2,1)} %emb_ref.1, ...), custom_call_target="tpu_custom_call" | custom-call | tf_op jit(solution)/shard_map/main/pallas_call | solution.py:314
  218.2 63.2 %end.1 = (bf16[8,256,384]{2,1,0:T(8,128)(2,1)}, f32[8,144,128]{2,1,0:T(8,128)}, f32[512,512]{1,0:T(8,128)}) custom-call(bf16[256,512]{1,0:T(8,128)(2,1)} %get-tuple-element.66.gg_rows, bf16[256,512]{1,0:T(8,128)(2,1)} %get-tuple-element.67.e_col, bf16[8,256,512]{2,1,0:T(8,128)(2,1)} %get-tuple-element.68.e_all, ...), custom_call_target="tpu_custom_call" | custom-call | tf_op jit(solution)/shard_map/end/pallas_call | solution.py:314
  281.4 0.0 copy-start.2
  281.4 10.7 %conditional.1 = (f32[1,512,3,512]{3,1,2,0:T(8,128)}, f32[128,512]{1,0:T(8,128)}, f32[1,3,3,512]{3,0,2,1:T(1,128)S(1)}) conditional(s32[]{:T(128)} %convert_element_type.24, (bf16[8,256,512]{2,1,0:T(8,128)(2,1)}, bf16[8,256,1536]{2,1,0:T(8,128)(2,1)}, f32[8,144,512]{2,1,0:T(8,128)S(1)}) %tuple.24, (bf16[8,64,512]{2,1,0:T(8,128)(2,1)}, ...), branch_computations={%region_0.2_spmd, %region_2.4_spmd} | conditional | flops 3221741568 | bytes 31377516 | solution.py:1185
  281.4 0.0 copy-start.4
  281.5 0.0 copy-start.3
  281.5 0.0 copy-start
  281.5 1.3 bitcast_reduce_fusion
  282.8 0.1 copy.79
  283.0 0.8 copy.96
  283.8 0.0 copy-done.4
  283.8 0.1 copy.85
  284.0 0.1 mul.8
  284.0 0.0 copy-done.3
  284.0 1.0 multiply_convert_fusion
  285.0 0.0 copy-done
  285.0 0.7 copy.86
  285.8 1.3 copy.76
  287.1 0.6 reshape.69
  287.7 0.7 copy.77
  288.4 3.7 %convolution_bitcast_fusion = f32[1,512,3,512]{3,1,2,0:T(8,128)} fusion(bf16[512,512,1]{1,0,2:T(8,128)(2,1)} %bitcast.40, bf16[3,512,512]{2,1,0:T(8,128)(2,1)S(1)} %bitcast.38), kind=kOutput, calls=%fused_computation | convolution fusion | flops 805306368 | bytes 5242880 | tf_op jit(solution)/shard_map/cond/branch_1_fun/dot_general | solution.py:1032
  292.2 0.0 copy-start.5
  292.2 0.0 copy-done.2
  292.2 1.8 multiply_reduce_fusion
  294.0 0.6 negate_multiply_fusion
  294.6 2.3 copy.108
  296.8 0.0 copy-done.5
  (5 shorter events, 0.1 us)
Async XLA Ops:
  6.4 4.0 %copy-start.1 = (f32[128,512]{1,0:T(8,128)}, f32[128,512]{1,0:T(8,128)S(1)}, u32[]{:S(2)}) copy-start(f32[128,512]{1,0:T(8,128)S(1)} %bitcast_multiply_fusion.kern1) | copy-start | bytes 786436
  281.4 10.7 %copy-start.2 = (f32[1,128,512]{2,1,0:T(8,128)S(1)}, f32[1,128,512]{2,1,0:T(8,128)}, u32[]{:S(2)}) copy-start(f32[1,128,512]{2,1,0:T(8,128)} %param.14) | copy-start | bytes 786436
  281.4 2.4 copy-start.4
  281.5 2.6 copy-start.3
  281.5 3.5 %copy-start = (bf16[8,256,384]{2,1,0:T(8,128)(2,1)S(1)}, bf16[8,256,384]{2,1,0:T(8,128)(2,1)}, u32[]{:S(2)}) copy-start(bf16[8,256,384]{2,1,0:T(8,128)(2,1)} %get-tuple-element.162) | copy-start | bytes 4718596 | tf_op jit(solution)/shard_map/cond
  292.2 4.7 %copy-start.5 = (f32[1,3,3,512]{3,0,2,1:T(1,128)}, f32[1,3,3,512]{3,0,2,1:T(1,128)S(1)}, u32[]{:S(2)}) copy-start(f32[1,3,3,512]{3,0,2,1:T(1,128)S(1)} %get-tuple-element.188) | copy-start | bytes 55300

commit v6 on v5

--- a/solution.py
+++ b/solution.py
@@ -118,7 +118,14 @@
     def pass_on(self):
         self.passed = self.turn(self.g.pair, self.copies[1], self.copies[2], 3, 4)
 
-    passed = None
+    def cross_on(self):
+        g, s = self.g, self.sems
+        right, left, mate = g.neighbours()
+        self.copies[0].wait_recv()
+        block = self.block(g.ring, g.mate)
+        self.crossed = (remote(block, block, s[5], right), remote(block, block, s[6], left))
+
+    passed = crossed = None
 
     def middle(self):
         g, s = self.g, self.sems
@@ -130,10 +137,9 @@
         self.sent = list(self.copies) + rest
         if self.pair_first:
             self.late = list(rest)
-            mate_copy.wait_recv()
-            block = self.block(g.ring, g.mate)
-            a = remote(block, block, s[5], right)
-            b = remote(block, block, s[6], left)
+            if self.crossed is None:
+                self.cross_on()
+            a, b = self.crossed
             more = self.turn(g.mate, a, b, 7, 8)
             self.sent += [a, b] + more
             self.late += more
@@ -546,12 +552,9 @@
     along = [{"ctx": (place + k) % n} for k in range(1, n)]
     opposite = {"section": 1 - lax.axis_index("section")}
     greet(along + others + [other_section(), opposite], barrier)
-
-    @pl.when(apart)
-    def _():
-        greet([partner], barrier)
-
-    pl.semaphore_wait(barrier, 2 * n + jnp.where(apart, 1, 0))
+    for k in range(n):
+        pl.when(jnp.logical_or(apart, place != k))(functools.partial(greet, [{"dp": place, "ctx": k}], barrier))
+    pl.semaphore_wait(barrier, 3 * n - 1 + jnp.where(apart, 1, 0))
     lane = 128
     strips = RING
     common = Pool(send, recv)
@@ -578,40 +581,28 @@
         tokens = Gather(ctx, tok_ref, tok_out, pool, False)
         tokens.start()
         outs = Gather(ctx, wo_far, wo, pool, False)
+        share = emb_out.shape[1]
+        spread = pool.count
+        pool.count += n
+        source = emb_ref.at[pl.ds(pl.multiple_of(place * share, share), share)]
+        away = [
+            pltpu.make_async_remote_copy(
+                src_ref=source, dst_ref=emb_out.at[place], send_sem=send.at[spread + k],
+                recv_sem=recv.at[spread + place], device_id={"dp": k, "ctx": me}, device_id_type=MESH,
+            )
+            for k in range(n)
+        ]
+        keep = pltpu.make_async_copy(source, emb_out.at[place], recv.at[spread + place])
+        for k in range(n):
+            pl.when(jnp.logical_or(apart, me != k))(away[k].start)
+        pl.when(jnp.logical_not(apart))(keep.start)
         outs.start()
-        spread = pool.take(n - 1)
-        share = piece.shape[0]
-        share_of = lambda k: emb_ref.at[pl.ds(pl.multiple_of(k * share, share), share)]
-        keep = pltpu.make_async_copy(share_of(me), piece, same_sem[0])
-        copies = [
-            pltpu.make_async_remote_copy(
-                src_ref=share_of((me + k + 1) % n), dst_ref=piece, send_sem=spread[k][0],
-                recv_sem=cross_sem[1], device_id=device, device_id_type=MESH,
-            )
-            for k, device in enumerate(others)
-        ]
-
-        @pl.when(jnp.logical_not(apart))
-        def _():
-            for copy in copies:
-                copy.start()
-            keep.start()
-            keep.wait()
-
-        @pl.when(apart)
-        def _():
-            copies[0].wait_recv()
-
-        table_rows = Gather(dp, piece, emb_out, pool, True)
-        table_rows.start()
+        tokens.pass_on()
+        for k in range(n):
+            pltpu.make_async_copy(source, emb_out.at[k], recv.at[spread + k]).wait()
+        for k in range(n):
+            pl.when(jnp.logical_or(apart, me != k))(away[k].wait_send)
         tokens.middle()
-        table_rows.middle()
-        table_rows.finish()
-
-        @pl.when(jnp.logical_not(apart))
-        def _():
-            for copy in copies:
-                copy.wait_send()
 
         vocab, width = emb_ref.shape
         hold = vocab // 2
@@ -630,9 +621,8 @@
             part[strip * 2, :, to] = product[:hold]
             part[strip * 2 + 1, :, to] = product[hold:]
 
+        PairThenRing(ctx, part, pool, pair_bufs).run(half_out)
         outs.pass_on()
-        PairThenRing(ctx, part, pool, pair_bufs).run(half_out)
-        outs.middle()
         here = pl.ds(pl.multiple_of(ctx.pair * hold, hold), hold)
         whole = half_out[...]
         inv = lax.rsqrt(whole[:, 3 * lane :] / (width * 2 * RING) + EPSILON)
@@ -655,6 +645,7 @@
         for k in range(2):
             hot = marks(tok_out, 2 * place + k, vocab)
             first_rows[k * 128 : (k + 1) * 128] = dot(hot, emb_ref[...], TRANS_A).astype(BF16)
+        outs.middle()
         span = gated0.shape[0]
         mix_first(proj0, taps0, kern0, filtered0, prod0, shifts, gated0, span)
         rows = x_block.shape[0]
@@ -722,20 +713,21 @@
         turned.middle()
         turned.finish()
         outs.pass_on()
+        weights.pass_on()
+        outs.middle()
+        outs.finish()
+        gg[...] = jnp.zeros_like(gg)
+        for k in range(n):
+            gg[...] += dot(part[k], wo[k], TRANS_B)
         pl.when(apart)(there.wait)
         pl.when(jnp.logical_not(apart))(here.wait)
         cots = Gather(dp, crossed, e_all, pool, True)
         cots.start()
-        weights.pass_on()
-        outs.middle()
+        weights.middle()
+        cots.pass_on()
+        cots.cross_on()
+        weights.finish()
         cots.middle()
-        outs.finish()
-        gg[...] = jnp.zeros_like(gg)
-        for k in range(n):
-            gg[...] += dot(part[k], wo[k], TRANS_B)
-        cots.finish()
-        weights.middle()
-        weights.finish()
         sums_own[REACH:] = jnp.zeros((16, width), F32)
         forth.wait_recv()
         gather = Gather(dp, arrived, all_ref, pool, True)
@@ -908,7 +900,7 @@
         jobs = [columns, grads, taps_job]
         for job in jobs:
             job.middle()
-        for job in [near] + jobs:
+        for job in [near, cots] + jobs:
             job.finish()
         for copy in (a_copy, b_copy, c_copy, d_copy):
             copy.wait_send()
@@ -995,7 +987,8 @@
         hold = got.shape[0]
         part = gp.shape[0]
         mix_back(gg, proj, taps, kern, filtered, gf, gprod, gs, shifts, gp, part)
-        columns.middle()
+        columns.pass_on()
+        columns.cross_on()
 
         sum_ref[...] = jnp.zeros_like(sum_ref)
 
@@ -1012,12 +1005,15 @@
         add_into(block, [halves(ctx.pair), got])
         table = Gather(ctx, block, gtab_all, pool, False)
         table.start()
-        columns.finish()
-        outer(e_got)
         mix_sums(gf, proj, taps, gs, prod, shifts, sums, part)
         job = Gather(ctx, sums, taps_all, pool, False)
         job.start()
+        table.pass_on()
+        columns.middle()
         table.middle()
+        columns.finish()
+        job.pass_on()
+        outer(e_got)
         job.middle()
         table.finish()
         job.finish()

time: 297 us -> 300 us (1.010)
  Pallas kernels: 271 us -> 274 us
where the time goes in v6:
time: 300 us
  Pallas kernels  274 us (91%)
  local copies, waits for them, and re-layouts  14.1 us (5%)
  other arithmetic  7.17 us (2%)
  matrix products  3.74 us (1%)
    pallas_call x2, Pallas kernels, call(): pl.pallas_call(body, out_shape=[jax.ShapeDtypeStruct(shape, dtype) for sh...  274 us

profile of v6, /device:TPU:1, one launch (start us, length us, event | category | flops | bytes accessed | tf_op | source)
XLA Modules:
  0.0 299.7 jit_solution(14414895462510959837)
XLA Ops:
  0.7 0.7 neg.14
  1.3 0.7 dynamic-slice_reduce_fusion
  2.1 0.6 reshape.72.taps0.taps
  2.7 1.3 tile.11
  3.9 0.8 reduce.2
  4.7 0.6 reshape_squeeze.7.taps1
  5.3 1.1 bitcast_multiply_fusion.kern1
  6.4 0.0 copy-start.1
  6.4 0.7 constant_dynamic-slice_fusion.kern0.kern
  7.1 1.7 copy.81
  8.9 1.6 copy.82.w_ref.w_far
  10.4 0.0 copy-done.1
  10.4 223.1 %main.1 = (bf16[8,64,512]{2,1,0:T(8,128)(2,1)}, f32[512,128]{1,0:T(8,128)}, s32[8,16,128]{2,1,0:T(8,128)}, bf16[8,256,512]{2,1,0:T(8,128)(2,1)}, bf16[2048,512]{...) custom-call(bf16[512,512]{1,0:T(8,128)(2,1)} %emb_ref.1, ...), custom_call_target="tpu_custom_call" | custom-call | tf_op jit(solution)/shard_map/main/pallas_call | solution.py:320
  233.5 50.8 %end.1 = (bf16[8,256,384]{2,1,0:T(8,128)(2,1)}, f32[8,144,128]{2,1,0:T(8,128)}, f32[512,512]{1,0:T(8,128)}) custom-call(bf16[256,512]{1,0:T(8,128)(2,1)} %get-tuple-element.66.gg_rows, bf16[256,512]{1,0:T(8,128)(2,1)} %get-tuple-element.67.e_col, bf16[8,256,512]{2,1,0:T(8,128)(2,1)} %get-tuple-element.68.e_all, ...), custom_call_target="tpu_custom_call" | custom-call | tf_op jit(solution)/shard_map/end/pallas_call | solution.py:320
  284.3 0.0 copy-start.2
  284.3 10.7 %conditional.1 = (f32[1,512,3,512]{3,1,2,0:T(8,128)}, f32[128,512]{1,0:T(8,128)}, f32[1,3,3,512]{3,0,2,1:T(1,128)S(1)}) conditional(s32[]{:T(128)} %convert_element_type.24, (bf16[8,256,512]{2,1,0:T(8,128)(2,1)}, bf16[8,256,1536]{2,1,0:T(8,128)(2,1)}, f32[8,144,512]{2,1,0:T(8,128)S(1)}) %tuple.24, (bf16[8,64,512]{2,1,0:T(8,128)(2,1)}, ...), branch_computations={%region_0.2_spmd, %region_2.4_spmd} | conditional | flops 3221741568 | bytes 31377516 | solution.py:1181
  284.4 0.0 copy-start.4
  284.4 0.0 copy-start.3
  284.4 0.0 copy-start
  284.4 1.3 bitcast_reduce_fusion
  285.7 0.1 copy.79
  285.9 0.8 copy.96
  286.7 0.0 copy-done.4
  286.7 0.1 copy.85
  286.9 0.1 mul.8
  287.0 0.0 copy-done.3
  287.0 1.0 multiply_convert_fusion
  287.9 0.0 copy-done
  287.9 0.7 copy.86
  288.7 1.3 copy.76
  290.0 0.6 reshape.69
  290.6 0.7 copy.77
  291.3 3.7 %convolution_bitcast_fusion = f32[1,512,3,512]{3,1,2,0:T(8,128)} fusion(bf16[512,512,1]{1,0,2:T(8,128)(2,1)} %bitcast.40, bf16[3,512,512]{2,1,0:T(8,128)(2,1)S(1)} %bitcast.38), kind=kOutput, calls=%fused_computation | convolution fusion | flops 805306368 | bytes 5242880 | tf_op jit(solution)/shard_map/cond/branch_1_fun/dot_general | solution.py:1028
  295.1 0.0 copy-start.5
  295.1 0.0 copy-done.2
  295.1 1.8 multiply_reduce_fusion
  296.9 0.6 negate_multiply_fusion
  297.5 2.3 copy.108
  299.7 0.0 copy-done.5
  (5 shorter events, 0.1 us)
Async XLA Ops:
  6.4 4.0 %copy-start.1 = (f32[128,512]{1,0:T(8,128)}, f32[128,512]{1,0:T(8,128)S(1)}, u32[]{:S(2)}) copy-start(f32[128,512]{1,0:T(8,128)S(1)} %bitcast_multiply_fusion.kern1) | copy-start | bytes 786436
  284.3 10.8 %copy-start.2 = (f32[1,128,512]{2,1,0:T(8,128)S(1)}, f32[1,128,512]{2,1,0:T(8,128)}, u32[]{:S(2)}) copy-start(f32[1,128,512]{2,1,0:T(8,128)} %param.14) | copy-start | bytes 786436
  284.4 2.4 copy-start.4
  284.4 2.6 copy-start.3
  284.4 3.5 %copy-start = (bf16[8,256,384]{2,1,0:T(8,128)(2,1)S(1)}, bf16[8,256,384]{2,1,0:T(8,128)(2,1)}, u32[]{:S(2)}) copy-start(bf16[8,256,384]{2,1,0:T(8,128)(2,1)} %get-tuple-element.162) | copy-start | bytes 4718596 | tf_op jit(solution)/shard_map/cond
  295.1 4.7 %copy-start.5 = (f32[1,3,3,512]{3,0,2,1:T(1,128)}, f32[1,3,3,512]{3,0,2,1:T(1,128)S(1)}, u32[]{:S(2)}) copy-start(f32[1,3,3,512]{3,0,2,1:T(1,128)S(1)} %get-tuple-element.188) | copy-start | bytes 55300

commit v7 on v5

--- a/solution.py
+++ b/solution.py
@@ -118,7 +118,14 @@
     def pass_on(self):
         self.passed = self.turn(self.g.pair, self.copies[1], self.copies[2], 3, 4)
 
-    passed = None
+    def cross_on(self):
+        g, s = self.g, self.sems
+        right, left, mate = g.neighbours()
+        self.copies[0].wait_recv()
+        block = self.block(g.ring, g.mate)
+        self.crossed = (remote(block, block, s[5], right), remote(block, block, s[6], left))
+
+    passed = crossed = None
 
     def middle(self):
         g, s = self.g, self.sems
@@ -130,10 +137,9 @@
         self.sent = list(self.copies) + rest
         if self.pair_first:
             self.late = list(rest)
-            mate_copy.wait_recv()
-            block = self.block(g.ring, g.mate)
-            a = remote(block, block, s[5], right)
-            b = remote(block, block, s[6], left)
+            if self.crossed is None:
+                self.cross_on()
+            a, b = self.crossed
             more = self.turn(g.mate, a, b, 7, 8)
             self.sent += [a, b] + more
             self.late += more
@@ -546,12 +552,9 @@
     along = [{"ctx": (place + k) % n} for k in range(1, n)]
     opposite = {"section": 1 - lax.axis_index("section")}
     greet(along + others + [other_section(), opposite], barrier)
-
-    @pl.when(apart)
-    def _():
-        greet([partner], barrier)
-
-    pl.semaphore_wait(barrier, 2 * n + jnp.where(apart, 1, 0))
+    for k in range(n):
+        pl.when(jnp.logical_or(apart, place != k))(functools.partial(greet, [{"dp": place, "ctx": k}], barrier))
+    pl.semaphore_wait(barrier, 3 * n - 1 + jnp.where(apart, 1, 0))
     lane = 128
     strips = RING
     common = Pool(send, recv)
@@ -630,9 +633,8 @@
             part[strip * 2, :, to] = product[:hold]
             part[strip * 2 + 1, :, to] = product[hold:]
 
+        PairThenRing(ctx, part, pool, pair_bufs).run(half_out)
         outs.pass_on()
-        PairThenRing(ctx, part, pool, pair_bufs).run(half_out)
-        outs.middle()
         here = pl.ds(pl.multiple_of(ctx.pair * hold, hold), hold)
         whole = half_out[...]
         inv = lax.rsqrt(whole[:, 3 * lane :] / (width * 2 * RING) + EPSILON)
@@ -655,6 +657,7 @@
         for k in range(2):
             hot = marks(tok_out, 2 * place + k, vocab)
             first_rows[k * 128 : (k + 1) * 128] = dot(hot, emb_ref[...], TRANS_A).astype(BF16)
+        outs.middle()
         span = gated0.shape[0]
         mix_first(proj0, taps0, kern0, filtered0, prod0, shifts, gated0, span)
         rows = x_block.shape[0]
@@ -708,8 +711,6 @@
         cot = cot_ref
         outs = Gather(ctx, wo_far, wo, pool, False)
         weights = Gather(ctx, w_far, wv, pool, False)
-        outs.start()
-        weights.start()
         there = pltpu.make_async_remote_copy(
             src_ref=cot_ref, dst_ref=crossed, send_sem=cross_sem[0], recv_sem=cross_sem[1],
             device_id=partner, device_id_type=MESH,
@@ -719,6 +720,8 @@
         pl.when(jnp.logical_not(apart))(here.start)
         turned = Gather(dp, cot_ref, part, pool, True)
         turned.start()
+        outs.start()
+        weights.start()
         turned.middle()
         turned.finish()
         outs.pass_on()
@@ -728,12 +731,12 @@
         cots.start()
         weights.pass_on()
         outs.middle()
-        cots.middle()
         outs.finish()
+        cots.pass_on()
+        cots.cross_on()
         gg[...] = jnp.zeros_like(gg)
         for k in range(n):
             gg[...] += dot(part[k], wo[k], TRANS_B)
-        cots.finish()
         weights.middle()
         weights.finish()
         sums_own[REACH:] = jnp.zeros((16, width), F32)
@@ -905,10 +908,11 @@
 
         taps_job = Gather(ctx, sums_own, sums_all, pool, False)
         taps_job.start()
+        cots.middle()
         jobs = [columns, grads, taps_job]
         for job in jobs:
             job.middle()
-        for job in [near] + jobs:
+        for job in [near, cots] + jobs:
             job.finish()
         for copy in (a_copy, b_copy, c_copy, d_copy):
             copy.wait_send()
@@ -995,7 +999,8 @@
         hold = got.shape[0]
         part = gp.shape[0]
         mix_back(gg, proj, taps, kern, filtered, gf, gprod, gs, shifts, gp, part)
-        columns.middle()
+        columns.pass_on()
+        columns.cross_on()
 
         sum_ref[...] = jnp.zeros_like(sum_ref)
 
@@ -1012,12 +1017,15 @@
         add_into(block, [halves(ctx.pair), got])
         table = Gather(ctx, block, gtab_all, pool, False)
         table.start()
-        columns.finish()
-        outer(e_got)
         mix_sums(gf, proj, taps, gs, prod, shifts, sums, part)
         job = Gather(ctx, sums, taps_all, pool, False)
         job.start()
+        table.pass_on()
+        columns.middle()
         table.middle()
+        columns.finish()
+        job.pass_on()
+        outer(e_got)
         job.middle()
         table.finish()
         job.finish()

time: 297 us -> 284 us (0.956)
  Pallas kernels: 271 us -> 258 us
    pallas_call x2, Pallas kernels: 271 us -> 258 us  [call(): pl.pallas_call(body, out_shape=[jax.ShapeDtypeStruct(shape, dtype) for sh...]
where the time goes in v7:
time: 284 us
  Pallas kernels  258 us (91%)
  local copies, waits for them, and re-layouts  14.1 us (5%)
  other arithmetic  7.17 us (3%)
  matrix products  3.74 us (1%)
    pallas_call x2, Pallas kernels, call(): pl.pallas_call(body, out_shape=[jax.ShapeDtypeStruct(shape, dtype) for sh...  258 us

profile of v7, /device:TPU:1, one launch (start us, length us, event | category | flops | bytes accessed | tf_op | source)
XLA Modules:
  0.0 284.1 jit_solution(4766117216149505214)
XLA Ops:
  0.7 0.7 neg.14
  1.3 0.7 dynamic-slice_reduce_fusion
  2.1 0.6 reshape.72.taps0.taps
  2.7 1.3 tile.11
  3.9 0.8 reduce.2
  4.7 0.6 reshape_squeeze.7.taps1
  5.3 1.1 bitcast_multiply_fusion.kern1
  6.4 0.0 copy-start.1
  6.4 0.7 constant_dynamic-slice_fusion.kern0.kern
  7.1 1.7 copy.81
  8.9 1.6 copy.82.w_ref.w_far
  10.4 0.0 copy-done.1
  10.4 207.6 %main.1 = (bf16[8,64,512]{2,1,0:T(8,128)(2,1)}, f32[512,128]{1,0:T(8,128)}, s32[8,16,128]{2,1,0:T(8,128)}, bf16[8,256,512]{2,1,0:T(8,128)(2,1)}, bf16[2048,512]{...) custom-call(bf16[512,512]{1,0:T(8,128)(2,1)} %emb_ref.1, ...), custom_call_target="tpu_custom_call" | custom-call | tf_op jit(solution)/shard_map/main/pallas_call | solution.py:320
  218.1 50.6 %end.1 = (bf16[8,256,384]{2,1,0:T(8,128)(2,1)}, f32[8,144,128]{2,1,0:T(8,128)}, f32[512,512]{1,0:T(8,128)}) custom-call(bf16[256,512]{1,0:T(8,128)(2,1)} %get-tuple-element.66.gg_rows, bf16[256,512]{1,0:T(8,128)(2,1)} %get-tuple-element.67.e_col, bf16[8,256,512]{2,1,0:T(8,128)(2,1)} %get-tuple-element.68.e_all, ...), custom_call_target="tpu_custom_call" | custom-call | tf_op jit(solution)/shard_map/end/pallas_call | solution.py:320
  268.6 0.0 copy-start.2
  268.7 10.7 %conditional.1 = (f32[1,512,3,512]{3,1,2,0:T(8,128)}, f32[128,512]{1,0:T(8,128)}, f32[1,3,3,512]{3,0,2,1:T(1,128)S(1)}) conditional(s32[]{:T(128)} %convert_element_type.24, (bf16[8,256,512]{2,1,0:T(8,128)(2,1)}, bf16[8,256,1536]{2,1,0:T(8,128)(2,1)}, f32[8,144,512]{2,1,0:T(8,128)S(1)}) %tuple.24, (bf16[8,64,512]{2,1,0:T(8,128)(2,1)}, ...), branch_computations={%region_0.2_spmd, %region_2.4_spmd} | conditional | flops 3221741568 | bytes 31377516 | solution.py:1193
  268.7 0.0 copy-start.4
  268.7 0.0 copy-start.3
  268.7 0.0 copy-start
  268.7 1.3 bitcast_reduce_fusion
  270.1 0.1 copy.79
  270.2 0.8 copy.96
  271.0 0.0 copy-done.4
  271.0 0.1 copy.85
  271.2 0.1 mul.8
  271.3 0.0 copy-done.3
  271.3 1.0 multiply_convert_fusion
  272.2 0.0 copy-done
  272.2 0.7 copy.86
  273.0 1.3 copy.76
  274.3 0.6 reshape.69
  274.9 0.7 copy.77
  275.7 3.7 %convolution_bitcast_fusion = f32[1,512,3,512]{3,1,2,0:T(8,128)} fusion(bf16[512,512,1]{1,0,2:T(8,128)(2,1)} %bitcast.40, bf16[3,512,512]{2,1,0:T(8,128)(2,1)S(1)} %bitcast.38), kind=kOutput, calls=%fused_computation | convolution fusion | flops 805306368 | bytes 5242880 | tf_op jit(solution)/shard_map/cond/branch_1_fun/dot_general | solution.py:1040
  279.4 0.0 copy-start.5
  279.4 0.0 copy-done.2
  279.4 1.8 multiply_reduce_fusion
  281.2 0.6 negate_multiply_fusion
  281.8 2.3 copy.108
  284.1 0.0 copy-done.5
  (5 shorter events, 0.1 us)
Async XLA Ops:
  6.4 4.0 %copy-start.1 = (f32[128,512]{1,0:T(8,128)}, f32[128,512]{1,0:T(8,128)S(1)}, u32[]{:S(2)}) copy-start(f32[128,512]{1,0:T(8,128)S(1)} %bitcast_multiply_fusion.kern1) | copy-start | bytes 786436
  268.6 10.8 %copy-start.2 = (f32[1,128,512]{2,1,0:T(8,128)S(1)}, f32[1,128,512]{2,1,0:T(8,128)}, u32[]{:S(2)}) copy-start(f32[1,128,512]{2,1,0:T(8,128)} %param.14) | copy-start | bytes 786436
  268.7 2.4 copy-start.4
  268.7 2.6 copy-start.3
  268.7 3.5 %copy-start = (bf16[8,256,384]{2,1,0:T(8,128)(2,1)S(1)}, bf16[8,256,384]{2,1,0:T(8,128)(2,1)}, u32[]{:S(2)}) copy-start(bf16[8,256,384]{2,1,0:T(8,128)(2,1)} %get-tuple-element.162) | copy-start | bytes 4718596 | tf_op jit(solution)/shard_map/cond
  279.4 4.7 %copy-start.5 = (f32[1,3,3,512]{3,0,2,1:T(1,128)}, f32[1,3,3,512]{3,0,2,1:T(1,128)S(1)}, u32[]{:S(2)}) copy-start(f32[1,3,3,512]{3,0,2,1:T(1,128)S(1)} %get-tuple-element.188) | copy-start | bytes 55300
